TPU v7x, 128 devices: a whole 4x4x4 slice. The times are simulated.
128 devices in a mesh: slab: 32 (over z, x, core), energy: 4 (over y).
Axes of the slice: x: 4, y: 4, z: 4, core: 2. Of those that a mesh axis runs over, the one named last changes fastest.
Arguments:
- onsite: float32 [64, 2, 256, 256], P('slab'), as said below
- hop: float32 [64, 2, 256, 256], P('slab'), may hold values from -0.1875 to 0.1875
- energy_level: float32 [4], P('energy'), parts along dimension 0, may hold values from -0.5 to 0.5
- broadening: float32 [4], P('energy'), parts along dimension 0, may hold values from 0.4 to 0.8
Outputs:
- diagonal: float32 [256, 2, 256, 256], P(('energy', 'slab')), parts along dimension 0
- upper: float32 [256, 2, 256, 256], P(('energy', 'slab')), parts along dimension 0
- lower: float32 [256, 2, 256, 256], P(('energy', 'slab')), parts along dimension 0
There are 4 independent parts, one for each index of `energy`. A program takes and returns all parts, laid end to end along the dimension named above; an argument that names none is the same for every part. Nothing has to cross between parts.
Inputs may be any that keep to these rules, and one draw needn't show every extreme that they name: Each block of onsite is Hermitian: real part symmetric, imaginary part antisymmetric.
All inputs are finite; a program needn't handle non-finite values.
Results may differ from a plain program's by a relative error of at most 0.0003.
Values sent between devices are 32-bit elements; how exact they have to be, the bound alone decides.
No kernel may reach another device: no remote copies, remote signals or barrier semaphores. Data moves between devices by JAX's collectives and lax.ppermute only.
A program may use at most 128 MiB of HBM per device.

v0:
```python
import functools

import jax
import jax.numpy as jnp
from jax import lax
from jax.experimental import pallas as pl
from jax.experimental.pallas import tpu as pltpu
from jax.sharding import PartitionSpec as P


BF = jnp.bfloat16
F32 = jnp.float32
HIGHEST = lax.Precision.HIGHEST
CONVERGED = 0.998
TRUSTED = 0.012
VMEM = pl.BlockSpec(memory_space=pltpu.VMEM)
SMEM = pl.BlockSpec(memory_space=pltpu.SMEM)


def dot(a, b):
    return jnp.dot(a, b, preferred_element_type=F32)


def exact_dot(a, b):
    return jnp.dot(a, b, precision=HIGHEST, preferred_element_type=F32)


def row(c):
    w = c.shape[1]
    return jnp.concatenate([c[:w], c[w:]], axis=1)


def put(out, r, at=0):
    w = r.shape[0]
    out[at : at + w] = r[:, :w]
    out[at + w : at + 2 * w] = r[:, w:]


def turned(r):
    w = r.shape[1] // 2
    return jnp.concatenate([-r[:, w:], r[:, :w]], axis=1)


def emb(r):
    return jnp.concatenate([r, turned(r)], axis=0)


def adjoint(r):
    w = r.shape[0]
    return jnp.concatenate([r[:, :w].T, -r[:, w:].T], axis=1)


def split(x):
    high = x.astype(BF)
    return high, (x - high.astype(F32)).astype(BF)


def product(a, b):
    a_high, a_low = split(a)
    b_high, b_low = split(b)
    e_high, e_low = emb(b_high), emb(b_low)
    return dot(a_high, e_high) + dot(a_high, e_low) + dot(a_low, e_high)


def unit(w):
    at = lax.broadcasted_iota(jnp.int32, (w, 2 * w), 0)
    return (at == lax.broadcasted_iota(jnp.int32, (w, 2 * w), 1)).astype(F32)


def invert(blocks, eta, work, side=()):
    z, ea, el, ex, full, spread, rest = work
    w = blocks[0].shape[0]
    one = unit(w)
    halves = [slice(k * w // 2, (k + 1) * w // 2) for k in range(2)]

    def place(i, x):
        ex[i, :w] = x
        ex[i, w:] = turned(x)

    norms = []
    for i, a in enumerate(blocks):
        high, low = split(a)
        ea[i] = emb(high)
        el[i] = emb(low)
        ah = adjoint(high)
        gram = dot(ah, ea[i])
        size = jnp.sqrt(gram[:, :w] * gram[:, :w] + gram[:, w:] * gram[:, w:])
        norm = 1.02 * jnp.max(jnp.sum(size, axis=1))
        place(i, (ah.astype(F32) * (1.0 / norm)).astype(BF))
        norms.append(norm)
    largest = functools.reduce(jnp.maximum, norms)
    bound = jnp.maximum(0.9 * eta * eta / largest, 1e-10)

    def step(bound, piece=None):
        mu = 2.0 / (bound + 1.03)
        for i in range(len(blocks)):
            errors = [(one[h] - mu * dot(ex[i, h], ea[i])).astype(BF) for h in halves]
            if piece is not None:
                piece()
            news = [
                (mu * (ex[i, h].astype(F32) + dot(e, ex[i]))).astype(BF)
                for h, e in zip(halves, errors)
            ]
            place(i, jnp.concatenate(news, axis=0))
        gap = 1.0 - mu * bound
        return 1.0 - gap * gap

    for piece in side:
        bound = step(bound, piece)
    lax.while_loop(lambda bound: bound < CONVERGED, step, bound)
    for i, a in enumerate(blocks):
        x = ex[i, :w]
        error = one - (dot(x, ea[i]) + dot(x, el[i]))
        z[i] = x.astype(F32) + dot(error.astype(BF), ex[i])
        left = jnp.sum(error * error)

        @pl.when(jnp.logical_not(left <= TRUSTED))
        def _():
            polish(a, norms[i], left, z, i, full, spread, rest)


def polish(a, norm, left, z, i, full, spread, rest):
    w = a.shape[0]
    high, wide = min(64, w), min(128, w)
    across = 2 * w // wide
    full[...] = emb(a)

    @pl.when(jnp.logical_not(left <= 0.25))
    def _():
        z[i] = adjoint(a) * (1.0 / norm)

    def cut(k):
        top, side = k // across * high, k % across * wide
        return (
            top,
            side,
            pl.ds(pl.multiple_of(top, high), high),
            pl.ds(pl.multiple_of(side, wide), wide),
        )

    def once(state):
        def residual(k, total):
            top, side, rows, cols = cut(k)
            at = lax.broadcasted_iota(jnp.int32, (high, wide), 0) + top
            to = lax.broadcasted_iota(jnp.int32, (high, wide), 1) + side
            part = jnp.where(at == to, 1.0, 0.0) - exact_dot(z[i, rows, :], full[:, cols])
            rest[rows, cols] = part
            return total + jnp.sum(part * part)

        tiles = w // high * across
        total = lax.fori_loop(0, tiles, residual, jnp.float32(0.0))
        spread[...] = emb(z[i])

        def correct(k, _):
            _, _, rows, cols = cut(k)
            z[i, rows, cols] += exact_dot(rest[rows, :], spread[:, cols])
            return 0

        lax.fori_loop(0, tiles, correct, 0)
        return state[0] + 1, total

    lax.while_loop(
        lambda state: (state[0] < 64) & jnp.logical_not(state[1] <= 1e-6),
        once,
        (0, jnp.float32(1.0)),
    )


def initial(onsite, scalars):
    w = onsite.shape[0]
    at = lax.broadcasted_iota(jnp.int32, (w, 2 * w), 0)
    to = lax.broadcasted_iota(jnp.int32, (w, 2 * w), 1)
    shift = jnp.where(at == to, scalars[0], jnp.where(at + w == to, scalars[1], 0.0))
    return shift - onsite


def deferred(out, a, b, sign):
    a_high, a_low = split(a)
    b_high, b_low = split(b)

    def lead():
        put(out, sign * dot(a_high, emb(b_high)))

    def middle():
        put(out, row(out[...]) + sign * dot(a_high, emb(b_low)))

    def trail():
        put(out, row(out[...]) + sign * dot(a_low, emb(b_high)))

    return lead, middle, trail


def paired(first, second):
    def piece():
        first()
        second()

    return piece


def solve(d, lower, upper, side, eta, payload, work):
    invert([d], eta, work, side)
    z = work[0][0]
    put(payload, product(z, row(upper[...])))
    put(payload, product(z, row(lower[...])), upper.shape[0])


def first_kernel(onsite, hop, scalars, up, down, sem, *work):
    w = onsite.shape[2]
    beside = pltpu.make_async_copy(hop.at[0], down.at[pl.ds(2 * w, 2 * w)], sem)
    beside.start()
    invert([initial(row(onsite[i]), scalars) for i in range(2)], scalars[1], work)
    put(up, work[0][1])
    put(down, work[0][0])
    beside.wait()


def second_kernel(
    onsite, h_m2, h_m1, h_0, h_p1, z_m, z_p, scalars, d_out, l_out, u_out, payload, *work
):
    h0, hm = row(h_0[...]), row(h_m1[...])
    from_above = product(h0, row(z_p[...]))
    from_below = product(adjoint(hm), row(z_m[...]))
    d = (
        initial(row(onsite[...]), scalars)
        - product(from_above, adjoint(h0))
        - product(from_below, hm)
    )
    put(d_out, d)
    set_upper = deferred(u_out, from_above, row(h_p1[...]), -scalars[2])
    set_lower = deferred(l_out, from_below, adjoint(row(h_m2[...])), -1.0)
    side = [paired(*pair) for pair in zip(set_upper, set_lower)]
    solve(row(d_out[...]), l_out, u_out, side, scalars[1], payload, work)


def third_kernel(
    d_in, l_in, u_in, below, above, scalars, d_out, l_out, u_out, payload, *work
):
    w = d_in.shape[1]
    lower, upper = row(l_in[...]), row(u_in[...])
    d = (
        row(d_in[...])
        - product(lower, row(below[: 2 * w]))
        - product(upper, row(above[2 * w :]))
    )
    put(d_out, d)
    set_upper = deferred(u_out, upper, row(above[: 2 * w]), -1.0)
    set_lower = deferred(l_out, lower, row(below[2 * w :]), -1.0)
    side = [paired(*pair) for pair in zip(set_upper, set_lower)]
    solve(row(d_out[...]), l_out, u_out, side, scalars[1], payload, work)


def last_kernel(d_in, l_in, u_in, below, above, d_out, u_out, l_out):
    w = d_in.shape[1]
    lower, upper = row(l_in[...]), row(u_in[...])
    d = (
        row(d_in[...])
        - product(lower, row(below[: 2 * w]))
        - product(upper, row(above[2 * w :]))
    )
    put(d_out.at[0], d)
    put(l_out.at[0], -product(lower, row(below[2 * w :])))
    put(u_out.at[0], -product(upper, row(above[: 2 * w])))


def last_below(d_in, l_in, below, l_old, d_mid, l_out):
    w = d_in.shape[1]
    lower = row(l_in[...])
    put(d_mid, row(d_in[...]) - product(lower, row(below[: 2 * w])))
    put(l_out.at[0], -product(lower, row(below[2 * w :])))


def last_above(d_mid, u_in, above, d_old, u_old, d_out, u_out):
    w = d_mid.shape[1]
    upper = row(u_in[...])
    put(d_out.at[0], row(d_mid[...]) - product(upper, row(above[2 * w :])))
    put(u_out.at[0], -product(upper, row(above[: 2 * w])))


def shape(*dims):
    return jax.ShapeDtypeStruct(dims, F32)


def work(count, w):
    return [
        pltpu.VMEM((count, w, 2 * w), F32),
        pltpu.VMEM((count, 2 * w, 2 * w), BF),
        pltpu.VMEM((count, 2 * w, 2 * w), BF),
        pltpu.VMEM((count, 2 * w, 2 * w), BF),
        pltpu.VMEM((2 * w, 2 * w), F32),
        pltpu.VMEM((2 * w, 2 * w), F32),
        pltpu.VMEM((w, 2 * w), F32),
    ]


PARAMS = pltpu.CompilerParams(vmem_limit_bytes=24 << 20)


def send(x, by):
    size = lax.axis_size("slab")
    return lax.ppermute(x, "slab", [(i, i + by) for i in range(size) if 0 <= i + by < size])


def reduce_levels(onsite, hop, energy_level, broadening):
    rows, _, w, _ = onsite.shape
    onsite = onsite.reshape(rows, 2 * w, w)
    hop = hop.reshape(rows, 2 * w, w)
    last = lax.axis_index("slab") == lax.axis_size("slab") - 1
    keep = jnp.where(last, 0.0, 1.0).astype(F32)
    scalars_a = jnp.stack([energy_level[0], broadening[0], keep])
    scalars_b = jnp.stack([energy_level[0], broadening[0], jnp.float32(1.0)])

    hop_left = send(hop, 1)
    block = shape(2 * w, w)
    inverse_b, inverse_hop_a = pl.pallas_call(
        first_kernel,
        out_shape=(block, shape(4 * w, w)),
        in_specs=[VMEM, pl.BlockSpec(memory_space=pltpu.HBM), SMEM],
        out_specs=(VMEM, VMEM),
        scratch_shapes=[pltpu.SemaphoreType.DMA] + work(rows, w),
        compiler_params=PARAMS,
        name="first",
    )(onsite, hop, scalars_a)
    z_left = send(inverse_b, 1)
    z_hop_right = send(inverse_hop_a, -1)
    inverse_a = inverse_hop_a[: 2 * w]
    z_right, hop_right = z_hop_right[: 2 * w], z_hop_right[2 * w :]

    second = pl.pallas_call(
        second_kernel,
        out_shape=(block, block, block, shape(4 * w, w)),
        in_specs=[VMEM] * 7 + [SMEM],
        out_specs=(VMEM,) * 4,
        scratch_shapes=work(1, w),
        compiler_params=PARAMS,
        name="second",
    )
    state_a = second(
        onsite[0], hop_left[0], hop_left[1], hop[0], hop[1], z_left, inverse_b, scalars_a
    )
    below_a, above_a = send(state_a[3], 1), send(state_a[3], -1)
    state_b = second(
        onsite[1], hop_left[1], hop[0], hop[1], hop_right, inverse_a, z_right, scalars_b
    )
    below_b, above_b = send(state_b[3], 1), send(state_b[3], -1)

    third = pl.pallas_call(
        third_kernel,
        out_shape=(block, block, block, shape(4 * w, w)),
        in_specs=[VMEM] * 5 + [SMEM],
        out_specs=(VMEM,) * 4,
        scratch_shapes=work(1, w),
        compiler_params=PARAMS,
        name="third",
    )
    state_a = third(*state_a[:3], below_a, above_a, scalars_a)
    below_a, above_a = send(state_a[3], 2), send(state_a[3], -2)
    state_b = third(*state_b[:3], below_b, above_b, scalars_a)
    below_b, above_b = send(state_b[3], 2), send(state_b[3], -2)

    def at(k):
        return pl.BlockSpec((1, 2 * w, w), lambda i: (k, 0, 0))

    whole = shape(rows, 2 * w, w)
    kept = pl.BlockSpec(memory_space=pl.ANY)
    d_out, u_out, l_out = pl.pallas_call(
        last_kernel,
        grid=(1,),
        out_shape=(whole,) * 3,
        in_specs=[VMEM] * 5,
        out_specs=(at(0),) * 3,
        compiler_params=PARAMS,
        name="last",
    )(*state_a[:3], below_a, above_a)
    d, lower, upper = state_b[:3]
    d, l_out = pl.pallas_call(
        last_below,
        grid=(1,),
        out_shape=(block, whole),
        in_specs=[VMEM] * 3 + [kept],
        out_specs=(VMEM, at(1)),
        input_output_aliases={3: 1},
        compiler_params=PARAMS,
        name="last_below",
    )(d, lower, below_b, l_out)
    d_out, u_out = pl.pallas_call(
        last_above,
        grid=(1,),
        out_shape=(whole, whole),
        in_specs=[VMEM] * 3 + [kept] * 2,
        out_specs=(at(1), at(1)),
        input_output_aliases={3: 0, 4: 1},
        compiler_params=PARAMS,
        name="last_above",
    )(d, upper, above_b, d_out, u_out)
    return tuple(x.reshape(rows, 2, w, w) for x in (d_out, u_out, l_out))


def solution(mesh):
    placed = (P("slab", None, None, None), P("slab", None, None, None), P("energy"), P("energy"))
    out = P(("energy", "slab"), None, None, None)
    return jax.shard_map(
        reduce_levels, mesh=mesh, in_specs=placed, out_specs=(out, out, out), check_vma=False
    )
```

profile of v0, /device:TPU:62, one launch (start us, length us, event | category | flops | bytes accessed | tf_op | source)
XLA Modules:
  0.0 128.8 jit_solution(297618260870463863)
XLA Ops:
  0.6 1.9 %collective-permute-start = (f32[2,512,256]{2,1,0:T(8,128)}, f32[2,512,256]{2,1,0:T(8,128)S(1)}, u32[]{:S(2)}, u32[]{:S(2)}) collective-permute-start(f32[2,512,256]{2,1,0:T(8,128)} %bitcast.19), channel_id=1, source_target_pairs={{0,4},{4,8},{8,12},{12,16},{16,20},{20,24},{24,28},{28,32},{32,36}... | collective-permute-start | bytes 3145736 | tf_op jit(solution)/shard_map/ppermute | solution.py:301
  3.9 0.1 pad_maximum_fusion.scalars
  3.9 1.2 copy-done
  5.2 1.2 copy-done.1
  6.4 7.0 %first.1 = (f32[512,256]{1,0:T(8,128)S(1)}, f32[1024,256]{1,0:T(8,128)S(1)}) custom-call(f32[2,512,256]{2,1,0:T(8,128)S(1)} %bitcast.18, f32[2,512,256]{2,1,0:T(8,128)S(1)} %bitcast.20, f32[3]{0:T(128)S(1)} %pad_maximum_fusion.scalars), custom_call_target="tpu_custom_call" | custom-call | tf_op jit(solution)/shard_map/first/pallas_call | solution.py:315
  13.4 4.6 %collective-permute-start.1 = (f32[1024,256]{1,0:T(8,128)S(1)}, f32[1024,256]{1,0:T(8,128)S(1)}, u32[]{:S(2)}, u32[]{:S(2)}) collective-permute-start(f32[1024,256]{1,0:T(8,128)S(1)} %get-tuple-element.28), channel_id=1, source_target_pairs={{4,0},{8,4},{12,8},{16,12},{20,16},{24,20},{28,24},{32,28},{36,32}... | collective-permute-start | bytes 3145736 | tf_op jit(solution)/shard_map/ppermute | solution.py:301
  18.0 1.9 %collective-permute-start.5 = (f32[512,256]{1,0:T(8,128)S(1)}, f32[512,256]{1,0:T(8,128)S(1)}, u32[]{:S(2)}, u32[]{:S(2)}) collective-permute-start(f32[512,256]{1,0:T(8,128)S(1)} %get-tuple-element.36.z_p), channel_id=1, source_target_pairs={{0,4},{4,8},{8,12},{12,16},{16,20},{20,24},{24,28},{28,32},{32,36}... | collective-permute-start | bytes 1572872 | tf_op jit(solution)/shard_map/ppermute | solution.py:301
  20.0 0.1 pad_maximum_fusion.2.scalars
  20.0 0.1 fusion.2
  20.1 0.1 fusion
  20.2 0.1 slice_bitcast_fusion
  20.3 8.2 %collective-permute-done.5.z_m = f32[512,256]{1,0:T(8,128)S(1)} collective-permute-done((f32[512,256]{1,0:T(8,128)S(1)}, f32[512,256]{1,0:T(8,128)S(1)}, u32[]{:S(2)}, u32[]{:S(2)}) %collective-permute-start.5) | collective-permute-done | bytes 524320 | tf_op jit(solution)/shard_map/ppermute | solution.py:301
  28.5 9.6 %second.3 = (f32[512,256]{1,0:T(8,128)S(1)}, f32[512,256]{1,0:T(8,128)S(1)}, f32[512,256]{1,0:T(8,128)S(1)}, f32[1024,256]{1,0:T(8,128)S(1)}) custom-call(f32[512,256]{1,0:T(8,128)S(1)} %bitcast.22, f32[512,256]{1,0:T(8,128)S(1)} %get-tuple-element.53.h_m2, f32[512,256]{1,0:T(8,128)S(1)} %get-tuple-element.54.h_m2.h_m1, f32[512,256]{1,0:T(8,128)S(1)} %bitcast.16, ...), custom_call_target="tpu_custom_call" | custom-call | tf_op jit(solution)/shard_map/second/pallas_call | solution.py:338
  38.1 2.7 %collective-permute-start.6 = (f32[1024,256]{1,0:T(8,128)S(1)}, f32[1024,256]{1,0:T(8,128)S(1)}, u32[]{:S(2)}, u32[]{:S(2)}) collective-permute-start(f32[1024,256]{1,0:T(8,128)S(1)} %get-tuple-element.40), channel_id=1, source_target_pairs={{0,4},{4,8},{8,12},{12,16},{16,20},{20,24},{24,28},{28,32},{32,36}... | collective-permute-start | bytes 3145736 | tf_op jit(solution)/shard_map/ppermute | solution.py:301
  40.8 3.1 %collective-permute-start.7 = (f32[1024,256]{1,0:T(8,128)S(1)}, f32[1024,256]{1,0:T(8,128)S(1)}, u32[]{:S(2)}, u32[]{:S(2)}) collective-permute-start(f32[1024,256]{1,0:T(8,128)S(1)} %get-tuple-element.40), channel_id=1, source_target_pairs={{4,0},{8,4},{12,8},{16,12},{20,16},{24,20},{28,24},{32,28},{36,32}... | collective-permute-start | bytes 3145736 | tf_op jit(solution)/shard_map/ppermute | solution.py:301
  43.9 0.1 fusion.1
  43.9 9.6 %second.2 = (f32[512,256]{1,0:T(8,128)S(1)}, f32[512,256]{1,0:T(8,128)S(1)}, f32[512,256]{1,0:T(8,128)S(1)}, f32[1024,256]{1,0:T(8,128)S(1)}) custom-call(f32[512,256]{1,0:T(8,128)S(1)} %bitcast.21, f32[512,256]{1,0:T(8,128)S(1)} %get-tuple-element.54.h_m2.h_m1, f32[512,256]{1,0:T(8,128)S(1)} %bitcast.17, f32[512,256]{1,0:T(8,128)S(1)} %bitcast.15, ...), custom_call_target="tpu_custom_call" | custom-call | tf_op jit(solution)/shard_map/second/pallas_call | solution.py:342
  53.6 5.1 %collective-permute-start.2 = (f32[1024,256]{1,0:T(8,128)S(1)}, f32[1024,256]{1,0:T(8,128)S(1)}, u32[]{:S(2)}, u32[]{:S(2)}) collective-permute-start(f32[1024,256]{1,0:T(8,128)S(1)} %get-tuple-element.32), channel_id=1, source_target_pairs={{0,4},{4,8},{8,12},{12,16},{16,20},{20,24},{24,28},{28,32},{32,36}... | collective-permute-start | bytes 3145736 | tf_op jit(solution)/shard_map/ppermute | solution.py:301
  58.6 1.9 %collective-permute-start.3 = (f32[1024,256]{1,0:T(8,128)S(1)}, f32[1024,256]{1,0:T(8,128)S(1)}, u32[]{:S(2)}, u32[]{:S(2)}) collective-permute-start(f32[1024,256]{1,0:T(8,128)S(1)} %get-tuple-element.32), channel_id=1, source_target_pairs={{4,0},{8,4},{12,8},{16,12},{20,16},{24,20},{28,24},{32,28},{36,32}... | collective-permute-start | bytes 3145736 | tf_op jit(solution)/shard_map/ppermute | solution.py:301
  60.6 8.3 %third.3 = (f32[512,256]{1,0:T(8,128)S(1)}, f32[512,256]{1,0:T(8,128)S(1)}, f32[512,256]{1,0:T(8,128)S(1)}, f32[1024,256]{1,0:T(8,128)S(1)}) custom-call(f32[512,256]{1,0:T(8,128)S(1)} %get-tuple-element.37.d_in, f32[512,256]{1,0:T(8,128)S(1)} %get-tuple-element.38.l_in, f32[512,256]{1,0:T(8,128)S(1)} %get-tuple-element.39.u_in, ...), custom_call_target="tpu_custom_call" | custom-call | tf_op jit(solution)/shard_map/third/pallas_call | solution.py:356
  68.9 10.2 %collective-permute-start.8 = (f32[1024,256]{1,0:T(8,128)S(1)}, f32[1024,256]{1,0:T(8,128)S(1)}, u32[]{:S(2)}, u32[]{:S(2)}) collective-permute-start(f32[1024,256]{1,0:T(8,128)S(1)} %get-tuple-element.44), channel_id=1, source_target_pairs={{0,8},{4,12},{8,16},{12,20},{16,24},{20,28},{24,32},{28,36},{32,40... | collective-permute-start | bytes 3145736 | tf_op jit(solution)/shard_map/ppermute | solution.py:301
  79.1 1.9 %collective-permute-start.9 = (f32[1024,256]{1,0:T(8,128)S(1)}, f32[1024,256]{1,0:T(8,128)S(1)}, u32[]{:S(2)}, u32[]{:S(2)}) collective-permute-start(f32[1024,256]{1,0:T(8,128)S(1)} %get-tuple-element.44), channel_id=1, source_target_pairs={{8,0},{12,4},{16,8},{20,12},{24,16},{28,20},{32,24},{36,28},{40,32... | collective-permute-start | bytes 3145736 | tf_op jit(solution)/shard_map/ppermute | solution.py:301
  81.1 8.8 %third.2 = (f32[512,256]{1,0:T(8,128)S(1)}, f32[512,256]{1,0:T(8,128)S(1)}, f32[512,256]{1,0:T(8,128)S(1)}, f32[1024,256]{1,0:T(8,128)S(1)}) custom-call(f32[512,256]{1,0:T(8,128)S(1)} %get-tuple-element.29.d_in, f32[512,256]{1,0:T(8,128)S(1)} %get-tuple-element.30.l_in, f32[512,256]{1,0:T(8,128)S(1)} %get-tuple-element.31.u_in, ...), custom_call_target="tpu_custom_call" | custom-call | tf_op jit(solution)/shard_map/third/pallas_call | solution.py:358
  89.8 6.0 %collective-permute-start.4 = (f32[1024,256]{1,0:T(8,128)S(1)}, f32[1024,256]{1,0:T(8,128)S(1)}, u32[]{:S(2)}, u32[]{:S(2)}) collective-permute-start(f32[1024,256]{1,0:T(8,128)S(1)} %get-tuple-element.35), channel_id=1, source_target_pairs={{0,8},{4,12},{8,16},{12,20},{16,24},{20,28},{24,32},{28,36},{32,40... | collective-permute-start | bytes 3145736 | tf_op jit(solution)/shard_map/ppermute | solution.py:301
  95.9 1.9 %collective-permute-start.10 = (f32[1024,256]{1,0:T(8,128)S(1)}, f32[1024,256]{1,0:T(8,128)S(1)}, u32[]{:S(2)}, u32[]{:S(2)}) collective-permute-start(f32[1024,256]{1,0:T(8,128)S(1)} %get-tuple-element.35), channel_id=1, source_target_pairs={{8,0},{12,4},{16,8},{20,12},{24,16},{28,20},{32,24},{36,28},{40,32... | collective-permute-start | bytes 3145736 | tf_op jit(solution)/shard_map/ppermute | solution.py:301
  97.8 4.6 %collective-permute-done.8.below = f32[1024,256]{1,0:T(8,128)S(1)} collective-permute-done((f32[1024,256]{1,0:T(8,128)S(1)}, f32[1024,256]{1,0:T(8,128)S(1)}, u32[]{:S(2)}, u32[]{:S(2)}) %collective-permute-start.8) | collective-permute-done | bytes 1048608 | tf_op jit(solution)/shard_map/ppermute | solution.py:301
  102.4 6.7 %collective-permute-done.9.above = f32[1024,256]{1,0:T(8,128)S(1)} collective-permute-done((f32[1024,256]{1,0:T(8,128)S(1)}, f32[1024,256]{1,0:T(8,128)S(1)}, u32[]{:S(2)}, u32[]{:S(2)}) %collective-permute-start.9) | collective-permute-done | bytes 1048608 | tf_op jit(solution)/shard_map/ppermute | solution.py:301
  109.1 2.8 %last.1 = (f32[2,512,256]{2,1,0:T(8,128)}, f32[2,512,256]{2,1,0:T(8,128)}, f32[2,512,256]{2,1,0:T(8,128)}) custom-call(f32[512,256]{1,0:T(8,128)S(1)} %get-tuple-element.41.d_in, f32[512,256]{1,0:T(8,128)S(1)} %get-tuple-element.42.l_in, f32[512,256]{1,0:T(8,128)S(1)} %get-tuple-element.43.u_in, f32[1024,256]{1,0:T(8,128)S(1)} %collective-permute-done.8.below, ...), custom_call_target="tpu_custom_call" | custom-call | tf_op jit(solution)/shard_map/last/pallas_call | solution.py:366
  112.0 8.6 %collective-permute-done.4.below = f32[1024,256]{1,0:T(8,128)S(1)} collective-permute-done((f32[1024,256]{1,0:T(8,128)S(1)}, f32[1024,256]{1,0:T(8,128)S(1)}, u32[]{:S(2)}, u32[]{:S(2)}) %collective-permute-start.4) | collective-permute-done | bytes 1048608 | tf_op jit(solution)/shard_map/ppermute | solution.py:301
  120.6 1.8 %last_below.1 = (f32[512,256]{1,0:T(8,128)S(1)}, f32[2,512,256]{2,1,0:T(8,128)}) custom-call(f32[512,256]{1,0:T(8,128)S(1)} %get-tuple-element.33.d_in, f32[512,256]{1,0:T(8,128)S(1)} %get-tuple-element.34.l_in, f32[1024,256]{1,0:T(8,128)S(1)} %collective-permute-done.4.below, f32[2,512,256]{2,1,0:T(8,128)} %get-tuple-element.45.l_old), custom_call_target="tpu_custom_call", output_to_operand_aliasing={{1}: (3, {})} | custom-call | tf_op jit(solution)/shard_map/last_below/pallas_call | solution.py:376
  122.4 4.6 %collective-permute-done.10.above = f32[1024,256]{1,0:T(8,128)S(1)} collective-permute-done((f32[1024,256]{1,0:T(8,128)S(1)}, f32[1024,256]{1,0:T(8,128)S(1)}, u32[]{:S(2)}, u32[]{:S(2)}) %collective-permute-start.10) | collective-permute-done | bytes 1048608 | tf_op jit(solution)/shard_map/ppermute | solution.py:301
  127.0 1.8 %last_above.1 = (f32[2,512,256]{2,1,0:T(8,128)}, f32[2,512,256]{2,1,0:T(8,128)}) custom-call(f32[512,256]{1,0:T(8,128)S(1)} %get-tuple-element.46.d_mid, f32[512,256]{1,0:T(8,128)S(1)} %get-tuple-element.47.u_in, f32[1024,256]{1,0:T(8,128)S(1)} %collective-permute-done.10.above, ...), custom_call_target="tpu_custom_call", output_to_operand_aliasing={{0}: (3, {}), {1}: (4, {})} | custom-call | tf_op jit(solution)/shard_map/last_above/pallas_call | solution.py:386
  (11 shorter events, 0.1 us)
Async XLA Ops:
  0.6 19.6 %collective-permute-start = (f32[2,512,256]{2,1,0:T(8,128)}, f32[2,512,256]{2,1,0:T(8,128)S(1)}, u32[]{:S(2)}, u32[]{:S(2)}) collective-permute-start(f32[2,512,256]{2,1,0:T(8,128)} %bitcast.19), channel_id=1, source_target_pairs={{0,4},{4,8},{8,12},{12,16},{16,20},{20,24},{24,28},{28,32},{32,36}... | collective-permute-start | bytes 3145736 | tf_op jit(solution)/shard_map/ppermute | solution.py:301
  3.9 1.2 copy-start
  5.2 1.2 copy-start.1
  13.4 6.6 %copy-start.2 = (f32[2,2,256,256]{3,2,1,0:T(8,128)S(1)}, f32[2,2,256,256]{3,2,1,0:T(8,128)}, u32[]{:S(2)}) copy-start(f32[2,2,256,256]{3,2,1,0:T(8,128)} %param.5) | copy-start | bytes 3145732
  13.4 30.5 %collective-permute-start.1 = (f32[1024,256]{1,0:T(8,128)S(1)}, f32[1024,256]{1,0:T(8,128)S(1)}, u32[]{:S(2)}, u32[]{:S(2)}) collective-permute-start(f32[1024,256]{1,0:T(8,128)S(1)} %get-tuple-element.28), channel_id=1, source_target_pairs={{4,0},{8,4},{12,8},{16,12},{20,16},{24,20},{28,24},{32,28},{36,32}... | collective-permute-start | bytes 3145736 | tf_op jit(solution)/shard_map/ppermute | solution.py:301
  18.0 10.5 %collective-permute-start.5 = (f32[512,256]{1,0:T(8,128)S(1)}, f32[512,256]{1,0:T(8,128)S(1)}, u32[]{:S(2)}, u32[]{:S(2)}) collective-permute-start(f32[512,256]{1,0:T(8,128)S(1)} %get-tuple-element.36.z_p), channel_id=1, source_target_pairs={{0,4},{4,8},{8,12},{12,16},{16,20},{20,24},{24,28},{28,32},{32,36}... | collective-permute-start | bytes 1572872 | tf_op jit(solution)/shard_map/ppermute | solution.py:301
  38.1 22.5 %collective-permute-start.6 = (f32[1024,256]{1,0:T(8,128)S(1)}, f32[1024,256]{1,0:T(8,128)S(1)}, u32[]{:S(2)}, u32[]{:S(2)}) collective-permute-start(f32[1024,256]{1,0:T(8,128)S(1)} %get-tuple-element.40), channel_id=1, source_target_pairs={{0,4},{4,8},{8,12},{12,16},{16,20},{20,24},{24,28},{28,32},{32,36}... | collective-permute-start | bytes 3145736 | tf_op jit(solution)/shard_map/ppermute | solution.py:301
  40.8 19.8 %collective-permute-start.7 = (f32[1024,256]{1,0:T(8,128)S(1)}, f32[1024,256]{1,0:T(8,128)S(1)}, u32[]{:S(2)}, u32[]{:S(2)}) collective-permute-start(f32[1024,256]{1,0:T(8,128)S(1)} %get-tuple-element.40), channel_id=1, source_target_pairs={{4,0},{8,4},{12,8},{16,12},{20,16},{24,20},{28,24},{32,28},{36,32}... | collective-permute-start | bytes 3145736 | tf_op jit(solution)/shard_map/ppermute | solution.py:301
  53.6 27.5 %collective-permute-start.2 = (f32[1024,256]{1,0:T(8,128)S(1)}, f32[1024,256]{1,0:T(8,128)S(1)}, u32[]{:S(2)}, u32[]{:S(2)}) collective-permute-start(f32[1024,256]{1,0:T(8,128)S(1)} %get-tuple-element.32), channel_id=1, source_target_pairs={{0,4},{4,8},{8,12},{12,16},{16,20},{20,24},{24,28},{28,32},{32,36}... | collective-permute-start | bytes 3145736 | tf_op jit(solution)/shard_map/ppermute | solution.py:301
  58.6 22.4 %collective-permute-start.3 = (f32[1024,256]{1,0:T(8,128)S(1)}, f32[1024,256]{1,0:T(8,128)S(1)}, u32[]{:S(2)}, u32[]{:S(2)}) collective-permute-start(f32[1024,256]{1,0:T(8,128)S(1)} %get-tuple-element.32), channel_id=1, source_target_pairs={{4,0},{8,4},{12,8},{16,12},{20,16},{24,20},{28,24},{32,28},{36,32}... | collective-permute-start | bytes 3145736 | tf_op jit(solution)/shard_map/ppermute | solution.py:301
  68.9 33.5 %collective-permute-start.8 = (f32[1024,256]{1,0:T(8,128)S(1)}, f32[1024,256]{1,0:T(8,128)S(1)}, u32[]{:S(2)}, u32[]{:S(2)}) collective-permute-start(f32[1024,256]{1,0:T(8,128)S(1)} %get-tuple-element.44), channel_id=1, source_target_pairs={{0,8},{4,12},{8,16},{12,20},{16,24},{20,28},{24,32},{28,36},{32,40... | collective-permute-start | bytes 3145736 | tf_op jit(solution)/shard_map/ppermute | solution.py:301
  79.1 30.0 %collective-permute-start.9 = (f32[1024,256]{1,0:T(8,128)S(1)}, f32[1024,256]{1,0:T(8,128)S(1)}, u32[]{:S(2)}, u32[]{:S(2)}) collective-permute-start(f32[1024,256]{1,0:T(8,128)S(1)} %get-tuple-element.44), channel_id=1, source_target_pairs={{8,0},{12,4},{16,8},{20,12},{24,16},{28,20},{32,24},{36,28},{40,32... | collective-permute-start | bytes 3145736 | tf_op jit(solution)/shard_map/ppermute | solution.py:301
  89.8 30.8 %collective-permute-start.4 = (f32[1024,256]{1,0:T(8,128)S(1)}, f32[1024,256]{1,0:T(8,128)S(1)}, u32[]{:S(2)}, u32[]{:S(2)}) collective-permute-start(f32[1024,256]{1,0:T(8,128)S(1)} %get-tuple-element.35), channel_id=1, source_target_pairs={{0,8},{4,12},{8,16},{12,20},{16,24},{20,28},{24,32},{28,36},{32,40... | collective-permute-start | bytes 3145736 | tf_op jit(solution)/shard_map/ppermute | solution.py:301
  95.9 31.2 %collective-permute-start.10 = (f32[1024,256]{1,0:T(8,128)S(1)}, f32[1024,256]{1,0:T(8,128)S(1)}, u32[]{:S(2)}, u32[]{:S(2)}) collective-permute-start(f32[1024,256]{1,0:T(8,128)S(1)} %get-tuple-element.35), channel_id=1, source_target_pairs={{8,0},{12,4},{16,8},{20,12},{24,16},{28,20},{32,24},{36,28},{40,32... | collective-permute-start | bytes 3145736 | tf_op jit(solution)/shard_map/ppermute | solution.py:301
where the time goes:
time: 129 us
  Pallas kernels  49.8 us (39%)
  starting transfers between devices  41.2 us (32%)
  waiting for transfers between devices  32.8 us (25%)
  local copies, waits for them, and re-layouts  2.77 us (2%)
  between operations  2.15 us (2%)
    ppermute x11, starting transfers between devices, send(): lax.ppermute(x, 'slab', [(i, i + by) for i in range(size) if 0 <= i + by...  41.2 us
    ppermute x11, waiting for transfers between devices, send(): lax.ppermute(x, 'slab', [(i, i + by) for i in range(size) if 0 <= i + by...  32.8 us
    pallas_call x1, Pallas kernels, reduce_levels(): second(onsite[0], hop_left[0], hop_left[1], hop[0], hop[1], z_left, inver...  9.61 us
    pallas_call x1, Pallas kernels, reduce_levels(): second(onsite[1], hop_left[1], hop[0], hop[1], hop_right, inverse_a, z_ri...  9.6 us
    pallas_call x1, Pallas kernels, reduce_levels(): state_b = third(*state_b[:3], below_b, above_b, scalars_a)  8.76 us
    pallas_call x1, Pallas kernels, reduce_levels(): state_a = third(*state_a[:3], below_a, above_a, scalars_a)  8.34 us
    pallas_call x1, Pallas kernels, reduce_levels(): pl.pallas_call(first_kernel, out_shape=(block, shape(4 * w, w)), in_specs...  7 us
    pallas_call x1, Pallas kernels, reduce_levels(): pl.pallas_call(last_kernel, grid=(1,), out_shape=(whole,) * 3, in_specs=[...  2.85 us
  transfers between devices with their start and end apart: 11, of which 5 were waited for; matrix products, arithmetic and copies ran while one was open for 0% of the time, Pallas kernels for 37%

commit v1 on v0

--- a/solution.py
+++ b/solution.py
@@ -174,18 +174,18 @@
     return shift - onsite
 
 
-def deferred(out, a, b, sign):
+def deferred(out, k, a, b, sign):
     a_high, a_low = split(a)
     b_high, b_low = split(b)
 
     def lead():
-        put(out, sign * dot(a_high, emb(b_high)))
+        put(out.at[k], sign * dot(a_high, emb(b_high)))
 
     def middle():
-        put(out, row(out[...]) + sign * dot(a_high, emb(b_low)))
+        put(out.at[k], row(out[k]) + sign * dot(a_high, emb(b_low)))
 
     def trail():
-        put(out, row(out[...]) + sign * dot(a_low, emb(b_high)))
+        put(out.at[k], row(out[k]) + sign * dot(a_low, emb(b_high)))
 
     return lead, middle, trail
 
@@ -198,11 +198,15 @@
     return piece
 
 
-def solve(d, lower, upper, side, eta, payload, work):
+def solve(d, couplings, side, eta, payload, work):
     invert([d], eta, work, side)
     z = work[0][0]
-    put(payload, product(z, row(upper[...])))
-    put(payload, product(z, row(lower[...])), upper.shape[0])
+    for k in range(2):
+        put(payload.at[k], product(z, row(couplings[1 - k])))
+
+
+def sides(parity):
+    return 1 - parity, parity
 
 
 def first_kernel(onsite, hop, scalars, up, down, sem, *work):
@@ -216,7 +220,7 @@
 
 
 def second_kernel(
-    onsite, h_m2, h_m1, h_0, h_p1, z_m, z_p, scalars, d_out, l_out, u_out, payload, *work
+    onsite, h_m2, h_m1, h_0, h_p1, z_m, z_p, scalars, d_out, c_out, payload, *work
 ):
     h0, hm = row(h_0[...]), row(h_m1[...])
     from_above = product(h0, row(z_p[...]))
@@ -227,54 +231,43 @@
         - product(from_below, hm)
     )
     put(d_out, d)
-    set_upper = deferred(u_out, from_above, row(h_p1[...]), -scalars[2])
-    set_lower = deferred(l_out, from_below, adjoint(row(h_m2[...])), -1.0)
+    set_upper = deferred(c_out, 1, from_above, row(h_p1[...]), -scalars[2])
+    set_lower = deferred(c_out, 0, from_below, adjoint(row(h_m2[...])), -1.0)
     side = [paired(*pair) for pair in zip(set_upper, set_lower)]
-    solve(row(d_out[...]), l_out, u_out, side, scalars[1], payload, work)
-
-
-def third_kernel(
-    d_in, l_in, u_in, below, above, scalars, d_out, l_out, u_out, payload, *work
+    solve(row(d_out[...]), c_out, side, scalars[1], payload, work)
+
+
+def third_kernel(d_in, c_in, even, odd, scalars, parity, d_out, c_out, payload, *work):
+    i, j = sides(parity[0])
+    one, two = row(c_in[i]), row(c_in[j])
+    d = row(d_in[...]) - product(one, row(even[i])) - product(two, row(odd[j]))
+    put(d_out, d)
+    set_one = deferred(c_out, i, one, row(even[1 - i]), -1.0)
+    set_two = deferred(c_out, j, two, row(odd[1 - j]), -1.0)
+    side = [paired(*pair) for pair in zip(set_one, set_two)]
+    solve(row(d_out[...]), c_out, side, scalars[1], payload, work)
+
+
+def last_odd(d_in, c_in, odd, parity, d_mid, c_mid):
+    _, j = sides(parity[1])
+    two = row(c_in[j])
+    put(d_mid, row(d_in[...]) - product(two, row(odd[j])))
+    put(c_mid, -product(two, row(odd[1 - j])))
+
+
+def last_even(d_mid, c_mid, c_in, even, parity, d_out, u_out, l_out):
+    i, _ = sides(parity[1])
+    one = row(c_in[i])
+    put(d_out.at[0], row(d_mid[...]) - product(one, row(even[i])))
+    mine, other = -product(one, row(even[1 - i])), row(c_mid[...])
+    put(u_out.at[0], jnp.where(i == 1, mine, other))
+    put(l_out.at[0], jnp.where(i == 1, other, mine))
+
+
+def last_even_beside(
+    d_mid, c_mid, c_in, even, parity, d_old, u_old, l_old, d_out, u_out, l_out
 ):
-    w = d_in.shape[1]
-    lower, upper = row(l_in[...]), row(u_in[...])
-    d = (
-        row(d_in[...])
-        - product(lower, row(below[: 2 * w]))
-        - product(upper, row(above[2 * w :]))
-    )
-    put(d_out, d)
-    set_upper = deferred(u_out, upper, row(above[: 2 * w]), -1.0)
-    set_lower = deferred(l_out, lower, row(below[2 * w :]), -1.0)
-    side = [paired(*pair) for pair in zip(set_upper, set_lower)]
-    solve(row(d_out[...]), l_out, u_out, side, scalars[1], payload, work)
-
-
-def last_kernel(d_in, l_in, u_in, below, above, d_out, u_out, l_out):
-    w = d_in.shape[1]
-    lower, upper = row(l_in[...]), row(u_in[...])
-    d = (
-        row(d_in[...])
-        - product(lower, row(below[: 2 * w]))
-        - product(upper, row(above[2 * w :]))
-    )
-    put(d_out.at[0], d)
-    put(l_out.at[0], -product(lower, row(below[2 * w :])))
-    put(u_out.at[0], -product(upper, row(above[: 2 * w])))
-
-
-def last_below(d_in, l_in, below, l_old, d_mid, l_out):
-    w = d_in.shape[1]
-    lower = row(l_in[...])
-    put(d_mid, row(d_in[...]) - product(lower, row(below[: 2 * w])))
-    put(l_out.at[0], -product(lower, row(below[2 * w :])))
-
-
-def last_above(d_mid, u_in, above, d_old, u_old, d_out, u_out):
-    w = d_mid.shape[1]
-    upper = row(u_in[...])
-    put(d_out.at[0], row(d_mid[...]) - product(upper, row(above[2 * w :])))
-    put(u_out.at[0], -product(upper, row(above[: 2 * w])))
+    last_even(d_mid, c_mid, c_in, even, parity, d_out, u_out, l_out)
 
 
 def shape(*dims):
@@ -293,12 +286,23 @@
     ]
 
 
-PARAMS = pltpu.CompilerParams(vmem_limit_bytes=24 << 20)
+PARAMS = pltpu.CompilerParams(vmem_limit_bytes=20 << 20)
 
 
 def send(x, by):
     size = lax.axis_size("slab")
     return lax.ppermute(x, "slab", [(i, i + by) for i in range(size) if 0 <= i + by < size])
+
+
+def swaps(x, by):
+    size = lax.axis_size("slab")
+    even, odd = [], []
+    for i in range(size - by):
+        pairs = odd if i // by % 2 else even
+        pairs += [(i, i + by), (i + by, i)]
+    from_odd = lax.ppermute(x, "slab", odd)
+    from_even = lax.ppermute(x, "slab", even)
+    return from_even, from_odd
 
 
 def reduce_levels(onsite, hop, energy_level, broadening):
@@ -326,74 +330,75 @@
     inverse_a = inverse_hop_a[: 2 * w]
     z_right, hop_right = z_hop_right[: 2 * w], z_hop_right[2 * w :]
 
+    position = lax.axis_index("slab")
+    parity = jnp.stack([position % 2, position // 2 % 2]).astype(jnp.int32)
+    two = shape(2, 2 * w, w)
     second = pl.pallas_call(
         second_kernel,
-        out_shape=(block, block, block, shape(4 * w, w)),
+        out_shape=(block, two, two),
         in_specs=[VMEM] * 7 + [SMEM],
-        out_specs=(VMEM,) * 4,
+        out_specs=(VMEM,) * 3,
         scratch_shapes=work(1, w),
         compiler_params=PARAMS,
         name="second",
     )
-    state_a = second(
+    d_a, c_a, p_a = second(
         onsite[0], hop_left[0], hop_left[1], hop[0], hop[1], z_left, inverse_b, scalars_a
     )
-    below_a, above_a = send(state_a[3], 1), send(state_a[3], -1)
-    state_b = second(
+    even_a, odd_a = swaps(p_a, 1)
+    d_b, c_b, p_b = second(
         onsite[1], hop_left[1], hop[0], hop[1], hop_right, inverse_a, z_right, scalars_b
     )
-    below_b, above_b = send(state_b[3], 1), send(state_b[3], -1)
+    even_b, odd_b = swaps(p_b, 1)
 
     third = pl.pallas_call(
         third_kernel,
-        out_shape=(block, block, block, shape(4 * w, w)),
-        in_specs=[VMEM] * 5 + [SMEM],
-        out_specs=(VMEM,) * 4,
+        out_shape=(block, two, two),
+        in_specs=[VMEM] * 4 + [SMEM] * 2,
+        out_specs=(VMEM,) * 3,
         scratch_shapes=work(1, w),
         compiler_params=PARAMS,
         name="third",
     )
-    state_a = third(*state_a[:3], below_a, above_a, scalars_a)
-    below_a, above_a = send(state_a[3], 2), send(state_a[3], -2)
-    state_b = third(*state_b[:3], below_b, above_b, scalars_a)
-    below_b, above_b = send(state_b[3], 2), send(state_b[3], -2)
+    d_a, c_a, p_a = third(d_a, c_a, even_a, odd_a, scalars_a, parity)
+    even_a, odd_a = swaps(p_a, 2)
+    d_b, c_b, p_b = third(d_b, c_b, even_b, odd_b, scalars_a, parity)
+    even_b, odd_b = swaps(p_b, 2)
 
     def at(k):
-        return pl.BlockSpec((1, 2 * w, w), lambda i: (k, 0, 0))
+        return (pl.BlockSpec((1, 2 * w, w), lambda i: (k, 0, 0)),) * 3
 
     whole = shape(rows, 2 * w, w)
-    kept = pl.BlockSpec(memory_space=pl.ANY)
-    d_out, u_out, l_out = pl.pallas_call(
-        last_kernel,
+    half = pl.pallas_call(
+        last_odd,
+        out_shape=(block, block),
+        in_specs=[VMEM] * 3 + [SMEM],
+        out_specs=(VMEM,) * 2,
+        compiler_params=PARAMS,
+        name="last_odd",
+    )
+    d_a, o_a = half(d_a, c_a, odd_a, parity)
+    out = pl.pallas_call(
+        last_even,
         grid=(1,),
         out_shape=(whole,) * 3,
-        in_specs=[VMEM] * 5,
-        out_specs=(at(0),) * 3,
-        compiler_params=PARAMS,
-        name="last",
-    )(*state_a[:3], below_a, above_a)
-    d, lower, upper = state_b[:3]
-    d, l_out = pl.pallas_call(
-        last_below,
+        in_specs=[VMEM] * 4 + [SMEM],
+        out_specs=at(0),
+        compiler_params=PARAMS,
+        name="last_even",
+    )(d_a, o_a, c_a, even_a, parity)
+    d_b, o_b = half(d_b, c_b, odd_b, parity)
+    out = pl.pallas_call(
+        last_even_beside,
         grid=(1,),
-        out_shape=(block, whole),
-        in_specs=[VMEM] * 3 + [kept],
-        out_specs=(VMEM, at(1)),
-        input_output_aliases={3: 1},
-        compiler_params=PARAMS,
-        name="last_below",
-    )(d, lower, below_b, l_out)
-    d_out, u_out = pl.pallas_call(
-        last_above,
-        grid=(1,),
-        out_shape=(whole, whole),
-        in_specs=[VMEM] * 3 + [kept] * 2,
-        out_specs=(at(1), at(1)),
-        input_output_aliases={3: 0, 4: 1},
-        compiler_params=PARAMS,
-        name="last_above",
-    )(d, upper, above_b, d_out, u_out)
-    return tuple(x.reshape(rows, 2, w, w) for x in (d_out, u_out, l_out))
+        out_shape=(whole,) * 3,
+        in_specs=[VMEM] * 4 + [SMEM] + [pl.BlockSpec(memory_space=pl.ANY)] * 3,
+        out_specs=at(1),
+        input_output_aliases={5: 0, 6: 1, 7: 2},
+        compiler_params=PARAMS,
+        name="last_even_beside",
+    )(d_b, o_b, c_b, even_b, parity, *out)
+    return tuple(x.reshape(rows, 2, w, w) for x in out)
 
 
 def solution(mesh):

time: 129 us -> 140 us (1.085)
  the two profiles are of different devices: /device:TPU:62 before, /device:TPU:32 now
where the time goes in v1:
time: 140 us; the launch traced here: 139 us
  waiting for transfers between devices  52.4 us (37%)
  Pallas kernels  52.1 us (37%)
  starting transfers between devices  27.1 us (19%)
  local copies, waits for them, and re-layouts  4.62 us (3%)
  between operations  2.15 us (2%)
    ppermute x4, waiting for transfers between devices, swaps(): from_odd = lax.ppermute(x, 'slab', odd)  31.2 us
    ppermute x4, starting transfers between devices, swaps(): from_odd = lax.ppermute(x, 'slab', odd)  15.4 us
    ppermute x4, waiting for transfers between devices, swaps(): from_even = lax.ppermute(x, 'slab', even)  11.1 us
    pallas_call x1, Pallas kernels, reduce_levels(): second(onsite[1], hop_left[1], hop[0], hop[1], hop_right, inverse_a, z_ri...  10.1 us
    ppermute x3, waiting for transfers between devices, send(): lax.ppermute(x, 'slab', [(i, i + by) for i in range(size) if 0 <= i + by...  10 us
    pallas_call x1, Pallas kernels, reduce_levels(): second(onsite[0], hop_left[0], hop_left[1], hop[0], hop[1], z_left, inver...  9.59 us
    ppermute x3, starting transfers between devices, send(): lax.ppermute(x, 'slab', [(i, i + by) for i in range(size) if 0 <= i + by...  9.56 us
    pallas_call x1, Pallas kernels, reduce_levels(): d_a, c_a, p_a = third(d_a, c_a, even_a, odd_a, scalars_a, parity)  8.75 us
  transfers between devices with their start and end apart: 11, of which 5 were waited for; matrix products, arithmetic and copies ran while one was open for 0% of the time, Pallas kernels for 36%

profile of v1, /device:TPU:32, one launch (start us, length us, event | category | flops | bytes accessed | tf_op | source)
XLA Modules:
  0.0 138.5 jit_solution(4854029944239785517)
XLA Ops:
  0.6 1.9 %collective-permute-start = (f32[2,512,256]{2,1,0:T(8,128)}, f32[2,512,256]{2,1,0:T(8,128)S(1)}, u32[]{:S(2)}, u32[]{:S(2)}) collective-permute-start(f32[2,512,256]{2,1,0:T(8,128)} %bitcast.21), channel_id=1, source_target_pairs={{0,4},{4,8},{8,12},{12,16},{16,20},{20,24},{24,28},{28,32},{32,36}... | collective-permute-start | bytes 3145736 | tf_op jit(solution)/shard_map/ppermute | solution.py:294
  3.9 0.1 pad_maximum_fusion.scalars
  3.9 1.2 copy-done
  5.2 1.2 copy-done.1
  6.4 7.0 %first.1 = (f32[512,256]{1,0:T(8,128)S(1)}, f32[1024,256]{1,0:T(8,128)S(1)}) custom-call(f32[2,512,256]{2,1,0:T(8,128)S(1)} %bitcast.20, f32[2,512,256]{2,1,0:T(8,128)S(1)} %bitcast.22, f32[3]{0:T(128)S(1)} %pad_maximum_fusion.scalars), custom_call_target="tpu_custom_call" | custom-call | tf_op jit(solution)/shard_map/first/pallas_call | solution.py:319
  13.4 5.7 %collective-permute-start.1 = (f32[1024,256]{1,0:T(8,128)S(1)}, f32[1024,256]{1,0:T(8,128)S(1)}, u32[]{:S(2)}, u32[]{:S(2)}) collective-permute-start(f32[1024,256]{1,0:T(8,128)S(1)} %get-tuple-element.27), channel_id=1, source_target_pairs={{4,0},{8,4},{12,8},{16,12},{20,16},{24,20},{28,24},{32,28},{36,32}... | collective-permute-start | bytes 3145736 | tf_op jit(solution)/shard_map/ppermute | solution.py:294
  19.1 1.9 %collective-permute-start.6 = (f32[512,256]{1,0:T(8,128)S(1)}, f32[512,256]{1,0:T(8,128)S(1)}, u32[]{:S(2)}, u32[]{:S(2)}) collective-permute-start(f32[512,256]{1,0:T(8,128)S(1)} %get-tuple-element.36.z_p), channel_id=1, source_target_pairs={{0,4},{4,8},{8,12},{12,16},{16,20},{20,24},{24,28},{28,32},{32,36}... | collective-permute-start | bytes 1572872 | tf_op jit(solution)/shard_map/ppermute | solution.py:294
  21.1 0.1 pad_maximum_fusion.2.scalars
  21.2 0.1 fusion
  21.3 0.1 fusion.2
  21.4 10.0 %collective-permute-done.1 = f32[1024,256]{1,0:T(8,128)S(1)} collective-permute-done((f32[1024,256]{1,0:T(8,128)S(1)}, f32[1024,256]{1,0:T(8,128)S(1)}, u32[]{:S(2)}, u32[]{:S(2)}) %collective-permute-start.1) | collective-permute-done | bytes 1048608 | tf_op jit(solution)/shard_map/ppermute | solution.py:294
  31.5 10.1 %second.2 = (f32[512,256]{1,0:T(8,128)S(1)}, f32[2,512,256]{2,1,0:T(8,128)S(1)}, f32[2,512,256]{2,1,0:T(8,128)}) custom-call(f32[512,256]{1,0:T(8,128)S(1)} %bitcast.24, f32[512,256]{1,0:T(8,128)S(1)} %get-tuple-element.52.h_m2.h_m1, f32[512,256]{1,0:T(8,128)S(1)} %bitcast.18, f32[512,256]{1,0:T(8,128)S(1)} %bitcast.16, ...), custom_call_target="tpu_custom_call" | custom-call | tf_op jit(solution)/shard_map/second/pallas_call | solution.py:349
  41.6 5.1 %collective-permute-start.3 = (f32[2,512,256]{2,1,0:T(8,128)}, f32[2,512,256]{2,1,0:T(8,128)}, u32[]{:S(2)}, u32[]{:S(2)}) collective-permute-start(f32[2,512,256]{2,1,0:T(8,128)} %get-tuple-element.30), channel_id=1, source_target_pairs={{4,8},{8,4},{12,16},{16,12},{20,24},{24,20},{28,32},{32,28},{36,40... | collective-permute-start | bytes 3145736 | tf_op jit(solution)/shard_map/ppermute | solution.py:303
  46.7 9.6 %second.3 = (f32[512,256]{1,0:T(8,128)S(1)}, f32[2,512,256]{2,1,0:T(8,128)S(1)}, f32[2,512,256]{2,1,0:T(8,128)}) custom-call(f32[512,256]{1,0:T(8,128)S(1)} %bitcast.23, f32[512,256]{1,0:T(8,128)S(1)} %get-tuple-element.51.h_m2, f32[512,256]{1,0:T(8,128)S(1)} %get-tuple-element.52.h_m2.h_m1, f32[512,256]{1,0:T(8,128)S(1)} %bitcast.19, ...), custom_call_target="tpu_custom_call" | custom-call | tf_op jit(solution)/shard_map/second/pallas_call | solution.py:345
  56.3 0.8 copy-done.4
  57.1 3.4 %collective-permute-start.8 = (f32[2,512,256]{2,1,0:T(8,128)}, f32[2,512,256]{2,1,0:T(8,128)}, u32[]{:S(2)}, u32[]{:S(2)}) collective-permute-start(f32[2,512,256]{2,1,0:T(8,128)} %get-tuple-element.39), channel_id=1, source_target_pairs={{4,8},{8,4},{12,16},{16,12},{20,24},{24,20},{28,32},{32,28},{36,40... | collective-permute-start | bytes 3145736 | tf_op jit(solution)/shard_map/ppermute | solution.py:303
  60.5 0.1 pad_add_fusion.parity
  60.6 1.0 copy-done.3
  61.6 8.5 %third.2 = (f32[512,256]{1,0:T(8,128)S(1)}, f32[2,512,256]{2,1,0:T(8,128)S(1)}, f32[2,512,256]{2,1,0:T(8,128)S(1)}) custom-call(f32[512,256]{1,0:T(8,128)S(1)} %copy-done.3, f32[2,512,256]{2,1,0:T(8,128)S(1)} %get-tuple-element.29.c_in, f32[2,512,256]{2,1,0:T(8,128)S(1)} %collective-permute-done.2.even, f32[2,512,256]{2,1,0:T(8,128)} %collective-permute-done.3.odd, ...), custom_call_target="tpu_custom_call" | custom-call | tf_op jit(solution)/shard_map/third/pallas_call | solution.py:365
  70.1 3.8 %collective-permute-start.4 = (f32[2,512,256]{2,1,0:T(8,128)S(1)}, f32[2,512,256]{2,1,0:T(8,128)S(1)}, u32[]{:S(2)}, u32[]{:S(2)}) collective-permute-start(f32[2,512,256]{2,1,0:T(8,128)S(1)} %get-tuple-element.33), channel_id=1, source_target_pairs={{8,16},{16,8},{12,20},{20,12},{24,32},{32,24},{28,36},{36,28},{40,... | collective-permute-start | bytes 3145736 | tf_op jit(solution)/shard_map/ppermute | solution.py:303
  73.9 1.7 %collective-permute-done.8.odd = f32[2,512,256]{2,1,0:T(8,128)} collective-permute-done((f32[2,512,256]{2,1,0:T(8,128)}, f32[2,512,256]{2,1,0:T(8,128)}, u32[]{:S(2)}, u32[]{:S(2)}) %collective-permute-start.8) | collective-permute-done | bytes 1048608 | tf_op jit(solution)/shard_map/ppermute | solution.py:303
  75.6 8.7 %third.3 = (f32[512,256]{1,0:T(8,128)S(1)}, f32[2,512,256]{2,1,0:T(8,128)S(1)}, f32[2,512,256]{2,1,0:T(8,128)S(1)}) custom-call(f32[512,256]{1,0:T(8,128)S(1)} %copy-done.5, f32[2,512,256]{2,1,0:T(8,128)S(1)} %get-tuple-element.38.c_in, f32[2,512,256]{2,1,0:T(8,128)} %collective-permute-done.7.even, f32[2,512,256]{2,1,0:T(8,128)} %collective-permute-done.8.odd, ...), custom_call_target="tpu_custom_call" | custom-call | tf_op jit(solution)/shard_map/third/pallas_call | solution.py:363
  84.4 3.2 %collective-permute-start.9 = (f32[2,512,256]{2,1,0:T(8,128)S(1)}, f32[2,512,256]{2,1,0:T(8,128)S(1)}, u32[]{:S(2)}, u32[]{:S(2)}) collective-permute-start(f32[2,512,256]{2,1,0:T(8,128)S(1)} %get-tuple-element.42), channel_id=1, source_target_pairs={{8,16},{16,8},{12,20},{20,12},{24,32},{32,24},{28,36},{36,28},{40,... | collective-permute-start | bytes 3145736 | tf_op jit(solution)/shard_map/ppermute | solution.py:303
  87.6 0.1 collective-permute-start.10
  87.7 2.0 %collective-permute-start.5 = (f32[2,512,256]{2,1,0:T(8,128)S(1)}, f32[2,512,256]{2,1,0:T(8,128)S(1)}, u32[]{:S(2)}, u32[]{:S(2)}) collective-permute-start(f32[2,512,256]{2,1,0:T(8,128)S(1)} %get-tuple-element.33), channel_id=1, source_target_pairs={{0,8},{8,0},{4,12},{12,4},{16,24},{24,16},{20,28},{28,20},{32,40},... | collective-permute-start | bytes 3145736 | tf_op jit(solution)/shard_map/ppermute | solution.py:304
  89.7 10.5 %collective-permute-done.4.odd = f32[2,512,256]{2,1,0:T(8,128)S(1)} collective-permute-done((f32[2,512,256]{2,1,0:T(8,128)S(1)}, f32[2,512,256]{2,1,0:T(8,128)S(1)}, u32[]{:S(2)}, u32[]{:S(2)}) %collective-permute-start.4) | collective-permute-done | bytes 1048608 | tf_op jit(solution)/shard_map/ppermute | solution.py:303
  100.2 1.6 %last_odd.2 = (f32[512,256]{1,0:T(8,128)S(1)}, f32[512,256]{1,0:T(8,128)S(1)}) custom-call(f32[512,256]{1,0:T(8,128)S(1)} %get-tuple-element.31.d_in, f32[2,512,256]{2,1,0:T(8,128)S(1)} %get-tuple-element.32.c_in, f32[2,512,256]{2,1,0:T(8,128)S(1)} %collective-permute-done.4.odd, s32[2]{0:T(128)S(1)} %pad_add_fusion.parity), custom_call_target="tpu_custom_call" | custom-call | tf_op jit(solution)/shard_map/last_odd/pallas_call | solution.py:390
  101.7 19.0 %collective-permute-done.9.odd = f32[2,512,256]{2,1,0:T(8,128)S(1)} collective-permute-done((f32[2,512,256]{2,1,0:T(8,128)S(1)}, f32[2,512,256]{2,1,0:T(8,128)S(1)}, u32[]{:S(2)}, u32[]{:S(2)}) %collective-permute-start.9) | collective-permute-done | bytes 1048608 | tf_op jit(solution)/shard_map/ppermute | solution.py:303
  120.7 1.6 %last_odd.3 = (f32[512,256]{1,0:T(8,128)S(1)}, f32[512,256]{1,0:T(8,128)S(1)}) custom-call(f32[512,256]{1,0:T(8,128)S(1)} %get-tuple-element.40.d_in, f32[2,512,256]{2,1,0:T(8,128)S(1)} %get-tuple-element.41.c_in, f32[2,512,256]{2,1,0:T(8,128)S(1)} %collective-permute-done.9.odd, s32[2]{0:T(128)S(1)} %pad_add_fusion.parity), custom_call_target="tpu_custom_call" | custom-call | tf_op jit(solution)/shard_map/last_odd/pallas_call | solution.py:380
  122.3 2.5 %last_even.1 = (f32[2,512,256]{2,1,0:T(8,128)}, f32[2,512,256]{2,1,0:T(8,128)}, f32[2,512,256]{2,1,0:T(8,128)}) custom-call(f32[512,256]{1,0:T(8,128)S(1)} %get-tuple-element.43.d_mid, f32[512,256]{1,0:T(8,128)S(1)} %get-tuple-element.44.c_mid, f32[2,512,256]{2,1,0:T(8,128)S(1)} %get-tuple-element.41.c_in, f32[2,512,256]{2,1,0:T(8,128)S(1)} %collective-permute-done.10.even, ...), custom_call_target="tpu_custom_call" | custom-call | tf_op jit(solution)/shard_map/last_even/pallas_call | solution.py:381
  124.8 11.1 %collective-permute-done.5.even = f32[2,512,256]{2,1,0:T(8,128)S(1)} collective-permute-done((f32[2,512,256]{2,1,0:T(8,128)S(1)}, f32[2,512,256]{2,1,0:T(8,128)S(1)}, u32[]{:S(2)}, u32[]{:S(2)}) %collective-permute-start.5) | collective-permute-done | bytes 1048608 | tf_op jit(solution)/shard_map/ppermute | solution.py:304
  136.0 2.5 %last_even_beside.1 = (f32[2,512,256]{2,1,0:T(8,128)}, f32[2,512,256]{2,1,0:T(8,128)}, f32[2,512,256]{2,1,0:T(8,128)}) custom-call(f32[512,256]{1,0:T(8,128)S(1)} %get-tuple-element.34.d_mid, f32[512,256]{1,0:T(8,128)S(1)} %get-tuple-element.35.c_mid, ...), custom_call_target="tpu_custom_call", output_to_operand_aliasing={{0}: (5, {}), {1}: (6, {}), {2}: (7, {})} | custom-call | tf_op jit(solution)/shard_map/last_even_beside/pallas_call | solution.py:391
  (19 shorter events, 0.2 us)
Async XLA Ops:
  0.6 20.7 %collective-permute-start = (f32[2,512,256]{2,1,0:T(8,128)}, f32[2,512,256]{2,1,0:T(8,128)S(1)}, u32[]{:S(2)}, u32[]{:S(2)}) collective-permute-start(f32[2,512,256]{2,1,0:T(8,128)} %bitcast.21), channel_id=1, source_target_pairs={{0,4},{4,8},{8,12},{12,16},{16,20},{20,24},{24,28},{28,32},{32,36}... | collective-permute-start | bytes 3145736 | tf_op jit(solution)/shard_map/ppermute | solution.py:294
  3.9 1.2 copy-start
  5.2 1.2 copy-start.1
  13.4 18.0 %collective-permute-start.1 = (f32[1024,256]{1,0:T(8,128)S(1)}, f32[1024,256]{1,0:T(8,128)S(1)}, u32[]{:S(2)}, u32[]{:S(2)}) collective-permute-start(f32[1024,256]{1,0:T(8,128)S(1)} %get-tuple-element.27), channel_id=1, source_target_pairs={{4,0},{8,4},{12,8},{16,12},{20,16},{24,20},{28,24},{32,28},{36,32}... | collective-permute-start | bytes 3145736 | tf_op jit(solution)/shard_map/ppermute | solution.py:294
  19.1 27.6 %collective-permute-start.6 = (f32[512,256]{1,0:T(8,128)S(1)}, f32[512,256]{1,0:T(8,128)S(1)}, u32[]{:S(2)}, u32[]{:S(2)}) collective-permute-start(f32[512,256]{1,0:T(8,128)S(1)} %get-tuple-element.36.z_p), channel_id=1, source_target_pairs={{0,4},{4,8},{8,12},{12,16},{16,20},{20,24},{24,28},{28,32},{32,36}... | collective-permute-start | bytes 1572872 | tf_op jit(solution)/shard_map/ppermute | solution.py:294
  41.6 14.7 %copy-start.2 = (f32[512,256]{1,0:T(8,128)}, f32[512,256]{1,0:T(8,128)S(1)}, u32[]{:S(2)}) copy-start(f32[512,256]{1,0:T(8,128)S(1)} %get-tuple-element.28.d_in) | copy-start | bytes 1572868
  41.6 19.0 %collective-permute-start.2 = (f32[2,512,256]{2,1,0:T(8,128)}, f32[2,512,256]{2,1,0:T(8,128)S(1)}, u32[]{:S(2)}, u32[]{:S(2)}) collective-permute-start(f32[2,512,256]{2,1,0:T(8,128)} %get-tuple-element.30), channel_id=1, source_target_pairs={{0,4},{4,0},{8,12},{12,8},{16,20},{20,16},{24,28},{28,24},{32,36},... | collective-permute-start | bytes 3145736 | tf_op jit(solution)/shard_map/ppermute | solution.py:304
  41.6 19.0 %collective-permute-start.3 = (f32[2,512,256]{2,1,0:T(8,128)}, f32[2,512,256]{2,1,0:T(8,128)}, u32[]{:S(2)}, u32[]{:S(2)}) collective-permute-start(f32[2,512,256]{2,1,0:T(8,128)} %get-tuple-element.30), channel_id=1, source_target_pairs={{4,8},{8,4},{12,16},{16,12},{20,24},{24,20},{28,32},{32,28},{36,40... | collective-permute-start | bytes 3145736 | tf_op jit(solution)/shard_map/ppermute | solution.py:303
  56.3 0.8 copy-start.4
  57.1 16.8 %collective-permute-start.7 = (f32[2,512,256]{2,1,0:T(8,128)}, f32[2,512,256]{2,1,0:T(8,128)}, u32[]{:S(2)}, u32[]{:S(2)}) collective-permute-start(f32[2,512,256]{2,1,0:T(8,128)} %get-tuple-element.39), channel_id=1, source_target_pairs={{0,4},{4,0},{8,12},{12,8},{16,20},{20,16},{24,28},{28,24},{32,36},... | collective-permute-start | bytes 3145736 | tf_op jit(solution)/shard_map/ppermute | solution.py:304
  57.1 18.5 %collective-permute-start.8 = (f32[2,512,256]{2,1,0:T(8,128)}, f32[2,512,256]{2,1,0:T(8,128)}, u32[]{:S(2)}, u32[]{:S(2)}) collective-permute-start(f32[2,512,256]{2,1,0:T(8,128)} %get-tuple-element.39), channel_id=1, source_target_pairs={{4,8},{8,4},{12,16},{16,12},{20,24},{24,20},{28,32},{32,28},{36,40... | collective-permute-start | bytes 3145736 | tf_op jit(solution)/shard_map/ppermute | solution.py:303
  60.6 1.0 copy-start.3
  61.6 14.0 %copy-start.5 = (f32[512,256]{1,0:T(8,128)S(1)}, f32[512,256]{1,0:T(8,128)}, u32[]{:S(2)}) copy-start(f32[512,256]{1,0:T(8,128)} %copy-done.4) | copy-start | bytes 1572868
  70.1 30.0 %collective-permute-start.4 = (f32[2,512,256]{2,1,0:T(8,128)S(1)}, f32[2,512,256]{2,1,0:T(8,128)S(1)}, u32[]{:S(2)}, u32[]{:S(2)}) collective-permute-start(f32[2,512,256]{2,1,0:T(8,128)S(1)} %get-tuple-element.33), channel_id=1, source_target_pairs={{8,16},{16,8},{12,20},{20,12},{24,32},{32,24},{28,36},{36,28},{40,... | collective-permute-start | bytes 3145736 | tf_op jit(solution)/shard_map/ppermute | solution.py:303
  84.4 36.3 %collective-permute-start.9 = (f32[2,512,256]{2,1,0:T(8,128)S(1)}, f32[2,512,256]{2,1,0:T(8,128)S(1)}, u32[]{:S(2)}, u32[]{:S(2)}) collective-permute-start(f32[2,512,256]{2,1,0:T(8,128)S(1)} %get-tuple-element.42), channel_id=1, source_target_pairs={{8,16},{16,8},{12,20},{20,12},{24,32},{32,24},{28,36},{36,28},{40,... | collective-permute-start | bytes 3145736 | tf_op jit(solution)/shard_map/ppermute | solution.py:303
  87.6 34.7 %collective-permute-start.10 = (f32[2,512,256]{2,1,0:T(8,128)S(1)}, f32[2,512,256]{2,1,0:T(8,128)S(1)}, u32[]{:S(2)}, u32[]{:S(2)}) collective-permute-start(f32[2,512,256]{2,1,0:T(8,128)S(1)} %get-tuple-element.42), channel_id=1, source_target_pairs={{0,8},{8,0},{4,12},{12,4},{16,24},{24,16},{20,28},{28,20},{32,40},... | collective-permute-start | bytes 3145736 | tf_op jit(solution)/shard_map/ppermute | solution.py:304
  87.7 48.3 %collective-permute-start.5 = (f32[2,512,256]{2,1,0:T(8,128)S(1)}, f32[2,512,256]{2,1,0:T(8,128)S(1)}, u32[]{:S(2)}, u32[]{:S(2)}) collective-permute-start(f32[2,512,256]{2,1,0:T(8,128)S(1)} %get-tuple-element.33), channel_id=1, source_target_pairs={{0,8},{8,0},{4,12},{12,4},{16,24},{24,16},{20,28},{28,20},{32,40},... | collective-permute-start | bytes 3145736 | tf_op jit(solution)/shard_map/ppermute | solution.py:304

commit v2 on v1

--- a/solution.py
+++ b/solution.py
@@ -11,7 +11,7 @@
 BF = jnp.bfloat16
 F32 = jnp.float32
 HIGHEST = lax.Precision.HIGHEST
-CONVERGED = 0.998
+CONVERGED = 0.985
 TRUSTED = 0.012
 VMEM = pl.BlockSpec(memory_space=pltpu.VMEM)
 SMEM = pl.BlockSpec(memory_space=pltpu.SMEM)
@@ -202,7 +202,12 @@
     invert([d], eta, work, side)
     z = work[0][0]
     for k in range(2):
-        put(payload.at[k], product(z, row(couplings[1 - k])))
+        put(payload, product(z, row(couplings[1 - k])), k * d.shape[1])
+
+
+def part(payload, k):
+    rows = 2 * payload.shape[1]
+    return row(payload[pl.ds(pl.multiple_of(k * rows, rows), rows)])
 
 
 def sides(parity):
@@ -219,31 +224,36 @@
     beside.wait()
 
 
-def second_kernel(
-    onsite, h_m2, h_m1, h_0, h_p1, z_m, z_p, scalars, d_out, c_out, payload, *work
-):
-    h0, hm = row(h_0[...]), row(h_m1[...])
-    from_above = product(h0, row(z_p[...]))
-    from_below = product(adjoint(hm), row(z_m[...]))
-    d = (
-        initial(row(onsite[...]), scalars)
-        - product(from_above, adjoint(h0))
-        - product(from_below, hm)
-    )
-    put(d_out, d)
-    set_upper = deferred(c_out, 1, from_above, row(h_p1[...]), -scalars[2])
-    set_lower = deferred(c_out, 0, from_below, adjoint(row(h_m2[...])), -1.0)
-    side = [paired(*pair) for pair in zip(set_upper, set_lower)]
-    solve(row(d_out[...]), c_out, side, scalars[1], payload, work)
+def near_kernel(onsite, hop, hop_left, z_b, z_hop_a, scalars, d_a, d_b, u_a, l_b, g_a, k_a):
+    h = row(hop[0])
+    before = row(hop_left[1])
+    put(g_a, adjoint(before))
+    put(k_a, adjoint(row(hop_left[0])))
+    t = product(h, row(z_b[...]))
+    put(d_a, initial(row(onsite[0]), scalars) - product(t, adjoint(h)))
+    put(u_a, product(t, row(hop[1])) * (-scalars[2]))
+    t = product(adjoint(h), part(z_hop_a, 0))
+    put(d_b, initial(row(onsite[1]), scalars) - product(t, h))
+    put(l_b, -product(t, adjoint(before)))
+
+
+def second_kernel(d_in, c_in, g, z, k, scalars, side, d_out, c_out, payload, *work):
+    at = side[0]
+    gain = row(g[...])
+    t = product(gain, row(z[...]))
+    put(d_out, row(d_in[...]) - product(t, adjoint(gain)))
+    c_out[1 - at] = c_in[...]
+    pieces = deferred(c_out, at, t, row(k[...]), -1.0)
+    solve(row(d_out[...]), c_out, pieces, scalars[1], payload, work)
 
 
 def third_kernel(d_in, c_in, even, odd, scalars, parity, d_out, c_out, payload, *work):
     i, j = sides(parity[0])
     one, two = row(c_in[i]), row(c_in[j])
-    d = row(d_in[...]) - product(one, row(even[i])) - product(two, row(odd[j]))
+    d = row(d_in[...]) - product(one, part(even, i)) - product(two, part(odd, j))
     put(d_out, d)
-    set_one = deferred(c_out, i, one, row(even[1 - i]), -1.0)
-    set_two = deferred(c_out, j, two, row(odd[1 - j]), -1.0)
+    set_one = deferred(c_out, i, one, part(even, 1 - i), -1.0)
+    set_two = deferred(c_out, j, two, part(odd, 1 - j), -1.0)
     side = [paired(*pair) for pair in zip(set_one, set_two)]
     solve(row(d_out[...]), c_out, side, scalars[1], payload, work)
 
@@ -251,23 +261,32 @@
 def last_odd(d_in, c_in, odd, parity, d_mid, c_mid):
     _, j = sides(parity[1])
     two = row(c_in[j])
-    put(d_mid, row(d_in[...]) - product(two, row(odd[j])))
-    put(c_mid, -product(two, row(odd[1 - j])))
-
-
-def last_even(d_mid, c_mid, c_in, even, parity, d_out, u_out, l_out):
+    put(d_mid, row(d_in[...]) - product(two, part(odd, j)))
+    put(c_mid, -product(two, part(odd, 1 - j)))
+
+
+def last_even(slab, d_mid, c_mid, c_in, even, parity, d_out, u_out, l_out, hold, sems):
     i, _ = sides(parity[1])
     one = row(c_in[i])
-    put(d_out.at[0], row(d_mid[...]) - product(one, row(even[i])))
-    mine, other = -product(one, row(even[1 - i])), row(c_mid[...])
-    put(u_out.at[0], jnp.where(i == 1, mine, other))
-    put(l_out.at[0], jnp.where(i == 1, other, mine))
+    mine, other = -product(one, part(even, 1 - i)), row(c_mid[...])
+    copies = [
+        pltpu.make_async_copy(hold.at[k], out.at[slab], sems.at[k])
+        for k, out in enumerate((u_out, l_out, d_out))
+    ]
+    put(hold.at[0], jnp.where(i == 1, mine, other))
+    put(hold.at[1], jnp.where(i == 1, other, mine))
+    copies[0].start()
+    copies[1].start()
+    put(hold.at[2], row(d_mid[...]) - product(one, part(even, i)))
+    copies[2].start()
+    for copy in copies:
+        copy.wait()
 
 
 def last_even_beside(
-    d_mid, c_mid, c_in, even, parity, d_old, u_old, l_old, d_out, u_out, l_out
+    d_mid, c_mid, c_in, even, parity, d_old, u_old, l_old, d_out, u_out, l_out, hold, sems
 ):
-    last_even(d_mid, c_mid, c_in, even, parity, d_out, u_out, l_out)
+    last_even(1, d_mid, c_mid, c_in, even, parity, d_out, u_out, l_out, hold, sems)
 
 
 def shape(*dims):
@@ -311,64 +330,72 @@
     hop = hop.reshape(rows, 2 * w, w)
     last = lax.axis_index("slab") == lax.axis_size("slab") - 1
     keep = jnp.where(last, 0.0, 1.0).astype(F32)
-    scalars_a = jnp.stack([energy_level[0], broadening[0], keep])
-    scalars_b = jnp.stack([energy_level[0], broadening[0], jnp.float32(1.0)])
+    scalars = jnp.stack([energy_level[0], broadening[0], keep])
+    position = lax.axis_index("slab")
+    parity = jnp.stack([position & 1, (position >> 1) & 1])
+    scalars, parity = lax.optimization_barrier((scalars, parity))
 
     hop_left = send(hop, 1)
-    block = shape(2 * w, w)
-    inverse_b, inverse_hop_a = pl.pallas_call(
+    block, pair, two = shape(2 * w, w), shape(4 * w, w), shape(2, 2 * w, w)
+    up, down = pl.pallas_call(
         first_kernel,
-        out_shape=(block, shape(4 * w, w)),
-        in_specs=[VMEM, pl.BlockSpec(memory_space=pltpu.HBM), SMEM],
-        out_specs=(VMEM, VMEM),
+        out_shape=(block, pair),
+        in_specs=[VMEM, pl.BlockSpec(memory_space=pl.ANY), SMEM],
+        out_specs=(VMEM,) * 2,
         scratch_shapes=[pltpu.SemaphoreType.DMA] + work(rows, w),
         compiler_params=PARAMS,
         name="first",
-    )(onsite, hop, scalars_a)
-    z_left = send(inverse_b, 1)
-    z_hop_right = send(inverse_hop_a, -1)
-    inverse_a = inverse_hop_a[: 2 * w]
-    z_right, hop_right = z_hop_right[: 2 * w], z_hop_right[2 * w :]
-
-    position = lax.axis_index("slab")
-    parity = jnp.stack([position % 2, position // 2 % 2]).astype(jnp.int32)
-    two = shape(2, 2 * w, w)
+    )(onsite, pltpu.with_memory_space_constraint(hop, pltpu.HBM), scalars)
+    z_left = send(up, 1)
+    z_hop_right = send(down, -1)
+    d_a, d_b, u_a, l_b, g_a, k_a = pl.pallas_call(
+        near_kernel,
+        out_shape=(block,) * 6,
+        in_specs=[VMEM] * 5 + [SMEM],
+        out_specs=(VMEM,) * 6,
+        compiler_params=PARAMS,
+        name="near",
+    )(onsite, hop, hop_left, up, down, scalars)
+
     second = pl.pallas_call(
         second_kernel,
-        out_shape=(block, two, two),
-        in_specs=[VMEM] * 7 + [SMEM],
+        out_shape=(block, two, pair),
+        in_specs=[VMEM] * 5 + [SMEM] * 2,
         out_specs=(VMEM,) * 3,
         scratch_shapes=work(1, w),
         compiler_params=PARAMS,
         name="second",
     )
-    d_a, c_a, p_a = second(
-        onsite[0], hop_left[0], hop_left[1], hop[0], hop[1], z_left, inverse_b, scalars_a
-    )
+    d_a, c_a, p_a = second(d_a, u_a, g_a, z_left, k_a, scalars, jnp.zeros((1,), jnp.int32))
     even_a, odd_a = swaps(p_a, 1)
     d_b, c_b, p_b = second(
-        onsite[1], hop_left[1], hop[0], hop[1], hop_right, inverse_a, z_right, scalars_b
+        d_b,
+        l_b,
+        hop[1],
+        z_hop_right[: 2 * w],
+        z_hop_right[2 * w :],
+        scalars,
+        jnp.ones((1,), jnp.int32),
     )
     even_b, odd_b = swaps(p_b, 1)
 
     third = pl.pallas_call(
         third_kernel,
-        out_shape=(block, two, two),
+        out_shape=(block, two, pair),
         in_specs=[VMEM] * 4 + [SMEM] * 2,
         out_specs=(VMEM,) * 3,
         scratch_shapes=work(1, w),
         compiler_params=PARAMS,
         name="third",
     )
-    d_a, c_a, p_a = third(d_a, c_a, even_a, odd_a, scalars_a, parity)
+    d_a, c_a, p_a = third(d_a, c_a, even_a, odd_a, scalars, parity)
     even_a, odd_a = swaps(p_a, 2)
-    d_b, c_b, p_b = third(d_b, c_b, even_b, odd_b, scalars_a, parity)
+    d_b, c_b, p_b = third(d_b, c_b, even_b, odd_b, scalars, parity)
     even_b, odd_b = swaps(p_b, 2)
 
-    def at(k):
-        return (pl.BlockSpec((1, 2 * w, w), lambda i: (k, 0, 0)),) * 3
-
     whole = shape(rows, 2 * w, w)
+    kept = pl.BlockSpec(memory_space=pl.ANY)
+    hold = [pltpu.VMEM((3, 2 * w, w), F32), pltpu.SemaphoreType.DMA((3,))]
     half = pl.pallas_call(
         last_odd,
         out_shape=(block, block),
@@ -378,23 +405,24 @@
         name="last_odd",
     )
     d_a, o_a = half(d_a, c_a, odd_a, parity)
-    out = pl.pallas_call(
-        last_even,
-        grid=(1,),
+    first_half = pl.pallas_call(
+        functools.partial(last_even, 0),
         out_shape=(whole,) * 3,
         in_specs=[VMEM] * 4 + [SMEM],
-        out_specs=at(0),
+        out_specs=(kept,) * 3,
+        scratch_shapes=hold,
         compiler_params=PARAMS,
         name="last_even",
-    )(d_a, o_a, c_a, even_a, parity)
+    )
+    out = first_half(d_a, o_a, c_a, even_a, parity)
     d_b, o_b = half(d_b, c_b, odd_b, parity)
     out = pl.pallas_call(
         last_even_beside,
-        grid=(1,),
         out_shape=(whole,) * 3,
-        in_specs=[VMEM] * 4 + [SMEM] + [pl.BlockSpec(memory_space=pl.ANY)] * 3,
-        out_specs=at(1),
+        in_specs=[VMEM] * 4 + [SMEM] + [kept] * 3,
+        out_specs=(kept,) * 3,
         input_output_aliases={5: 0, 6: 1, 7: 2},
+        scratch_shapes=hold,
         compiler_params=PARAMS,
         name="last_even_beside",
     )(d_b, o_b, c_b, even_b, parity, *out)

time: 140 us -> 153 us (1.093)
  the two profiles are of different devices: /device:TPU:32 before, /device:TPU:88 now
where the time goes in v2:
time: 153 us
  Pallas kernels  72.4 us (47%)
  waiting for transfers between devices  49.5 us (32%)
  starting transfers between devices  27.1 us (18%)
  between operations  2.31 us (2%)
    ppermute x4, waiting for transfers between devices, swaps(): from_odd = lax.ppermute(x, 'slab', odd)  32.7 us
    pallas_call x1, Pallas kernels, reduce_levels(): second(d_b, l_b, hop[1], z_hop_right[:2 * w], z_hop_right[2 * w:], scalar...  29.7 us
    ppermute x4, starting transfers between devices, swaps(): from_odd = lax.ppermute(x, 'slab', odd)  15 us
    ppermute x4, waiting for transfers between devices, swaps(): from_even = lax.ppermute(x, 'slab', even)  9.82 us
    ppermute x3, starting transfers between devices, send(): lax.ppermute(x, 'slab', [(i, i + by) for i in range(size) if 0 <= i + by...  9.6 us
    pallas_call x1, Pallas kernels, reduce_levels(): d_b, c_b, p_b = third(d_b, c_b, even_b, odd_b, scalars, parity)  8.25 us
    pallas_call x1, Pallas kernels, reduce_levels(): d_a, c_a, p_a = third(d_a, c_a, even_a, odd_a, scalars, parity)  8.25 us
    pallas_call x1, Pallas kernels, reduce_levels(): second(d_a, u_a, g_a, z_left, k_a, scalars, jnp.zeros((1,), jnp.int32))  7.91 us
  transfers between devices with their start and end apart: 11, of which 6 were waited for; matrix products, arithmetic and copies ran while one was open for 0% of the time, Pallas kernels for 46%

profile of v2, /device:TPU:88, one launch (start us, length us, event | category | flops | bytes accessed | tf_op | source)
XLA Modules:
  0.0 152.7 jit_solution(16757133043570784908)
XLA Ops:
  0.6 1.9 %collective-permute-start = (f32[2,512,256]{2,1,0:T(8,128)}, f32[2,512,256]{2,1,0:T(8,128)S(1)}, u32[]{:S(2)}, u32[]{:S(2)}) collective-permute-start(f32[2,512,256]{2,1,0:T(8,128)} %bitcast.9), channel_id=1, source_target_pairs={{0,4},{4,8},{8,12},{12,16},{16,20},{20,24},{24,28},{28,32},{32,36}... | collective-permute-start | bytes 3145736 | tf_op jit(solution)/shard_map/ppermute | solution.py:313
  3.9 0.1 pad_add_fusion.parity
  3.9 0.1 pad_maximum_fusion.scalars
  4.0 1.2 copy-done.1
  5.2 6.9 %first.1 = (f32[512,256]{1,0:T(8,128)S(1)}, f32[1024,256]{1,0:T(8,128)S(1)}) custom-call(f32[2,512,256]{2,1,0:T(8,128)S(1)} %bitcast.12, f32[2,512,256]{2,1,0:T(8,128)} %bitcast.10, f32[3]{0:T(128)S(1)} %pad_maximum_fusion.scalars), custom_call_target="tpu_custom_call" | custom-call | tf_op jit(solution)/shard_map/first/pallas_call | solution.py:340
  12.2 5.8 %collective-permute-start.1 = (f32[1024,256]{1,0:T(8,128)S(1)}, f32[1024,256]{1,0:T(8,128)S(1)}, u32[]{:S(2)}, u32[]{:S(2)}) collective-permute-start(f32[1024,256]{1,0:T(8,128)S(1)} %get-tuple-element.37.z_hop_a), channel_id=1, source_target_pairs={{4,0},{8,4},{12,8},{16,12},{20,16},{24,20},{28,24},{32,28},{36,32}... | collective-permute-start | bytes 3145736 | tf_op jit(solution)/shard_map/ppermute | solution.py:313
  18.0 1.9 %collective-permute-start.6 = (f32[512,256]{1,0:T(8,128)S(1)}, f32[512,256]{1,0:T(8,128)S(1)}, u32[]{:S(2)}, u32[]{:S(2)}) collective-permute-start(f32[512,256]{1,0:T(8,128)S(1)} %get-tuple-element.36.z_b), channel_id=1, source_target_pairs={{0,4},{4,8},{8,12},{12,16},{16,20},{20,24},{24,28},{28,32},{32,36}... | collective-permute-start | bytes 1572872 | tf_op jit(solution)/shard_map/ppermute | solution.py:313
  20.0 3.3 %near.1 = (f32[512,256]{1,0:T(8,128)S(1)}, f32[512,256]{1,0:T(8,128)S(1)}, f32[512,256]{1,0:T(8,128)S(1)}, f32[512,256]{1,0:T(8,128)S(1)}, f32[512,256]{1,0:T(8,128)S(1)}, /*index=5*/f32[512,256]{1,0:T(8,128)S(1)}) custom-call(f32[2,512,256]{2,1,0:T(8,128)S(1)} %bitcast.13, f32[2,512,256]{2,1,0:T(8,128)S(1)} %bitcast.11, ...), custom_call_target="tpu_custom_call" | custom-call | tf_op jit(solution)/shard_map/near/pallas_call | solution.py:351
  23.3 7.0 %collective-permute-done.1 = f32[1024,256]{1,0:T(8,128)S(1)} collective-permute-done((f32[1024,256]{1,0:T(8,128)S(1)}, f32[1024,256]{1,0:T(8,128)S(1)}, u32[]{:S(2)}, u32[]{:S(2)}) %collective-permute-start.1) | collective-permute-done | bytes 1048608 | tf_op jit(solution)/shard_map/ppermute | solution.py:313
  30.3 0.1 fusion
  30.3 29.7 %second.2 = (f32[512,256]{1,0:T(8,128)S(1)}, f32[2,512,256]{2,1,0:T(8,128)S(1)}, f32[1024,256]{1,0:T(8,128)S(1)}) custom-call(f32[512,256]{1,0:T(8,128)S(1)} %get-tuple-element.38.d_in, f32[512,256]{1,0:T(8,128)S(1)} %get-tuple-element.39.c_in, f32[512,256]{1,0:T(8,128)S(1)} %bitcast.14, f32[512,256]{1,0:T(8,128)S(1)} %get-tuple-element.68.z, ...), custom_call_target="tpu_custom_call" | custom-call | tf_op jit(solution)/shard_map/second/pallas_call | solution.py:371
  60.1 1.9 %collective-permute-start.3 = (f32[1024,256]{1,0:T(8,128)S(1)}, f32[1024,256]{1,0:T(8,128)S(1)}, u32[]{:S(2)}, u32[]{:S(2)}) collective-permute-start(f32[1024,256]{1,0:T(8,128)S(1)} %get-tuple-element.42), channel_id=1, source_target_pairs={{4,8},{8,4},{12,16},{16,12},{20,24},{24,20},{28,32},{32,28},{36,40... | collective-permute-start | bytes 3145736 | tf_op jit(solution)/shard_map/ppermute | solution.py:322
  62.0 0.3 collective-permute-start.2
  62.3 7.9 %second.3 = (f32[512,256]{1,0:T(8,128)S(1)}, f32[2,512,256]{2,1,0:T(8,128)S(1)}, f32[1024,256]{1,0:T(8,128)S(1)}) custom-call(f32[512,256]{1,0:T(8,128)S(1)} %get-tuple-element.49.d_in, f32[512,256]{1,0:T(8,128)S(1)} %get-tuple-element.50.c_in, f32[512,256]{1,0:T(8,128)S(1)} %get-tuple-element.51.g, f32[512,256]{1,0:T(8,128)S(1)} %collective-permute-done.6.z, ...), custom_call_target="tpu_custom_call" | custom-call | tf_op jit(solution)/shard_map/second/pallas_call | solution.py:369
  70.2 5.7 %collective-permute-start.8 = (f32[1024,256]{1,0:T(8,128)S(1)}, f32[1024,256]{1,0:T(8,128)S(1)}, u32[]{:S(2)}, u32[]{:S(2)}) collective-permute-start(f32[1024,256]{1,0:T(8,128)S(1)} %get-tuple-element.55), channel_id=1, source_target_pairs={{4,8},{8,4},{12,16},{16,12},{20,24},{24,20},{28,32},{32,28},{36,40... | collective-permute-start | bytes 3145736 | tf_op jit(solution)/shard_map/ppermute | solution.py:322
  75.9 0.1 collective-permute-start.7
  76.0 2.3 %collective-permute-done.3.odd = f32[1024,256]{1,0:T(8,128)S(1)} collective-permute-done((f32[1024,256]{1,0:T(8,128)S(1)}, f32[1024,256]{1,0:T(8,128)S(1)}, u32[]{:S(2)}, u32[]{:S(2)}) %collective-permute-start.3) | collective-permute-done | bytes 1048608 | tf_op jit(solution)/shard_map/ppermute | solution.py:322
  78.3 8.3 %third.2 = (f32[512,256]{1,0:T(8,128)S(1)}, f32[2,512,256]{2,1,0:T(8,128)S(1)}, f32[1024,256]{1,0:T(8,128)S(1)}) custom-call(f32[512,256]{1,0:T(8,128)S(1)} %get-tuple-element.40.d_in, f32[2,512,256]{2,1,0:T(8,128)S(1)} %get-tuple-element.41.c_in, f32[1024,256]{1,0:T(8,128)S(1)} %collective-permute-done.2.even, f32[1024,256]{1,0:T(8,128)S(1)} %collective-permute-done.3.odd, ...), custom_call_target="tpu_custom_call" | custom-call | tf_op jit(solution)/shard_map/third/pallas_call | solution.py:393
  86.6 2.1 %collective-permute-start.4 = (f32[1024,256]{1,0:T(8,128)S(1)}, f32[1024,256]{1,0:T(8,128)S(1)}, u32[]{:S(2)}, u32[]{:S(2)}) collective-permute-start(f32[1024,256]{1,0:T(8,128)S(1)} %get-tuple-element.46), channel_id=1, source_target_pairs={{8,16},{16,8},{12,20},{20,12},{24,32},{32,24},{28,36},{36,28},{40,... | collective-permute-start | bytes 3145736 | tf_op jit(solution)/shard_map/ppermute | solution.py:322
  88.7 0.8 collective-permute-done.8.odd
  89.5 8.2 %third.3 = (f32[512,256]{1,0:T(8,128)S(1)}, f32[2,512,256]{2,1,0:T(8,128)S(1)}, f32[1024,256]{1,0:T(8,128)S(1)}) custom-call(f32[512,256]{1,0:T(8,128)S(1)} %get-tuple-element.53.d_in, f32[2,512,256]{2,1,0:T(8,128)S(1)} %get-tuple-element.54.c_in, f32[1024,256]{1,0:T(8,128)S(1)} %collective-permute-done.7.even, f32[1024,256]{1,0:T(8,128)S(1)} %collective-permute-done.8.odd, ...), custom_call_target="tpu_custom_call" | custom-call | tf_op jit(solution)/shard_map/third/pallas_call | solution.py:391
  97.8 5.2 %collective-permute-start.9 = (f32[1024,256]{1,0:T(8,128)S(1)}, f32[1024,256]{1,0:T(8,128)S(1)}, u32[]{:S(2)}, u32[]{:S(2)}) collective-permute-start(f32[1024,256]{1,0:T(8,128)S(1)} %get-tuple-element.58), channel_id=1, source_target_pairs={{8,16},{16,8},{12,20},{20,12},{24,32},{32,24},{28,36},{36,28},{40,... | collective-permute-start | bytes 3145736 | tf_op jit(solution)/shard_map/ppermute | solution.py:322
  103.0 0.1 collective-permute-start.10
  103.1 2.0 %collective-permute-start.5 = (f32[1024,256]{1,0:T(8,128)S(1)}, f32[1024,256]{1,0:T(8,128)S(1)}, u32[]{:S(2)}, u32[]{:S(2)}) collective-permute-start(f32[1024,256]{1,0:T(8,128)S(1)} %get-tuple-element.46), channel_id=1, source_target_pairs={{0,8},{8,0},{4,12},{12,4},{16,24},{24,16},{20,28},{28,20},{32,40},... | collective-permute-start | bytes 3145736 | tf_op jit(solution)/shard_map/ppermute | solution.py:323
  105.2 11.4 %collective-permute-done.4.odd = f32[1024,256]{1,0:T(8,128)S(1)} collective-permute-done((f32[1024,256]{1,0:T(8,128)S(1)}, f32[1024,256]{1,0:T(8,128)S(1)}, u32[]{:S(2)}, u32[]{:S(2)}) %collective-permute-start.4) | collective-permute-done | bytes 1048608 | tf_op jit(solution)/shard_map/ppermute | solution.py:322
  116.6 1.6 %last_odd.2 = (f32[512,256]{1,0:T(8,128)S(1)}, f32[512,256]{1,0:T(8,128)S(1)}) custom-call(f32[512,256]{1,0:T(8,128)S(1)} %get-tuple-element.44.d_in, f32[2,512,256]{2,1,0:T(8,128)S(1)} %get-tuple-element.45.c_in, f32[1024,256]{1,0:T(8,128)S(1)} %collective-permute-done.4.odd, s32[2]{0:T(128)S(1)} %pad_add_fusion.parity), custom_call_target="tpu_custom_call" | custom-call | tf_op jit(solution)/shard_map/last_odd/pallas_call | solution.py:418
  118.2 18.2 %collective-permute-done.9.odd = f32[1024,256]{1,0:T(8,128)S(1)} collective-permute-done((f32[1024,256]{1,0:T(8,128)S(1)}, f32[1024,256]{1,0:T(8,128)S(1)}, u32[]{:S(2)}, u32[]{:S(2)}) %collective-permute-start.9) | collective-permute-done | bytes 1048608 | tf_op jit(solution)/shard_map/ppermute | solution.py:322
  136.4 1.6 %last_odd.3 = (f32[512,256]{1,0:T(8,128)S(1)}, f32[512,256]{1,0:T(8,128)S(1)}) custom-call(f32[512,256]{1,0:T(8,128)S(1)} %get-tuple-element.56.d_in, f32[2,512,256]{2,1,0:T(8,128)S(1)} %get-tuple-element.57.c_in, f32[1024,256]{1,0:T(8,128)S(1)} %collective-permute-done.9.odd, s32[2]{0:T(128)S(1)} %pad_add_fusion.parity), custom_call_target="tpu_custom_call" | custom-call | tf_op jit(solution)/shard_map/last_odd/pallas_call | solution.py:407
  137.9 0.0 collective-permute-done.10.even
  137.9 2.4 %last_even.1 = (f32[2,512,256]{2,1,0:T(8,128)}, f32[2,512,256]{2,1,0:T(8,128)}, f32[2,512,256]{2,1,0:T(8,128)}) custom-call(f32[512,256]{1,0:T(8,128)S(1)} %get-tuple-element.59.d_mid, f32[512,256]{1,0:T(8,128)S(1)} %get-tuple-element.60.c_mid, f32[2,512,256]{2,1,0:T(8,128)S(1)} %get-tuple-element.57.c_in, f32[1024,256]{1,0:T(8,128)S(1)} %collective-permute-done.10.even, ...), custom_call_target="tpu_custom_call" | custom-call | tf_op jit(solution)/shard_map/last_even/pallas_call | solution.py:417
  140.3 9.8 %collective-permute-done.5.even = f32[1024,256]{1,0:T(8,128)S(1)} collective-permute-done((f32[1024,256]{1,0:T(8,128)S(1)}, f32[1024,256]{1,0:T(8,128)S(1)}, u32[]{:S(2)}, u32[]{:S(2)}) %collective-permute-start.5) | collective-permute-done | bytes 1048608 | tf_op jit(solution)/shard_map/ppermute | solution.py:323
  150.2 2.4 %last_even_beside.1 = (f32[2,512,256]{2,1,0:T(8,128)}, f32[2,512,256]{2,1,0:T(8,128)}, f32[2,512,256]{2,1,0:T(8,128)}) custom-call(f32[512,256]{1,0:T(8,128)S(1)} %get-tuple-element.47.d_mid, f32[512,256]{1,0:T(8,128)S(1)} %get-tuple-element.48.c_mid, ...), custom_call_target="tpu_custom_call", output_to_operand_aliasing={{0}: (5, {}), {1}: (6, {}), {2}: (7, {})} | custom-call | tf_op jit(solution)/shard_map/last_even_beside/pallas_call | solution.py:419
  (8 shorter events, 0.1 us)
Async XLA Ops:
  0.6 19.3 %collective-permute-start = (f32[2,512,256]{2,1,0:T(8,128)}, f32[2,512,256]{2,1,0:T(8,128)S(1)}, u32[]{:S(2)}, u32[]{:S(2)}) collective-permute-start(f32[2,512,256]{2,1,0:T(8,128)} %bitcast.9), channel_id=1, source_target_pairs={{0,4},{4,8},{8,12},{12,16},{16,20},{20,24},{24,28},{28,32},{32,36}... | collective-permute-start | bytes 3145736 | tf_op jit(solution)/shard_map/ppermute | solution.py:313
  4.0 1.2 copy-start.1
  5.2 14.7 %copy-start = (f32[2,2,256,256]{3,2,1,0:T(8,128)S(1)}, f32[2,2,256,256]{3,2,1,0:T(8,128)}, u32[]{:S(2)}) copy-start(f32[2,2,256,256]{3,2,1,0:T(8,128)} %param.5) | copy-start | bytes 3145732
  12.2 18.1 %collective-permute-start.1 = (f32[1024,256]{1,0:T(8,128)S(1)}, f32[1024,256]{1,0:T(8,128)S(1)}, u32[]{:S(2)}, u32[]{:S(2)}) collective-permute-start(f32[1024,256]{1,0:T(8,128)S(1)} %get-tuple-element.37.z_hop_a), channel_id=1, source_target_pairs={{4,0},{8,4},{12,8},{16,12},{20,16},{24,20},{28,24},{32,28},{36,32}... | collective-permute-start | bytes 3145736 | tf_op jit(solution)/shard_map/ppermute | solution.py:313
  18.0 44.3 %collective-permute-start.6 = (f32[512,256]{1,0:T(8,128)S(1)}, f32[512,256]{1,0:T(8,128)S(1)}, u32[]{:S(2)}, u32[]{:S(2)}) collective-permute-start(f32[512,256]{1,0:T(8,128)S(1)} %get-tuple-element.36.z_b), channel_id=1, source_target_pairs={{0,4},{4,8},{8,12},{12,16},{16,20},{20,24},{24,28},{28,32},{32,36}... | collective-permute-start | bytes 1572872 | tf_op jit(solution)/shard_map/ppermute | solution.py:313
  60.1 18.2 %collective-permute-start.3 = (f32[1024,256]{1,0:T(8,128)S(1)}, f32[1024,256]{1,0:T(8,128)S(1)}, u32[]{:S(2)}, u32[]{:S(2)}) collective-permute-start(f32[1024,256]{1,0:T(8,128)S(1)} %get-tuple-element.42), channel_id=1, source_target_pairs={{4,8},{8,4},{12,16},{16,12},{20,24},{24,20},{28,32},{32,28},{36,40... | collective-permute-start | bytes 3145736 | tf_op jit(solution)/shard_map/ppermute | solution.py:322
  62.0 16.3 %collective-permute-start.2 = (f32[1024,256]{1,0:T(8,128)S(1)}, f32[1024,256]{1,0:T(8,128)S(1)}, u32[]{:S(2)}, u32[]{:S(2)}) collective-permute-start(f32[1024,256]{1,0:T(8,128)S(1)} %get-tuple-element.42), channel_id=1, source_target_pairs={{0,4},{4,0},{8,12},{12,8},{16,20},{20,16},{24,28},{28,24},{32,36},... | collective-permute-start | bytes 3145736 | tf_op jit(solution)/shard_map/ppermute | solution.py:323
  70.2 19.3 %collective-permute-start.8 = (f32[1024,256]{1,0:T(8,128)S(1)}, f32[1024,256]{1,0:T(8,128)S(1)}, u32[]{:S(2)}, u32[]{:S(2)}) collective-permute-start(f32[1024,256]{1,0:T(8,128)S(1)} %get-tuple-element.55), channel_id=1, source_target_pairs={{4,8},{8,4},{12,16},{16,12},{20,24},{24,20},{28,32},{32,28},{36,40... | collective-permute-start | bytes 3145736 | tf_op jit(solution)/shard_map/ppermute | solution.py:322
  75.9 13.6 %collective-permute-start.7 = (f32[1024,256]{1,0:T(8,128)S(1)}, f32[1024,256]{1,0:T(8,128)S(1)}, u32[]{:S(2)}, u32[]{:S(2)}) collective-permute-start(f32[1024,256]{1,0:T(8,128)S(1)} %get-tuple-element.55), channel_id=1, source_target_pairs={{0,4},{4,0},{8,12},{12,8},{16,20},{20,16},{24,28},{28,24},{32,36},... | collective-permute-start | bytes 3145736 | tf_op jit(solution)/shard_map/ppermute | solution.py:323
  86.6 30.0 %collective-permute-start.4 = (f32[1024,256]{1,0:T(8,128)S(1)}, f32[1024,256]{1,0:T(8,128)S(1)}, u32[]{:S(2)}, u32[]{:S(2)}) collective-permute-start(f32[1024,256]{1,0:T(8,128)S(1)} %get-tuple-element.46), channel_id=1, source_target_pairs={{8,16},{16,8},{12,20},{20,12},{24,32},{32,24},{28,36},{36,28},{40,... | collective-permute-start | bytes 3145736 | tf_op jit(solution)/shard_map/ppermute | solution.py:322
  97.8 38.6 %collective-permute-start.9 = (f32[1024,256]{1,0:T(8,128)S(1)}, f32[1024,256]{1,0:T(8,128)S(1)}, u32[]{:S(2)}, u32[]{:S(2)}) collective-permute-start(f32[1024,256]{1,0:T(8,128)S(1)} %get-tuple-element.58), channel_id=1, source_target_pairs={{8,16},{16,8},{12,20},{20,12},{24,32},{32,24},{28,36},{36,28},{40,... | collective-permute-start | bytes 3145736 | tf_op jit(solution)/shard_map/ppermute | solution.py:322
  103.0 34.9 %collective-permute-start.10 = (f32[1024,256]{1,0:T(8,128)S(1)}, f32[1024,256]{1,0:T(8,128)S(1)}, u32[]{:S(2)}, u32[]{:S(2)}) collective-permute-start(f32[1024,256]{1,0:T(8,128)S(1)} %get-tuple-element.58), channel_id=1, source_target_pairs={{0,8},{8,0},{4,12},{12,4},{16,24},{24,16},{20,28},{28,20},{32,40},... | collective-permute-start | bytes 3145736 | tf_op jit(solution)/shard_map/ppermute | solution.py:323
  103.1 47.0 %collective-permute-start.5 = (f32[1024,256]{1,0:T(8,128)S(1)}, f32[1024,256]{1,0:T(8,128)S(1)}, u32[]{:S(2)}, u32[]{:S(2)}) collective-permute-start(f32[1024,256]{1,0:T(8,128)S(1)} %get-tuple-element.46), channel_id=1, source_target_pairs={{0,8},{8,0},{4,12},{12,4},{16,24},{24,16},{20,28},{28,20},{32,40},... | collective-permute-start | bytes 3145736 | tf_op jit(solution)/shard_map/ppermute | solution.py:323

commit v3 on v2

--- a/solution.py
+++ b/solution.py
@@ -56,7 +56,11 @@
 
 
 def product(a, b):
-    a_high, a_low = split(a)
+    return times(split(a), b)
+
+
+def times(a, b):
+    a_high, a_low = a
     b_high, b_low = split(b)
     e_high, e_low = emb(b_high), emb(b_low)
     return dot(a_high, e_high) + dot(a_high, e_low) + dot(a_low, e_high)
@@ -77,7 +81,7 @@
         ex[i, :w] = x
         ex[i, w:] = turned(x)
 
-    norms = []
+    norms, grams = [], []
     for i, a in enumerate(blocks):
         high, low = split(a)
         ea[i] = emb(high)
@@ -88,13 +92,17 @@
         norm = 1.02 * jnp.max(jnp.sum(size, axis=1))
         place(i, (ah.astype(F32) * (1.0 / norm)).astype(BF))
         norms.append(norm)
+        grams.append(gram)
     largest = functools.reduce(jnp.maximum, norms)
     bound = jnp.maximum(0.9 * eta * eta / largest, 1e-10)
 
-    def step(bound, piece=None):
+    def step(bound, piece=None, known=None):
         mu = 2.0 / (bound + 1.03)
         for i in range(len(blocks)):
-            errors = [(one[h] - mu * dot(ex[i, h], ea[i])).astype(BF) for h in halves]
+            if known is None:
+                errors = [(one[h] - mu * dot(ex[i, h], ea[i])).astype(BF) for h in halves]
+            else:
+                errors = [(one[h] - (mu / norms[i]) * known[i][h]).astype(BF) for h in halves]
             if piece is not None:
                 piece()
             news = [
@@ -105,7 +113,8 @@
         gap = 1.0 - mu * bound
         return 1.0 - gap * gap
 
-    for piece in side:
+    bound = step(bound, side[0] if side else None, grams)
+    for piece in side[1:]:
         bound = step(bound, piece)
     lax.while_loop(lambda bound: bound < CONVERGED, step, bound)
     for i, a in enumerate(blocks):
@@ -121,7 +130,7 @@
 
 def polish(a, norm, left, z, i, full, spread, rest):
     w = a.shape[0]
-    high, wide = min(64, w), min(128, w)
+    high, wide = min(32, w), min(128, w)
     across = 2 * w // wide
     full[...] = emb(a)
 
@@ -200,9 +209,9 @@
 
 def solve(d, couplings, side, eta, payload, work):
     invert([d], eta, work, side)
-    z = work[0][0]
+    z = split(work[0][0])
     for k in range(2):
-        put(payload, product(z, row(couplings[1 - k])), k * d.shape[1])
+        put(payload, times(z, row(couplings[1 - k])), k * d.shape[1])
 
 
 def part(payload, k):
@@ -224,7 +233,9 @@
     beside.wait()
 
 
-def near_kernel(onsite, hop, hop_left, z_b, z_hop_a, scalars, d_a, d_b, u_a, l_b, g_a, k_a):
+def near_kernel(
+    onsite, hop, hop_left, z_b, z_hop_a, scalars, d_a, d_b, u_a, l_b, g_a, k_a, *outputs
+):
     h = row(hop[0])
     before = row(hop_left[1])
     put(g_a, adjoint(before))
@@ -258,35 +269,25 @@
     solve(row(d_out[...]), c_out, side, scalars[1], payload, work)
 
 
-def last_odd(d_in, c_in, odd, parity, d_mid, c_mid):
-    _, j = sides(parity[1])
-    two = row(c_in[j])
-    put(d_mid, row(d_in[...]) - product(two, part(odd, j)))
-    put(c_mid, -product(two, part(odd, 1 - j)))
-
-
-def last_even(slab, d_mid, c_mid, c_in, even, parity, d_out, u_out, l_out, hold, sems):
-    i, _ = sides(parity[1])
-    one = row(c_in[i])
-    mine, other = -product(one, part(even, 1 - i)), row(c_mid[...])
-    copies = [
-        pltpu.make_async_copy(hold.at[k], out.at[slab], sems.at[k])
-        for k, out in enumerate((u_out, l_out, d_out))
-    ]
-    put(hold.at[0], jnp.where(i == 1, mine, other))
-    put(hold.at[1], jnp.where(i == 1, other, mine))
+def last_kernel(k, d_in, c_in, even, odd, ints, c_old, *refs):
+    d_out, c_out = refs[-4:-2]
+    hold, sems = refs[-2:]
+    slab = ints[2]
+    is_even = sides(ints[1])[0] == k
+    to_d = row(jnp.where(is_even, even[...], odd[...]))
+    to_c = row(jnp.where(is_even, odd[...], even[...]))
+    put(hold.at[0], -product(row(c_in[1 - k]), to_c))
+    copies = [pltpu.make_async_copy(hold.at[0], c_out.at[slab], sems.at[0])]
     copies[0].start()
-    copies[1].start()
-    put(hold.at[2], row(d_mid[...]) - product(one, part(even, i)))
-    copies[2].start()
+    d = row(d_in[...]) - product(row(c_in[k]), to_d)
+    if k == 0:
+        put(d_out, d)
+    else:
+        put(hold.at[1], d)
+        copies.append(pltpu.make_async_copy(hold.at[1], d_out.at[slab], sems.at[1]))
+        copies[1].start()
     for copy in copies:
         copy.wait()
-
-
-def last_even_beside(
-    d_mid, c_mid, c_in, even, parity, d_old, u_old, l_old, d_out, u_out, l_out, hold, sems
-):
-    last_even(1, d_mid, c_mid, c_in, even, parity, d_out, u_out, l_out, hold, sems)
 
 
 def shape(*dims):
@@ -332,8 +333,9 @@
     keep = jnp.where(last, 0.0, 1.0).astype(F32)
     scalars = jnp.stack([energy_level[0], broadening[0], keep])
     position = lax.axis_index("slab")
-    parity = jnp.stack([position & 1, (position >> 1) & 1])
-    scalars, parity = lax.optimization_barrier((scalars, parity))
+    near, far = position & 1, (position >> 1) & 1
+    at_a, at_b = (jnp.stack([near, far, jnp.int32(k)]) for k in range(2))
+    scalars, at_a, at_b = lax.optimization_barrier((scalars, at_a, at_b))
 
     hop_left = send(hop, 1)
     block, pair, two = shape(2 * w, w), shape(4 * w, w), shape(2, 2 * w, w)
@@ -348,11 +350,13 @@
     )(onsite, pltpu.with_memory_space_constraint(hop, pltpu.HBM), scalars)
     z_left = send(up, 1)
     z_hop_right = send(down, -1)
-    d_a, d_b, u_a, l_b, g_a, k_a = pl.pallas_call(
+    whole = shape(rows, 2 * w, w)
+    kept = pl.BlockSpec(memory_space=pl.ANY)
+    d_a, d_b, u_a, l_b, g_a, k_a, d_out, u_out, l_out = pl.pallas_call(
         near_kernel,
-        out_shape=(block,) * 6,
+        out_shape=(block,) * 6 + (whole,) * 3,
         in_specs=[VMEM] * 5 + [SMEM],
-        out_specs=(VMEM,) * 6,
+        out_specs=(VMEM,) * 6 + (kept,) * 3,
         compiler_params=PARAMS,
         name="near",
     )(onsite, hop, hop_left, up, down, scalars)
@@ -388,45 +392,40 @@
         compiler_params=PARAMS,
         name="third",
     )
-    d_a, c_a, p_a = third(d_a, c_a, even_a, odd_a, scalars, parity)
+    d_a, c_a, p_a = third(d_a, c_a, even_a, odd_a, scalars, at_a)
     even_a, odd_a = swaps(p_a, 2)
-    d_b, c_b, p_b = third(d_b, c_b, even_b, odd_b, scalars, parity)
-    even_b, odd_b = swaps(p_b, 2)
-
-    whole = shape(rows, 2 * w, w)
-    kept = pl.BlockSpec(memory_space=pl.ANY)
-    hold = [pltpu.VMEM((3, 2 * w, w), F32), pltpu.SemaphoreType.DMA((3,))]
-    half = pl.pallas_call(
-        last_odd,
-        out_shape=(block, block),
-        in_specs=[VMEM] * 3 + [SMEM],
-        out_specs=(VMEM,) * 2,
-        compiler_params=PARAMS,
-        name="last_odd",
-    )
-    d_a, o_a = half(d_a, c_a, odd_a, parity)
-    first_half = pl.pallas_call(
-        functools.partial(last_even, 0),
-        out_shape=(whole,) * 3,
-        in_specs=[VMEM] * 4 + [SMEM],
-        out_specs=(kept,) * 3,
+    d_b, c_b, p_b = third(d_b, c_b, even_b, odd_b, scalars, at_a)
+    first_b = swaps(p_b[: 2 * w], 2)
+    second_b = swaps(p_b[2 * w :], 2)
+
+    hold = [pltpu.VMEM((2, 2 * w, w), F32), pltpu.SemaphoreType.DMA((2,))]
+    take_upper = pl.pallas_call(
+        functools.partial(last_kernel, 0),
+        out_shape=(block, whole),
+        in_specs=[VMEM] * 4 + [SMEM, kept],
+        out_specs=(VMEM, kept),
+        input_output_aliases={5: 1},
         scratch_shapes=hold,
         compiler_params=PARAMS,
-        name="last_even",
-    )
-    out = first_half(d_a, o_a, c_a, even_a, parity)
-    d_b, o_b = half(d_b, c_b, odd_b, parity)
-    out = pl.pallas_call(
-        last_even_beside,
-        out_shape=(whole,) * 3,
-        in_specs=[VMEM] * 4 + [SMEM] + [kept] * 3,
-        out_specs=(kept,) * 3,
-        input_output_aliases={5: 0, 6: 1, 7: 2},
+        name="take_upper",
+    )
+    take_lower = pl.pallas_call(
+        functools.partial(last_kernel, 1),
+        out_shape=(whole, whole),
+        in_specs=[VMEM] * 4 + [SMEM, kept, kept],
+        out_specs=(kept, kept),
+        input_output_aliases={5: 1, 6: 0},
         scratch_shapes=hold,
         compiler_params=PARAMS,
-        name="last_even_beside",
-    )(d_b, o_b, c_b, even_b, parity, *out)
-    return tuple(x.reshape(rows, 2, w, w) for x in out)
+        name="take_lower",
+    )
+    d_a, u_out = take_upper(d_a, c_a, even_a[: 2 * w], odd_a[: 2 * w], at_a, u_out)
+    d_out, l_out = take_lower(
+        d_a, c_a, even_a[2 * w :], odd_a[2 * w :], at_a, l_out, d_out
+    )
+    d_b, u_out = take_upper(d_b, c_b, *first_b, at_b, u_out)
+    d_out, l_out = take_lower(d_b, c_b, *second_b, at_b, l_out, d_out)
+    return tuple(x.reshape(rows, 2, w, w) for x in (d_out, u_out, l_out))
 
 
 def solution(mesh):

time: 153 us -> 154 us (level)
  the two profiles are of different devices: /device:TPU:88 before, /device:TPU:89 now
where the time goes in v3:
time: 154 us
  Pallas kernels  70.2 us (46%)
  starting transfers between devices  51.5 us (33%)
  waiting for transfers between devices  27.9 us (18%)
  between operations  2.36 us (2%)
  local copies, waits for them, and re-layouts  1.55 us (1%)
    pallas_call x1, Pallas kernels, reduce_levels(): second(d_b, l_b, hop[1], z_hop_right[:2 * w], z_hop_right[2 * w:], scalar...  27.6 us
    ppermute x5, starting transfers between devices, swaps(): from_even = lax.ppermute(x, 'slab', even)  27.4 us
    ppermute x5, waiting for transfers between devices, swaps(): from_odd = lax.ppermute(x, 'slab', odd)  15.3 us
    ppermute x5, starting transfers between devices, swaps(): from_odd = lax.ppermute(x, 'slab', odd)  14.8 us
    ppermute x5, waiting for transfers between devices, swaps(): from_even = lax.ppermute(x, 'slab', even)  9.93 us
    ppermute x3, starting transfers between devices, send(): lax.ppermute(x, 'slab', [(i, i + by) for i in range(size) if 0 <= i + by...  9.24 us
    pallas_call x1, Pallas kernels, reduce_levels(): d_a, c_a, p_a = third(d_a, c_a, even_a, odd_a, scalars, at_a)  7.97 us
    pallas_call x1, Pallas kernels, reduce_levels(): d_b, c_b, p_b = third(d_b, c_b, even_b, odd_b, scalars, at_a)  7.94 us
  transfers between devices with their start and end apart: 13, of which 7 were waited for; matrix products, arithmetic and copies ran while one was open for 0% of the time, Pallas kernels for 44%

profile of v3, /device:TPU:89, one launch (start us, length us, event | category | flops | bytes accessed | tf_op | source)
XLA Modules:
  0.0 153.6 jit_solution(9916289941224753791)
XLA Ops:
  0.6 3.7 %collective-permute-start = (f32[2,512,256]{2,1,0:T(8,128)}, f32[2,512,256]{2,1,0:T(8,128)S(1)}, u32[]{:S(2)}, u32[]{:S(2)}) collective-permute-start(f32[2,512,256]{2,1,0:T(8,128)} %bitcast.9), channel_id=1, source_target_pairs={{0,4},{4,8},{8,12},{12,16},{16,20},{20,24},{24,28},{28,32},{32,36}... | collective-permute-start | bytes 3145736 | tf_op jit(solution)/shard_map/ppermute | solution.py:314
  5.6 0.1 pad_maximum_fusion.scalars
  5.8 1.2 copy-done.1
  7.0 6.8 %first.1 = (f32[512,256]{1,0:T(8,128)S(1)}, f32[1024,256]{1,0:T(8,128)S(1)}) custom-call(f32[2,512,256]{2,1,0:T(8,128)S(1)} %bitcast.12, f32[2,512,256]{2,1,0:T(8,128)} %bitcast.10, f32[3]{0:T(128)S(1)} %pad_maximum_fusion.scalars), custom_call_target="tpu_custom_call" | custom-call | tf_op jit(solution)/shard_map/first/pallas_call | solution.py:342
  13.8 1.9 %collective-permute-start.1 = (f32[1024,256]{1,0:T(8,128)S(1)}, f32[1024,256]{1,0:T(8,128)S(1)}, u32[]{:S(2)}, u32[]{:S(2)}) collective-permute-start(f32[1024,256]{1,0:T(8,128)S(1)} %get-tuple-element.39.z_hop_a), channel_id=1, source_target_pairs={{4,0},{8,4},{12,8},{16,12},{20,16},{24,20},{28,24},{32,28},{36,32}... | collective-permute-start | bytes 3145736 | tf_op jit(solution)/shard_map/ppermute | solution.py:314
  15.7 3.6 %collective-permute-start.6 = (f32[512,256]{1,0:T(8,128)S(1)}, f32[512,256]{1,0:T(8,128)S(1)}, u32[]{:S(2)}, u32[]{:S(2)}) collective-permute-start(f32[512,256]{1,0:T(8,128)S(1)} %get-tuple-element.38.z_b), channel_id=1, source_target_pairs={{0,4},{4,8},{8,12},{12,16},{16,20},{20,24},{24,28},{28,32},{32,36}... | collective-permute-start | bytes 1572872 | tf_op jit(solution)/shard_map/ppermute | solution.py:314
  19.4 3.3 %near.1 = (f32[512,256]{1,0:T(8,128)S(1)}, f32[512,256]{1,0:T(8,128)S(1)}, f32[512,256]{1,0:T(8,128)S(1)}, f32[512,256]{1,0:T(8,128)S(1)}, f32[512,256]{1,0:T(8,...) custom-call(f32[2,512,256]{2,1,0:T(8,128)S(1)} %bitcast.13, ...), custom_call_target="tpu_custom_call" | custom-call | tf_op jit(solution)/shard_map/near/pallas_call | solution.py:355
  22.7 2.7 %collective-permute-done.6.z = f32[512,256]{1,0:T(8,128)S(1)} collective-permute-done((f32[512,256]{1,0:T(8,128)S(1)}, f32[512,256]{1,0:T(8,128)S(1)}, u32[]{:S(2)}, u32[]{:S(2)}) %collective-permute-start.6) | collective-permute-done | bytes 524320 | tf_op jit(solution)/shard_map/ppermute | solution.py:314
  25.5 7.7 %second.3 = (f32[512,256]{1,0:T(8,128)S(1)}, f32[2,512,256]{2,1,0:T(8,128)S(1)}, f32[1024,256]{1,0:T(8,128)S(1)}) custom-call(f32[512,256]{1,0:T(8,128)S(1)} %get-tuple-element.50.d_in, f32[512,256]{1,0:T(8,128)S(1)} %get-tuple-element.51.c_in, f32[512,256]{1,0:T(8,128)S(1)} %get-tuple-element.52.g, f32[512,256]{1,0:T(8,128)S(1)} %collective-permute-done.6.z, ...), custom_call_target="tpu_custom_call" | custom-call | tf_op jit(solution)/shard_map/second/pallas_call | solution.py:373
  33.2 5.8 %collective-permute-start.7 = (f32[1024,256]{1,0:T(8,128)S(1)}, f32[1024,256]{1,0:T(8,128)S(1)}, u32[]{:S(2)}, u32[]{:S(2)}) collective-permute-start(f32[1024,256]{1,0:T(8,128)S(1)} %get-tuple-element.56), channel_id=1, source_target_pairs={{0,4},{4,0},{8,12},{12,8},{16,20},{20,16},{24,28},{28,24},{32,36},... | collective-permute-start | bytes 3145736 | tf_op jit(solution)/shard_map/ppermute | solution.py:324
  39.0 1.9 %collective-permute-start.8 = (f32[1024,256]{1,0:T(8,128)S(1)}, f32[1024,256]{1,0:T(8,128)S(1)}, u32[]{:S(2)}, u32[]{:S(2)}) collective-permute-start(f32[1024,256]{1,0:T(8,128)S(1)} %get-tuple-element.56), channel_id=1, source_target_pairs={{4,8},{8,4},{12,16},{16,12},{20,24},{24,20},{28,32},{32,28},{36,40... | collective-permute-start | bytes 3145736 | tf_op jit(solution)/shard_map/ppermute | solution.py:323
  41.0 27.6 %second.2 = (f32[512,256]{1,0:T(8,128)S(1)}, f32[2,512,256]{2,1,0:T(8,128)S(1)}, f32[1024,256]{1,0:T(8,128)S(1)}) custom-call(f32[512,256]{1,0:T(8,128)S(1)} %get-tuple-element.40.d_in, f32[512,256]{1,0:T(8,128)S(1)} %get-tuple-element.41.c_in, f32[512,256]{1,0:T(8,128)S(1)} %bitcast.14, f32[512,256]{1,0:T(8,128)S(1)} %get-tuple-element.78.z, ...), custom_call_target="tpu_custom_call" | custom-call | tf_op jit(solution)/shard_map/second/pallas_call | solution.py:375
  68.6 19.9 %collective-permute-start.2 = (f32[1024,256]{1,0:T(8,128)S(1)}, f32[1024,256]{1,0:T(8,128)S(1)}, u32[]{:S(2)}, u32[]{:S(2)}) collective-permute-start(f32[1024,256]{1,0:T(8,128)S(1)} %get-tuple-element.44), channel_id=1, source_target_pairs={{0,4},{4,0},{8,12},{12,8},{16,20},{20,16},{24,28},{28,24},{32,36},... | collective-permute-start | bytes 3145736 | tf_op jit(solution)/shard_map/ppermute | solution.py:324
  88.5 1.9 %collective-permute-start.3 = (f32[1024,256]{1,0:T(8,128)S(1)}, f32[1024,256]{1,0:T(8,128)S(1)}, u32[]{:S(2)}, u32[]{:S(2)}) collective-permute-start(f32[1024,256]{1,0:T(8,128)S(1)} %get-tuple-element.44), channel_id=1, source_target_pairs={{4,8},{8,4},{12,16},{16,12},{20,24},{24,20},{28,32},{32,28},{36,40... | collective-permute-start | bytes 3145736 | tf_op jit(solution)/shard_map/ppermute | solution.py:323
  90.5 8.0 %third.3 = (f32[512,256]{1,0:T(8,128)S(1)}, f32[2,512,256]{2,1,0:T(8,128)S(1)}, f32[1024,256]{1,0:T(8,128)S(1)}) custom-call(f32[512,256]{1,0:T(8,128)S(1)} %get-tuple-element.54.d_in, f32[2,512,256]{2,1,0:T(8,128)S(1)} %get-tuple-element.55.c_in, f32[1024,256]{1,0:T(8,128)S(1)} %collective-permute-done.7.even, f32[1024,256]{1,0:T(8,128)S(1)} %collective-permute-done.8.odd, ...), custom_call_target="tpu_custom_call" | custom-call | tf_op jit(solution)/shard_map/third/pallas_call | solution.py:395
  98.5 5.4 %collective-permute-start.10 = (f32[1024,256]{1,0:T(8,128)S(1)}, f32[1024,256]{1,0:T(8,128)S(1)}, u32[]{:S(2)}, u32[]{:S(2)}) collective-permute-start(f32[1024,256]{1,0:T(8,128)S(1)} %get-tuple-element.59), channel_id=1, source_target_pairs={{8,16},{16,8},{12,20},{20,12},{24,32},{32,24},{28,36},{36,28},{40,... | collective-permute-start | bytes 3145736 | tf_op jit(solution)/shard_map/ppermute | solution.py:323
  103.9 0.3 collective-permute-start.9
  104.2 0.8 collective-permute-done.3.odd
  105.0 7.9 %third.2 = (f32[512,256]{1,0:T(8,128)S(1)}, f32[2,512,256]{2,1,0:T(8,128)S(1)}, f32[1024,256]{1,0:T(8,128)S(1)}) custom-call(f32[512,256]{1,0:T(8,128)S(1)} %get-tuple-element.42.d_in, f32[2,512,256]{2,1,0:T(8,128)S(1)} %get-tuple-element.43.c_in, f32[1024,256]{1,0:T(8,128)S(1)} %collective-permute-done.2.even, f32[1024,256]{1,0:T(8,128)S(1)} %collective-permute-done.3.odd, ...), custom_call_target="tpu_custom_call" | custom-call | tf_op jit(solution)/shard_map/third/pallas_call | solution.py:397
  113.0 0.8 collective-permute-start.4
  113.8 2.2 %collective-permute-start.5 = (f32[512,256]{1,0:T(8,128)S(1)}, f32[512,256]{1,0:T(8,128)S(1)}, u32[]{:S(2)}, u32[]{:S(2)}) collective-permute-start(f32[512,256]{1,0:T(8,128)S(1)} %get-tuple-element.76), channel_id=1, source_target_pairs={{8,16},{16,8},{12,20},{20,12},{24,32},{32,24},{28,36},{36,28},{40,... | collective-permute-start | bytes 1572872 | tf_op jit(solution)/shard_map/ppermute | solution.py:323
  116.0 0.6 collective-permute-start.11
  116.5 13.1 %collective-permute-done.10 = f32[1024,256]{1,0:T(8,128)S(1)} collective-permute-done((f32[1024,256]{1,0:T(8,128)S(1)}, f32[1024,256]{1,0:T(8,128)S(1)}, u32[]{:S(2)}, u32[]{:S(2)}) %collective-permute-start.10) | collective-permute-done | bytes 1048608 | tf_op jit(solution)/shard_map/ppermute | solution.py:323
  129.6 3.4 %collective-permute-start.12 = (f32[512,256]{1,0:T(8,128)S(1)}, f32[512,256]{1,0:T(8,128)S(1)}, u32[]{:S(2)}, u32[]{:S(2)}) collective-permute-start(f32[512,256]{1,0:T(8,128)S(1)} %get-tuple-element.75), channel_id=1, source_target_pairs={{8,16},{16,8},{12,20},{20,12},{24,32},{32,24},{28,36},{36,28},{40,... | collective-permute-start | bytes 1572872 | tf_op jit(solution)/shard_map/ppermute | solution.py:323
  133.2 2.0 %take_upper.2 = (f32[512,256]{1,0:T(8,128)S(1)}, f32[2,512,256]{2,1,0:T(8,128)}) custom-call(f32[512,256]{1,0:T(8,128)S(1)} %get-tuple-element.57.d_in, f32[2,512,256]{2,1,0:T(8,128)S(1)} %get-tuple-element.58.c_in, f32[512,256]{1,0:T(8,128)S(1)} %get-tuple-element.74.even, f32[512,256]{1,0:T(8,128)S(1)} %get-tuple-element.72.odd, ...), custom_call_target="tpu_custom_call", output_to_operand_aliasing={{1}: (5, {})} | custom-call | tf_op jit(solution)/shard_map/take_upper/pallas_call | solution.py:422
  135.2 2.4 %take_lower.2 = (f32[2,512,256]{2,1,0:T(8,128)}, f32[2,512,256]{2,1,0:T(8,128)}) custom-call(f32[512,256]{1,0:T(8,128)S(1)} %get-tuple-element.63.d_in, f32[2,512,256]{2,1,0:T(8,128)S(1)} %get-tuple-element.58.c_in, f32[512,256]{1,0:T(8,128)S(1)} %get-tuple-element.73.even, ...), custom_call_target="tpu_custom_call", output_to_operand_aliasing={{1}: (5, {}), {0}: (6, {})} | custom-call | tf_op jit(solution)/shard_map/take_lower/pallas_call | solution.py:423
  137.7 2.9 %collective-permute-done.4.even = f32[512,256]{1,0:T(8,128)S(1)} collective-permute-done((f32[512,256]{1,0:T(8,128)S(1)}, f32[512,256]{1,0:T(8,128)S(1)}, u32[]{:S(2)}, u32[]{:S(2)}) %collective-permute-start.4) | collective-permute-done | bytes 524320 | tf_op jit(solution)/shard_map/ppermute | solution.py:324
  140.6 0.3 collective-permute-done.5.odd
  140.8 2.0 %take_upper.3 = (f32[512,256]{1,0:T(8,128)S(1)}, f32[2,512,256]{2,1,0:T(8,128)}) custom-call(f32[512,256]{1,0:T(8,128)S(1)} %get-tuple-element.46.d_in, f32[2,512,256]{2,1,0:T(8,128)S(1)} %get-tuple-element.47.c_in, f32[512,256]{1,0:T(8,128)S(1)} %collective-permute-done.4.even, ...), custom_call_target="tpu_custom_call", output_to_operand_aliasing={{1}: (5, {})} | custom-call | tf_op jit(solution)/shard_map/take_upper/pallas_call | solution.py:426
  142.8 7.0 %collective-permute-done.11.even = f32[512,256]{1,0:T(8,128)S(1)} collective-permute-done((f32[512,256]{1,0:T(8,128)S(1)}, f32[512,256]{1,0:T(8,128)S(1)}, u32[]{:S(2)}, u32[]{:S(2)}) %collective-permute-start.11) | collective-permute-done | bytes 524320 | tf_op jit(solution)/shard_map/ppermute | solution.py:324
  149.9 1.1 collective-permute-done.12.odd
  151.0 2.4 %take_lower.3 = (f32[2,512,256]{2,1,0:T(8,128)}, f32[2,512,256]{2,1,0:T(8,128)}) custom-call(f32[512,256]{1,0:T(8,128)S(1)} %get-tuple-element.62.d_in, f32[2,512,256]{2,1,0:T(8,128)S(1)} %get-tuple-element.47.c_in, f32[512,256]{1,0:T(8,128)S(1)} %collective-permute-done.11.even, ...), custom_call_target="tpu_custom_call", output_to_operand_aliasing={{1}: (5, {}), {0}: (6, {})} | custom-call | tf_op jit(solution)/shard_map/take_lower/pallas_call | solution.py:427
  (15 shorter events, 0.4 us)
Async XLA Ops:
  0.6 18.7 %collective-permute-start = (f32[2,512,256]{2,1,0:T(8,128)}, f32[2,512,256]{2,1,0:T(8,128)S(1)}, u32[]{:S(2)}, u32[]{:S(2)}) collective-permute-start(f32[2,512,256]{2,1,0:T(8,128)} %bitcast.9), channel_id=1, source_target_pairs={{0,4},{4,8},{8,12},{12,16},{16,20},{20,24},{24,28},{28,32},{32,36}... | collective-permute-start | bytes 3145736 | tf_op jit(solution)/shard_map/ppermute | solution.py:314
  5.8 1.2 copy-start.1
  7.0 12.4 %copy-start = (f32[2,2,256,256]{3,2,1,0:T(8,128)S(1)}, f32[2,2,256,256]{3,2,1,0:T(8,128)}, u32[]{:S(2)}) copy-start(f32[2,2,256,256]{3,2,1,0:T(8,128)} %param.5) | copy-start | bytes 3145732
  13.8 27.2 %collective-permute-start.1 = (f32[1024,256]{1,0:T(8,128)S(1)}, f32[1024,256]{1,0:T(8,128)S(1)}, u32[]{:S(2)}, u32[]{:S(2)}) collective-permute-start(f32[1024,256]{1,0:T(8,128)S(1)} %get-tuple-element.39.z_hop_a), channel_id=1, source_target_pairs={{4,0},{8,4},{12,8},{16,12},{20,16},{24,20},{28,24},{32,28},{36,32}... | collective-permute-start | bytes 3145736 | tf_op jit(solution)/shard_map/ppermute | solution.py:314
  15.7 9.8 %collective-permute-start.6 = (f32[512,256]{1,0:T(8,128)S(1)}, f32[512,256]{1,0:T(8,128)S(1)}, u32[]{:S(2)}, u32[]{:S(2)}) collective-permute-start(f32[512,256]{1,0:T(8,128)S(1)} %get-tuple-element.38.z_b), channel_id=1, source_target_pairs={{0,4},{4,8},{8,12},{12,16},{16,20},{20,24},{24,28},{28,32},{32,36}... | collective-permute-start | bytes 1572872 | tf_op jit(solution)/shard_map/ppermute | solution.py:314
  33.2 57.3 %collective-permute-start.7 = (f32[1024,256]{1,0:T(8,128)S(1)}, f32[1024,256]{1,0:T(8,128)S(1)}, u32[]{:S(2)}, u32[]{:S(2)}) collective-permute-start(f32[1024,256]{1,0:T(8,128)S(1)} %get-tuple-element.56), channel_id=1, source_target_pairs={{0,4},{4,0},{8,12},{12,8},{16,20},{20,16},{24,28},{28,24},{32,36},... | collective-permute-start | bytes 3145736 | tf_op jit(solution)/shard_map/ppermute | solution.py:324
  39.0 51.5 %collective-permute-start.8 = (f32[1024,256]{1,0:T(8,128)S(1)}, f32[1024,256]{1,0:T(8,128)S(1)}, u32[]{:S(2)}, u32[]{:S(2)}) collective-permute-start(f32[1024,256]{1,0:T(8,128)S(1)} %get-tuple-element.56), channel_id=1, source_target_pairs={{4,8},{8,4},{12,16},{16,12},{20,24},{24,20},{28,32},{32,28},{36,40... | collective-permute-start | bytes 3145736 | tf_op jit(solution)/shard_map/ppermute | solution.py:323
  68.6 35.6 %collective-permute-start.2 = (f32[1024,256]{1,0:T(8,128)S(1)}, f32[1024,256]{1,0:T(8,128)S(1)}, u32[]{:S(2)}, u32[]{:S(2)}) collective-permute-start(f32[1024,256]{1,0:T(8,128)S(1)} %get-tuple-element.44), channel_id=1, source_target_pairs={{0,4},{4,0},{8,12},{12,8},{16,20},{20,16},{24,28},{28,24},{32,36},... | collective-permute-start | bytes 3145736 | tf_op jit(solution)/shard_map/ppermute | solution.py:324
  88.5 16.4 %collective-permute-start.3 = (f32[1024,256]{1,0:T(8,128)S(1)}, f32[1024,256]{1,0:T(8,128)S(1)}, u32[]{:S(2)}, u32[]{:S(2)}) collective-permute-start(f32[1024,256]{1,0:T(8,128)S(1)} %get-tuple-element.44), channel_id=1, source_target_pairs={{4,8},{8,4},{12,16},{16,12},{20,24},{24,20},{28,32},{32,28},{36,40... | collective-permute-start | bytes 3145736 | tf_op jit(solution)/shard_map/ppermute | solution.py:323
  98.5 31.1 %collective-permute-start.10 = (f32[1024,256]{1,0:T(8,128)S(1)}, f32[1024,256]{1,0:T(8,128)S(1)}, u32[]{:S(2)}, u32[]{:S(2)}) collective-permute-start(f32[1024,256]{1,0:T(8,128)S(1)} %get-tuple-element.59), channel_id=1, source_target_pairs={{8,16},{16,8},{12,20},{20,12},{24,32},{32,24},{28,36},{36,28},{40,... | collective-permute-start | bytes 3145736 | tf_op jit(solution)/shard_map/ppermute | solution.py:323
  103.9 29.2 %collective-permute-start.9 = (f32[1024,256]{1,0:T(8,128)S(1)}, f32[1024,256]{1,0:T(8,128)S(1)}, u32[]{:S(2)}, u32[]{:S(2)}) collective-permute-start(f32[1024,256]{1,0:T(8,128)S(1)} %get-tuple-element.59), channel_id=1, source_target_pairs={{0,8},{8,0},{4,12},{12,4},{16,24},{24,16},{20,28},{28,20},{32,40},... | collective-permute-start | bytes 3145736 | tf_op jit(solution)/shard_map/ppermute | solution.py:324
  113.0 27.6 %collective-permute-start.4 = (f32[512,256]{1,0:T(8,128)S(1)}, f32[512,256]{1,0:T(8,128)S(1)}, u32[]{:S(2)}, u32[]{:S(2)}) collective-permute-start(f32[512,256]{1,0:T(8,128)S(1)} %get-tuple-element.76), channel_id=1, source_target_pairs={{0,8},{8,0},{4,12},{12,4},{16,24},{24,16},{20,28},{28,20},{32,40},... | collective-permute-start | bytes 1572872 | tf_op jit(solution)/shard_map/ppermute | solution.py:324
  113.8 27.1 %collective-permute-start.5 = (f32[512,256]{1,0:T(8,128)S(1)}, f32[512,256]{1,0:T(8,128)S(1)}, u32[]{:S(2)}, u32[]{:S(2)}) collective-permute-start(f32[512,256]{1,0:T(8,128)S(1)} %get-tuple-element.76), channel_id=1, source_target_pairs={{8,16},{16,8},{12,20},{20,12},{24,32},{32,24},{28,36},{36,28},{40,... | collective-permute-start | bytes 1572872 | tf_op jit(solution)/shard_map/ppermute | solution.py:323
  116.0 33.9 %collective-permute-start.11 = (f32[512,256]{1,0:T(8,128)S(1)}, f32[512,256]{1,0:T(8,128)S(1)}, u32[]{:S(2)}, u32[]{:S(2)}) collective-permute-start(f32[512,256]{1,0:T(8,128)S(1)} %get-tuple-element.75), channel_id=1, source_target_pairs={{0,8},{8,0},{4,12},{12,4},{16,24},{24,16},{20,28},{28,20},{32,40},... | collective-permute-start | bytes 1572872 | tf_op jit(solution)/shard_map/ppermute | solution.py:324
  129.6 21.4 %collective-permute-start.12 = (f32[512,256]{1,0:T(8,128)S(1)}, f32[512,256]{1,0:T(8,128)S(1)}, u32[]{:S(2)}, u32[]{:S(2)}) collective-permute-start(f32[512,256]{1,0:T(8,128)S(1)} %get-tuple-element.75), channel_id=1, source_target_pairs={{8,16},{16,8},{12,20},{20,12},{24,32},{32,24},{28,36},{36,28},{40,... | collective-permute-start | bytes 1572872 | tf_op jit(solution)/shard_map/ppermute | solution.py:323

commit v4 on v3

--- a/solution.py
+++ b/solution.py
@@ -26,14 +26,14 @@
 
 
 def row(c):
-    w = c.shape[1]
-    return jnp.concatenate([c[:w], c[w:]], axis=1)
+    h = c.shape[0] // 2
+    return jnp.concatenate([c[:h], c[h:]], axis=1)
 
 
 def put(out, r, at=0):
-    w = r.shape[0]
-    out[at : at + w] = r[:, :w]
-    out[at + w : at + 2 * w] = r[:, w:]
+    h, w = r.shape[0], r.shape[1] // 2
+    out[at : at + h] = r[:, :w]
+    out[at + h : at + 2 * h] = r[:, w:]
 
 
 def turned(r):
@@ -60,8 +60,12 @@
 
 
 def times(a, b):
+    return multiply(a, split(b))
+
+
+def multiply(a, b):
     a_high, a_low = a
-    b_high, b_low = split(b)
+    b_high, b_low = b
     e_high, e_low = emb(b_high), emb(b_low)
     return dot(a_high, e_high) + dot(a_high, e_low) + dot(a_low, e_high)
 
@@ -234,25 +238,28 @@
 
 
 def near_kernel(
-    onsite, hop, hop_left, z_b, z_hop_a, scalars, d_a, d_b, u_a, l_b, g_a, k_a, *outputs
+    onsite, hop, hop_left, z_b, z_hop_a, scalars, d_a, d_b, u_a, l_b, g_a, g_b, k_a, *outputs
 ):
     h = row(hop[0])
-    before = row(hop_left[1])
-    put(g_a, adjoint(before))
+    h_adj = adjoint(h)
+    before, after = row(hop_left[1]), row(hop[1])
+    before_adj = adjoint(before)
+    for out, pair in ((g_a, (before_adj, before)), (g_b, (after, adjoint(after)))):
+        for k, value in enumerate(pair):
+            out[2 * k], out[2 * k + 1] = split(value)
     put(k_a, adjoint(row(hop_left[0])))
     t = product(h, row(z_b[...]))
-    put(d_a, initial(row(onsite[0]), scalars) - product(t, adjoint(h)))
-    put(u_a, product(t, row(hop[1])) * (-scalars[2]))
-    t = product(adjoint(h), part(z_hop_a, 0))
+    put(d_a, initial(row(onsite[0]), scalars) - product(t, h_adj))
+    put(u_a, product(t, after) * (-scalars[2]))
+    t = product(h_adj, part(z_hop_a, 0))
     put(d_b, initial(row(onsite[1]), scalars) - product(t, h))
-    put(l_b, -product(t, adjoint(before)))
+    put(l_b, -product(t, before_adj))
 
 
 def second_kernel(d_in, c_in, g, z, k, scalars, side, d_out, c_out, payload, *work):
     at = side[0]
-    gain = row(g[...])
-    t = product(gain, row(z[...]))
-    put(d_out, row(d_in[...]) - product(t, adjoint(gain)))
+    t = times((g[0], g[1]), row(z[...]))
+    put(d_out, row(d_in[...]) - multiply(split(t), (g[2], g[3])))
     c_out[1 - at] = c_in[...]
     pieces = deferred(c_out, at, t, row(k[...]), -1.0)
     solve(row(d_out[...]), c_out, pieces, scalars[1], payload, work)
@@ -269,22 +276,24 @@
     solve(row(d_out[...]), c_out, side, scalars[1], payload, work)
 
 
-def last_kernel(k, d_in, c_in, even, odd, ints, c_old, *refs):
+def last_kernel(k, start, d_in, c_in, even, odd, ints, c_old, *refs):
     d_out, c_out = refs[-4:-2]
     hold, sems = refs[-2:]
     slab = ints[2]
+    wide = even.shape[1]
+    cols = pl.ds(start, wide)
     is_even = sides(ints[1])[0] == k
     to_d = row(jnp.where(is_even, even[...], odd[...]))
     to_c = row(jnp.where(is_even, odd[...], even[...]))
     put(hold.at[0], -product(row(c_in[1 - k]), to_c))
-    copies = [pltpu.make_async_copy(hold.at[0], c_out.at[slab], sems.at[0])]
+    copies = [pltpu.make_async_copy(hold.at[0], c_out.at[slab, :, cols], sems.at[0])]
     copies[0].start()
-    d = row(d_in[...]) - product(row(c_in[k]), to_d)
+    d = row(d_in[:, start : start + wide]) - product(row(c_in[k]), to_d)
     if k == 0:
         put(d_out, d)
     else:
         put(hold.at[1], d)
-        copies.append(pltpu.make_async_copy(hold.at[1], d_out.at[slab], sems.at[1]))
+        copies.append(pltpu.make_async_copy(hold.at[1], d_out.at[slab, :, cols], sems.at[1]))
         copies[1].start()
     for copy in copies:
         copy.wait()
@@ -352,11 +361,12 @@
     z_hop_right = send(down, -1)
     whole = shape(rows, 2 * w, w)
     kept = pl.BlockSpec(memory_space=pl.ANY)
-    d_a, d_b, u_a, l_b, g_a, k_a, d_out, u_out, l_out = pl.pallas_call(
+    gain = jax.ShapeDtypeStruct((4, w, 2 * w), BF)
+    d_a, d_b, u_a, l_b, g_a, g_b, k_a, d_out, u_out, l_out = pl.pallas_call(
         near_kernel,
-        out_shape=(block,) * 6 + (whole,) * 3,
+        out_shape=(block,) * 4 + (gain, gain, block) + (whole,) * 3,
         in_specs=[VMEM] * 5 + [SMEM],
-        out_specs=(VMEM,) * 6 + (kept,) * 3,
+        out_specs=(VMEM,) * 7 + (kept,) * 3,
         compiler_params=PARAMS,
         name="near",
     )(onsite, hop, hop_left, up, down, scalars)
@@ -375,7 +385,7 @@
     d_b, c_b, p_b = second(
         d_b,
         l_b,
-        hop[1],
+        g_b,
         z_hop_right[: 2 * w],
         z_hop_right[2 * w :],
         scalars,
@@ -396,35 +406,41 @@
     even_a, odd_a = swaps(p_a, 2)
     d_b, c_b, p_b = third(d_b, c_b, even_b, odd_b, scalars, at_a)
     first_b = swaps(p_b[: 2 * w], 2)
-    second_b = swaps(p_b[2 * w :], 2)
-
-    hold = [pltpu.VMEM((2, 2 * w, w), F32), pltpu.SemaphoreType.DMA((2,))]
+    cuts = (0, w // 2)
+    lower_b = [swaps(p_b[2 * w :, cut : cut + w // 2], 2) for cut in cuts]
+
+    def hold(wide):
+        return [pltpu.VMEM((2, 2 * w, wide), F32), pltpu.SemaphoreType.DMA((2,))]
+
     take_upper = pl.pallas_call(
-        functools.partial(last_kernel, 0),
+        functools.partial(last_kernel, 0, 0),
         out_shape=(block, whole),
         in_specs=[VMEM] * 4 + [SMEM, kept],
         out_specs=(VMEM, kept),
         input_output_aliases={5: 1},
-        scratch_shapes=hold,
+        scratch_shapes=hold(w),
         compiler_params=PARAMS,
         name="take_upper",
     )
-    take_lower = pl.pallas_call(
-        functools.partial(last_kernel, 1),
-        out_shape=(whole, whole),
-        in_specs=[VMEM] * 4 + [SMEM, kept, kept],
-        out_specs=(kept, kept),
-        input_output_aliases={5: 1, 6: 0},
-        scratch_shapes=hold,
-        compiler_params=PARAMS,
-        name="take_lower",
-    )
+    take_lower = [
+        pl.pallas_call(
+            functools.partial(last_kernel, 1, cut),
+            out_shape=(whole, whole),
+            in_specs=[VMEM] * 4 + [SMEM, kept, kept],
+            out_specs=(kept, kept),
+            input_output_aliases={5: 1, 6: 0},
+            scratch_shapes=hold(w // 2),
+            compiler_params=PARAMS,
+        )
+        for cut in cuts
+    ]
     d_a, u_out = take_upper(d_a, c_a, even_a[: 2 * w], odd_a[: 2 * w], at_a, u_out)
-    d_out, l_out = take_lower(
-        d_a, c_a, even_a[2 * w :], odd_a[2 * w :], at_a, l_out, d_out
-    )
+    for take, cut in zip(take_lower, cuts):
+        arrived = (x[2 * w :, cut : cut + w // 2] for x in (even_a, odd_a))
+        d_out, l_out = take(d_a, c_a, *arrived, at_a, l_out, d_out)
     d_b, u_out = take_upper(d_b, c_b, *first_b, at_b, u_out)
-    d_out, l_out = take_lower(d_b, c_b, *second_b, at_b, l_out, d_out)
+    for take, arrived in zip(take_lower, lower_b):
+        d_out, l_out = take(d_b, c_b, *arrived, at_b, l_out, d_out)
     return tuple(x.reshape(rows, 2, w, w) for x in (d_out, u_out, l_out))
 
 

time: 154 us -> 162 us (1.052)
  the two profiles are of different devices: /device:TPU:89 before, /device:TPU:58 now
where the time goes in v4:
time: 162 us
  starting transfers between devices  74.5 us (46%)
  Pallas kernels  73.4 us (45%)
  waiting for transfers between devices  10.1 us (6%)
  between operations  2.49 us (2%)
    ppermute x6, starting transfers between devices, swaps(): from_odd = lax.ppermute(x, 'slab', odd)  66.3 us
    pallas_call x1, Pallas kernels, reduce_levels(): second(d_b, l_b, g_b, z_hop_right[:2 * w], z_hop_right[2 * w:], scalars,...  27.6 us
    pallas_call x1, Pallas kernels, reduce_levels(): d_a, c_a, p_a = third(d_a, c_a, even_a, odd_a, scalars, at_a)  7.97 us
    pallas_call x1, Pallas kernels, reduce_levels(): d_b, c_b, p_b = third(d_b, c_b, even_b, odd_b, scalars, at_a)  7.96 us
    pallas_call x1, Pallas kernels, reduce_levels(): second(d_a, u_a, g_a, z_left, k_a, scalars, jnp.zeros((1,), jnp.int32))  7.67 us
    ppermute x3, starting transfers between devices, send(): lax.ppermute(x, 'slab', [(i, i + by) for i in range(size) if 0 <= i + by...  7.48 us
    pallas_call x1, Pallas kernels, reduce_levels(): pl.pallas_call(first_kernel, out_shape=(block, pair), in_specs=[VMEM, pl....  6.77 us
    ppermute x3, waiting for transfers between devices, send(): lax.ppermute(x, 'slab', [(i, i + by) for i in range(size) if 0 <= i + by...  5.16 us
  transfers between devices with their start and end apart: 15, of which 2 were waited for; matrix products, arithmetic and copies ran while one was open for 0% of the time, Pallas kernels for 44%

profile of v4, /device:TPU:58, one launch (start us, length us, event | category | flops | bytes accessed | tf_op | source)
XLA Modules:
  0.0 162.1 jit_solution(15807228535775405924)
XLA Ops:
  0.6 1.9 %collective-permute-start = (f32[2,512,256]{2,1,0:T(8,128)}, f32[2,512,256]{2,1,0:T(8,128)S(1)}, u32[]{:S(2)}, u32[]{:S(2)}) collective-permute-start(f32[2,512,256]{2,1,0:T(8,128)} %bitcast.10), channel_id=1, source_target_pairs={{0,4},{4,8},{8,12},{12,16},{16,20},{20,24},{24,28},{28,32},{32,36}... | collective-permute-start | bytes 3145736 | tf_op jit(solution)/shard_map/ppermute | solution.py:323
  3.9 0.1 pad_maximum_fusion.scalars
  3.9 0.1 pad_add_fusion
  4.0 1.2 copy-done
  5.2 6.8 %first.1 = (f32[512,256]{1,0:T(8,128)S(1)}, f32[1024,256]{1,0:T(8,128)S(1)}) custom-call(f32[2,512,256]{2,1,0:T(8,128)S(1)} %bitcast.8, f32[2,512,256]{2,1,0:T(8,128)} %bitcast.11, f32[3]{0:T(128)S(1)} %pad_maximum_fusion.scalars), custom_call_target="tpu_custom_call" | custom-call | tf_op jit(solution)/shard_map/first/pallas_call | solution.py:351
  12.0 3.6 %collective-permute-start.1 = (f32[1024,256]{1,0:T(8,128)S(1)}, f32[1024,256]{1,0:T(8,128)S(1)}, u32[]{:S(2)}, u32[]{:S(2)}) collective-permute-start(f32[1024,256]{1,0:T(8,128)S(1)} %get-tuple-element.44.z_hop_a), channel_id=1, source_target_pairs={{4,0},{8,4},{12,8},{16,12},{20,16},{24,20},{28,24},{32,28},{36,32}... | collective-permute-start | bytes 3145736 | tf_op jit(solution)/shard_map/ppermute | solution.py:323
  15.7 1.9 %collective-permute-start.6 = (f32[512,256]{1,0:T(8,128)S(1)}, f32[512,256]{1,0:T(8,128)S(1)}, u32[]{:S(2)}, u32[]{:S(2)}) collective-permute-start(f32[512,256]{1,0:T(8,128)S(1)} %get-tuple-element.43.z_b), channel_id=1, source_target_pairs={{0,4},{4,8},{8,12},{12,16},{16,20},{20,24},{24,28},{28,32},{32,36}... | collective-permute-start | bytes 1572872 | tf_op jit(solution)/shard_map/ppermute | solution.py:323
  17.6 3.4 %near.1 = (f32[512,256]{1,0:T(8,128)S(1)}, f32[512,256]{1,0:T(8,128)S(1)}, f32[512,256]{1,0:T(8,128)S(1)}, f32[512,256]{1,0:T(8,128)S(1)}, bf16[4,256,512]{2,1,0...) custom-call(f32[2,512,256]{2,1,0:T(8,128)S(1)} %bitcast.9, ...), custom_call_target="tpu_custom_call" | custom-call | tf_op jit(solution)/shard_map/near/pallas_call | solution.py:365
  21.0 5.2 %collective-permute-done.6.z = f32[512,256]{1,0:T(8,128)S(1)} collective-permute-done((f32[512,256]{1,0:T(8,128)S(1)}, f32[512,256]{1,0:T(8,128)S(1)}, u32[]{:S(2)}, u32[]{:S(2)}) %collective-permute-start.6) | collective-permute-done | bytes 524320 | tf_op jit(solution)/shard_map/ppermute | solution.py:323
  26.2 7.7 %second.3 = (f32[512,256]{1,0:T(8,128)S(1)}, f32[2,512,256]{2,1,0:T(8,128)S(1)}, f32[1024,256]{1,0:T(8,128)S(1)}) custom-call(f32[512,256]{1,0:T(8,128)S(1)} %get-tuple-element.56.d_in, f32[512,256]{1,0:T(8,128)S(1)} %get-tuple-element.57.c_in, bf16[4,256,512]{2,1,0:T(8,128)(2,1)S(1)} %get-tuple-element.58.g, f32[512,256]{1,0:T(8,128)S(1)} %collective-permute-done.6.z, ...), custom_call_target="tpu_custom_call" | custom-call | tf_op jit(solution)/shard_map/second/pallas_call | solution.py:383
  33.8 0.3 collective-permute-start.7
  34.1 6.3 %collective-permute-start.8 = (f32[1024,256]{1,0:T(8,128)S(1)}, f32[1024,256]{1,0:T(8,128)S(1)}, u32[]{:S(2)}, u32[]{:S(2)}) collective-permute-start(f32[1024,256]{1,0:T(8,128)S(1)} %get-tuple-element.62), channel_id=1, source_target_pairs={{4,8},{8,4},{12,16},{16,12},{20,24},{24,20},{28,32},{32,28},{36,40... | collective-permute-start | bytes 3145736 | tf_op jit(solution)/shard_map/ppermute | solution.py:332
  40.5 27.6 %second.2 = (f32[512,256]{1,0:T(8,128)S(1)}, f32[2,512,256]{2,1,0:T(8,128)S(1)}, f32[1024,256]{1,0:T(8,128)S(1)}) custom-call(f32[512,256]{1,0:T(8,128)S(1)} %get-tuple-element.45.d_in, f32[512,256]{1,0:T(8,128)S(1)} %get-tuple-element.46.c_in, bf16[4,256,512]{2,1,0:T(8,128)(2,1)S(1)} %get-tuple-element.47.g, f32[512,256]{1,0:T(8,128)S(1)} %get-tuple-element.88.z, ...), custom_call_target="tpu_custom_call" | custom-call | tf_op jit(solution)/shard_map/second/pallas_call | solution.py:385
  68.1 0.1 collective-permute-start.2
  68.2 1.9 %collective-permute-start.3 = (f32[1024,256]{1,0:T(8,128)S(1)}, f32[1024,256]{1,0:T(8,128)S(1)}, u32[]{:S(2)}, u32[]{:S(2)}) collective-permute-start(f32[1024,256]{1,0:T(8,128)S(1)} %get-tuple-element.50), channel_id=1, source_target_pairs={{4,8},{8,4},{12,16},{16,12},{20,24},{24,20},{28,32},{32,28},{36,40... | collective-permute-start | bytes 3145736 | tf_op jit(solution)/shard_map/ppermute | solution.py:332
  70.1 8.0 %third.3 = (f32[512,256]{1,0:T(8,128)S(1)}, f32[2,512,256]{2,1,0:T(8,128)S(1)}, f32[1024,256]{1,0:T(8,128)S(1)}) custom-call(f32[512,256]{1,0:T(8,128)S(1)} %get-tuple-element.60.d_in, f32[2,512,256]{2,1,0:T(8,128)S(1)} %get-tuple-element.61.c_in, f32[1024,256]{1,0:T(8,128)S(1)} %collective-permute-done.7.even, f32[1024,256]{1,0:T(8,128)S(1)} %collective-permute-done.8.odd, ...), custom_call_target="tpu_custom_call" | custom-call | tf_op jit(solution)/shard_map/third/pallas_call | solution.py:405
  78.1 0.1 collective-permute-start.9
  78.2 3.8 %collective-permute-start.10 = (f32[1024,256]{1,0:T(8,128)S(1)}, f32[1024,256]{1,0:T(8,128)S(1)}, u32[]{:S(2)}, u32[]{:S(2)}) collective-permute-start(f32[1024,256]{1,0:T(8,128)S(1)} %get-tuple-element.65), channel_id=1, source_target_pairs={{8,16},{16,8},{12,20},{20,12},{24,32},{32,24},{28,36},{36,28},{40,... | collective-permute-start | bytes 3145736 | tf_op jit(solution)/shard_map/ppermute | solution.py:332
  81.9 4.9 %collective-permute-done.3.odd = f32[1024,256]{1,0:T(8,128)S(1)} collective-permute-done((f32[1024,256]{1,0:T(8,128)S(1)}, f32[1024,256]{1,0:T(8,128)S(1)}, u32[]{:S(2)}, u32[]{:S(2)}) %collective-permute-start.3) | collective-permute-done | bytes 1048608 | tf_op jit(solution)/shard_map/ppermute | solution.py:332
  86.8 8.0 %third.2 = (f32[512,256]{1,0:T(8,128)S(1)}, f32[2,512,256]{2,1,0:T(8,128)S(1)}, f32[1024,256]{1,0:T(8,128)S(1)}) custom-call(f32[512,256]{1,0:T(8,128)S(1)} %get-tuple-element.48.d_in, f32[2,512,256]{2,1,0:T(8,128)S(1)} %get-tuple-element.49.c_in, f32[1024,256]{1,0:T(8,128)S(1)} %collective-permute-done.2.even, f32[1024,256]{1,0:T(8,128)S(1)} %collective-permute-done.3.odd, ...), custom_call_target="tpu_custom_call" | custom-call | tf_op jit(solution)/shard_map/third/pallas_call | solution.py:407
  94.8 0.1 collective-permute-start.4
  94.9 21.7 %collective-permute-start.5 = (f32[512,256]{1,0:T(8,128)S(1)}, f32[512,256]{1,0:T(8,128)S(1)}, u32[]{:S(2)}, u32[]{:S(2)}) collective-permute-start(f32[512,256]{1,0:T(8,128)S(1)} %slice.35), channel_id=1, source_target_pairs={{8,16},{16,8},{12,20},{20,12},{24,32},{32,24},{28,36},{36,28},{40,... | collective-permute-start | bytes 1572872 | tf_op jit(solution)/shard_map/ppermute | solution.py:332
  116.7 0.1 collective-permute-start.13
  116.8 12.6 %collective-permute-start.14 = (f32[512,128]{1,0:T(8,128)S(1)}, f32[512,128]{1,0:T(8,128)S(1)}, u32[]{:S(2)}, u32[]{:S(2)}) collective-permute-start(f32[512,128]{1,0:T(8,128)S(1)} %get-tuple-element.85), channel_id=1, source_target_pairs={{8,16},{16,8},{12,20},{20,12},{24,32},{32,24},{28,36},{36,28},{40,... | collective-permute-start | bytes 786440 | tf_op jit(solution)/shard_map/ppermute | solution.py:332
  129.4 0.1 collective-permute-start.11
  129.5 20.1 %collective-permute-start.12 = (f32[512,128]{1,0:T(8,128)S(1)}, f32[512,128]{1,0:T(8,128)S(1)}, u32[]{:S(2)}, u32[]{:S(2)}) collective-permute-start(f32[512,128]{1,0:T(8,128)S(1)} %get-tuple-element.86), channel_id=1, source_target_pairs={{8,16},{16,8},{12,20},{20,12},{24,32},{32,24},{28,36},{36,28},{40,... | collective-permute-start | bytes 786440 | tf_op jit(solution)/shard_map/ppermute | solution.py:332
  149.7 2.0 %take_upper.2 = (f32[512,256]{1,0:T(8,128)S(1)}, f32[2,512,256]{2,1,0:T(8,128)}) custom-call(f32[512,256]{1,0:T(8,128)S(1)} %get-tuple-element.63.d_in, f32[2,512,256]{2,1,0:T(8,128)S(1)} %get-tuple-element.64.c_in, f32[512,256]{1,0:T(8,128)S(1)} %slice.46.even, f32[512,256]{1,0:T(8,128)S(1)} %slice.47.odd, ...), custom_call_target="tpu_custom_call", output_to_operand_aliasing={{1}: (5, {})} | custom-call | tf_op jit(solution)/shard_map/take_upper/pallas_call | solution.py:437
  151.8 2.0 %shard_map.67 = (f32[2,512,256]{2,1,0:T(8,128)}, f32[2,512,256]{2,1,0:T(8,128)}) custom-call(f32[512,256]{1,0:T(8,128)S(1)} %get-tuple-element.69.d_in, f32[2,512,256]{2,1,0:T(8,128)S(1)} %get-tuple-element.64.c_in, f32[512,128]{1,0:T(8,128)S(1)} %get-tuple-element.83.even, ...), custom_call_target="tpu_custom_call", output_to_operand_aliasing={{1}: (5, {}), {0}: (6, {})} | custom-call | tf_op jit(solution)/shard_map/pallas_call | solution.py:440
  153.8 2.0 %shard_map.68 = (f32[2,512,256]{2,1,0:T(8,128)}, f32[2,512,256]{2,1,0:T(8,128)}) custom-call(f32[512,256]{1,0:T(8,128)S(1)} %get-tuple-element.69.d_in, f32[2,512,256]{2,1,0:T(8,128)S(1)} %get-tuple-element.64.c_in, f32[512,128]{1,0:T(8,128)S(1)} %get-tuple-element.84.even, ...), custom_call_target="tpu_custom_call", output_to_operand_aliasing={{1}: (5, {}), {0}: (6, {})} | custom-call | tf_op jit(solution)/shard_map/pallas_call | solution.py:440
  155.8 2.0 %take_upper.3 = (f32[512,256]{1,0:T(8,128)S(1)}, f32[2,512,256]{2,1,0:T(8,128)}) custom-call(f32[512,256]{1,0:T(8,128)S(1)} %get-tuple-element.52.d_in, f32[2,512,256]{2,1,0:T(8,128)S(1)} %get-tuple-element.53.c_in, f32[512,256]{1,0:T(8,128)S(1)} %collective-permute-done.4.even, ...), custom_call_target="tpu_custom_call", output_to_operand_aliasing={{1}: (5, {})} | custom-call | tf_op jit(solution)/shard_map/take_upper/pallas_call | solution.py:441
  157.9 2.0 %shard_map.69 = (f32[2,512,256]{2,1,0:T(8,128)}, f32[2,512,256]{2,1,0:T(8,128)}) custom-call(f32[512,256]{1,0:T(8,128)S(1)} %get-tuple-element.68.d_in, f32[2,512,256]{2,1,0:T(8,128)S(1)} %get-tuple-element.53.c_in, f32[512,128]{1,0:T(8,128)S(1)} %collective-permute-done.13.even, ...), custom_call_target="tpu_custom_call", output_to_operand_aliasing={{1}: (5, {}), {0}: (6, {})} | custom-call | tf_op jit(solution)/shard_map/pallas_call | solution.py:443
  159.9 2.0 %shard_map.70 = (f32[2,512,256]{2,1,0:T(8,128)}, f32[2,512,256]{2,1,0:T(8,128)}) custom-call(f32[512,256]{1,0:T(8,128)S(1)} %get-tuple-element.68.d_in, f32[2,512,256]{2,1,0:T(8,128)S(1)} %get-tuple-element.53.c_in, f32[512,128]{1,0:T(8,128)S(1)} %collective-permute-done.11.even, ...), custom_call_target="tpu_custom_call", output_to_operand_aliasing={{1}: (5, {}), {0}: (6, {})} | custom-call | tf_op jit(solution)/shard_map/pallas_call | solution.py:443
  (23 shorter events, 0.3 us)
Async XLA Ops:
  0.6 17.0 %collective-permute-start = (f32[2,512,256]{2,1,0:T(8,128)}, f32[2,512,256]{2,1,0:T(8,128)S(1)}, u32[]{:S(2)}, u32[]{:S(2)}) collective-permute-start(f32[2,512,256]{2,1,0:T(8,128)} %bitcast.10), channel_id=1, source_target_pairs={{0,4},{4,8},{8,12},{12,16},{16,20},{20,24},{24,28},{28,32},{32,36}... | collective-permute-start | bytes 3145736 | tf_op jit(solution)/shard_map/ppermute | solution.py:323
  4.0 1.2 copy-start
  5.2 12.4 %copy-start.1 = (f32[2,2,256,256]{3,2,1,0:T(8,128)S(1)}, f32[2,2,256,256]{3,2,1,0:T(8,128)}, u32[]{:S(2)}) copy-start(f32[2,2,256,256]{3,2,1,0:T(8,128)} %param.5) | copy-start | bytes 3145732
  12.0 28.4 %collective-permute-start.1 = (f32[1024,256]{1,0:T(8,128)S(1)}, f32[1024,256]{1,0:T(8,128)S(1)}, u32[]{:S(2)}, u32[]{:S(2)}) collective-permute-start(f32[1024,256]{1,0:T(8,128)S(1)} %get-tuple-element.44.z_hop_a), channel_id=1, source_target_pairs={{4,0},{8,4},{12,8},{16,12},{20,16},{24,20},{28,24},{32,28},{36,32}... | collective-permute-start | bytes 3145736 | tf_op jit(solution)/shard_map/ppermute | solution.py:323
  15.7 10.5 %collective-permute-start.6 = (f32[512,256]{1,0:T(8,128)S(1)}, f32[512,256]{1,0:T(8,128)S(1)}, u32[]{:S(2)}, u32[]{:S(2)}) collective-permute-start(f32[512,256]{1,0:T(8,128)S(1)} %get-tuple-element.43.z_b), channel_id=1, source_target_pairs={{0,4},{4,8},{8,12},{12,16},{16,20},{20,24},{24,28},{28,32},{32,36}... | collective-permute-start | bytes 1572872 | tf_op jit(solution)/shard_map/ppermute | solution.py:323
  33.8 36.2 %collective-permute-start.7 = (f32[1024,256]{1,0:T(8,128)S(1)}, f32[1024,256]{1,0:T(8,128)S(1)}, u32[]{:S(2)}, u32[]{:S(2)}) collective-permute-start(f32[1024,256]{1,0:T(8,128)S(1)} %get-tuple-element.62), channel_id=1, source_target_pairs={{0,4},{4,0},{8,12},{12,8},{16,20},{20,16},{24,28},{28,24},{32,36},... | collective-permute-start | bytes 3145736 | tf_op jit(solution)/shard_map/ppermute | solution.py:333
  34.1 36.0 %collective-permute-start.8 = (f32[1024,256]{1,0:T(8,128)S(1)}, f32[1024,256]{1,0:T(8,128)S(1)}, u32[]{:S(2)}, u32[]{:S(2)}) collective-permute-start(f32[1024,256]{1,0:T(8,128)S(1)} %get-tuple-element.62), channel_id=1, source_target_pairs={{4,8},{8,4},{12,16},{16,12},{20,24},{24,20},{28,32},{32,28},{36,40... | collective-permute-start | bytes 3145736 | tf_op jit(solution)/shard_map/ppermute | solution.py:332
  68.1 13.9 %collective-permute-start.2 = (f32[1024,256]{1,0:T(8,128)S(1)}, f32[1024,256]{1,0:T(8,128)S(1)}, u32[]{:S(2)}, u32[]{:S(2)}) collective-permute-start(f32[1024,256]{1,0:T(8,128)S(1)} %get-tuple-element.50), channel_id=1, source_target_pairs={{0,4},{4,0},{8,12},{12,8},{16,20},{20,16},{24,28},{28,24},{32,36},... | collective-permute-start | bytes 3145736 | tf_op jit(solution)/shard_map/ppermute | solution.py:333
  68.2 18.7 %collective-permute-start.3 = (f32[1024,256]{1,0:T(8,128)S(1)}, f32[1024,256]{1,0:T(8,128)S(1)}, u32[]{:S(2)}, u32[]{:S(2)}) collective-permute-start(f32[1024,256]{1,0:T(8,128)S(1)} %get-tuple-element.50), channel_id=1, source_target_pairs={{4,8},{8,4},{12,16},{16,12},{20,24},{24,20},{28,32},{32,28},{36,40... | collective-permute-start | bytes 3145736 | tf_op jit(solution)/shard_map/ppermute | solution.py:332
  78.1 51.3 %collective-permute-start.9 = (f32[1024,256]{1,0:T(8,128)S(1)}, f32[1024,256]{1,0:T(8,128)S(1)}, u32[]{:S(2)}, u32[]{:S(2)}) collective-permute-start(f32[1024,256]{1,0:T(8,128)S(1)} %get-tuple-element.65), channel_id=1, source_target_pairs={{0,8},{8,0},{4,12},{12,4},{16,24},{24,16},{20,28},{28,20},{32,40},... | collective-permute-start | bytes 3145736 | tf_op jit(solution)/shard_map/ppermute | solution.py:333
  78.2 51.3 %collective-permute-start.10 = (f32[1024,256]{1,0:T(8,128)S(1)}, f32[1024,256]{1,0:T(8,128)S(1)}, u32[]{:S(2)}, u32[]{:S(2)}) collective-permute-start(f32[1024,256]{1,0:T(8,128)S(1)} %get-tuple-element.65), channel_id=1, source_target_pairs={{8,16},{16,8},{12,20},{20,12},{24,32},{32,24},{28,36},{36,28},{40,... | collective-permute-start | bytes 3145736 | tf_op jit(solution)/shard_map/ppermute | solution.py:332
  94.8 22.0 %collective-permute-start.4 = (f32[512,256]{1,0:T(8,128)S(1)}, f32[512,256]{1,0:T(8,128)S(1)}, u32[]{:S(2)}, u32[]{:S(2)}) collective-permute-start(f32[512,256]{1,0:T(8,128)S(1)} %slice.35), channel_id=1, source_target_pairs={{0,8},{8,0},{4,12},{12,4},{16,24},{24,16},{20,28},{28,20},{32,40},... | collective-permute-start | bytes 1572872 | tf_op jit(solution)/shard_map/ppermute | solution.py:333
  94.9 60.9 %collective-permute-start.5 = (f32[512,256]{1,0:T(8,128)S(1)}, f32[512,256]{1,0:T(8,128)S(1)}, u32[]{:S(2)}, u32[]{:S(2)}) collective-permute-start(f32[512,256]{1,0:T(8,128)S(1)} %slice.35), channel_id=1, source_target_pairs={{8,16},{16,8},{12,20},{20,12},{24,32},{32,24},{28,36},{36,28},{40,... | collective-permute-start | bytes 1572872 | tf_op jit(solution)/shard_map/ppermute | solution.py:332
  116.7 41.2 %collective-permute-start.13 = (f32[512,128]{1,0:T(8,128)S(1)}, f32[512,128]{1,0:T(8,128)S(1)}, u32[]{:S(2)}, u32[]{:S(2)}) collective-permute-start(f32[512,128]{1,0:T(8,128)S(1)} %get-tuple-element.85), channel_id=1, source_target_pairs={{0,8},{8,0},{4,12},{12,4},{16,24},{24,16},{20,28},{28,20},{32,40},... | collective-permute-start | bytes 786440 | tf_op jit(solution)/shard_map/ppermute | solution.py:333
  116.8 41.1 %collective-permute-start.14 = (f32[512,128]{1,0:T(8,128)S(1)}, f32[512,128]{1,0:T(8,128)S(1)}, u32[]{:S(2)}, u32[]{:S(2)}) collective-permute-start(f32[512,128]{1,0:T(8,128)S(1)} %get-tuple-element.85), channel_id=1, source_target_pairs={{8,16},{16,8},{12,20},{20,12},{24,32},{32,24},{28,36},{36,28},{40,... | collective-permute-start | bytes 786440 | tf_op jit(solution)/shard_map/ppermute | solution.py:332
  129.4 30.5 %collective-permute-start.11 = (f32[512,128]{1,0:T(8,128)S(1)}, f32[512,128]{1,0:T(8,128)S(1)}, u32[]{:S(2)}, u32[]{:S(2)}) collective-permute-start(f32[512,128]{1,0:T(8,128)S(1)} %get-tuple-element.86), channel_id=1, source_target_pairs={{0,8},{8,0},{4,12},{12,4},{16,24},{24,16},{20,28},{28,20},{32,40},... | collective-permute-start | bytes 786440 | tf_op jit(solution)/shard_map/ppermute | solution.py:333
  129.5 30.4 %collective-permute-start.12 = (f32[512,128]{1,0:T(8,128)S(1)}, f32[512,128]{1,0:T(8,128)S(1)}, u32[]{:S(2)}, u32[]{:S(2)}) collective-permute-start(f32[512,128]{1,0:T(8,128)S(1)} %get-tuple-element.86), channel_id=1, source_target_pairs={{8,16},{16,8},{12,20},{20,12},{24,32},{32,24},{28,36},{36,28},{40,... | collective-permute-start | bytes 786440 | tf_op jit(solution)/shard_map/ppermute | solution.py:332

commit v5 on v4

--- a/solution.py
+++ b/solution.py
@@ -227,41 +227,46 @@
     return 1 - parity, parity
 
 
-def first_kernel(onsite, hop, scalars, up, down, sem, *work):
-    w = onsite.shape[2]
-    beside = pltpu.make_async_copy(hop.at[0], down.at[pl.ds(2 * w, 2 * w)], sem)
-    beside.start()
+def first_kernel(onsite, scalars, ints, z_even, z_odd, z_own, *work):
     invert([initial(row(onsite[i]), scalars) for i in range(2)], scalars[1], work)
-    put(up, work[0][1])
-    put(down, work[0][0])
-    beside.wait()
+    for i in range(2):
+        put(z_own.at[i], work[0][i])
+    put(z_even, work[0][1 - ints[0]])
+    put(z_odd, work[0][ints[0]])
 
 
 def near_kernel(
-    onsite, hop, hop_left, z_b, z_hop_a, scalars, d_a, d_b, u_a, l_b, g_a, g_b, k_a, *outputs
+    onsite, hop, hop_even, hop_odd, z, scalars, ints, d_out, c_out, g_out, k_out, *outputs
 ):
+    run_b = ints[0]
+    run_a = 1 - run_b
+    left = [jnp.where(run_b == 0, hop_odd[k], hop_even[k]) for k in range(2)]
+    right = jnp.where(run_b == 0, hop_even[0], hop_odd[0])
     h = row(hop[0])
     h_adj = adjoint(h)
-    before, after = row(hop_left[1]), row(hop[1])
+    before, after = row(left[1]), row(hop[1])
     before_adj = adjoint(before)
-    for out, pair in ((g_a, (before_adj, before)), (g_b, (after, adjoint(after)))):
+    for run, pair in ((run_a, (before_adj, before)), (run_b, (after, adjoint(after)))):
         for k, value in enumerate(pair):
-            out[2 * k], out[2 * k + 1] = split(value)
-    put(k_a, adjoint(row(hop_left[0])))
-    t = product(h, row(z_b[...]))
-    put(d_a, initial(row(onsite[0]), scalars) - product(t, h_adj))
-    put(u_a, product(t, after) * (-scalars[2]))
-    t = product(h_adj, part(z_hop_a, 0))
-    put(d_b, initial(row(onsite[1]), scalars) - product(t, h))
-    put(l_b, -product(t, before_adj))
-
-
-def second_kernel(d_in, c_in, g, z, k, scalars, side, d_out, c_out, payload, *work):
-    at = side[0]
-    t = times((g[0], g[1]), row(z[...]))
-    put(d_out, row(d_in[...]) - multiply(split(t), (g[2], g[3])))
-    c_out[1 - at] = c_in[...]
-    pieces = deferred(c_out, at, t, row(k[...]), -1.0)
+            high, low = split(value)
+            g_out[run, 2 * k] = high
+            g_out[run, 2 * k + 1] = low
+    put(k_out.at[run_a], adjoint(row(left[0])))
+    k_out[run_b] = right
+    t = product(h, row(z[1]))
+    put(d_out.at[run_a], initial(row(onsite[0]), scalars) - product(t, h_adj))
+    put(c_out.at[run_a], product(t, after) * (-scalars[2]))
+    t = product(h_adj, row(z[0]))
+    put(d_out.at[run_b], initial(row(onsite[1]), scalars) - product(t, h))
+    put(c_out.at[run_b], -product(t, before_adj))
+
+
+def second_kernel(d_in, c_in, g, z, k, scalars, ints, d_out, c_out, payload, *work):
+    run, at = ints[0], ints[1]
+    t = times((g[run, 0], g[run, 1]), row(z[...]))
+    put(d_out, row(d_in[run]) - multiply(split(t), (g[run, 2], g[run, 3])))
+    c_out[1 - at] = c_in[run]
+    pieces = deferred(c_out, at, t, row(k[run]), -1.0)
     solve(row(d_out[...]), c_out, pieces, scalars[1], payload, work)
 
 
@@ -318,18 +323,13 @@
 PARAMS = pltpu.CompilerParams(vmem_limit_bytes=20 << 20)
 
 
-def send(x, by):
-    size = lax.axis_size("slab")
-    return lax.ppermute(x, "slab", [(i, i + by) for i in range(size) if 0 <= i + by < size])
-
-
-def swaps(x, by):
+def swaps(x, by, for_odd=None):
     size = lax.axis_size("slab")
     even, odd = [], []
     for i in range(size - by):
         pairs = odd if i // by % 2 else even
         pairs += [(i, i + by), (i + by, i)]
-    from_odd = lax.ppermute(x, "slab", odd)
+    from_odd = lax.ppermute(x if for_odd is None else for_odd, "slab", odd)
     from_even = lax.ppermute(x, "slab", even)
     return from_even, from_odd
 
@@ -343,33 +343,37 @@
     scalars = jnp.stack([energy_level[0], broadening[0], keep])
     position = lax.axis_index("slab")
     near, far = position & 1, (position >> 1) & 1
-    at_a, at_b = (jnp.stack([near, far, jnp.int32(k)]) for k in range(2))
-    scalars, at_a, at_b = lax.optimization_barrier((scalars, at_a, at_b))
-
-    hop_left = send(hop, 1)
+    at_a, at_b = (jnp.stack([near, far, slab]) for slab in (near, 1 - near))
+    run_a, run_b = (
+        jnp.stack([jnp.int32(run), side]) for run, side in ((0, 1 - near), (1, near))
+    )
+    scalars, at_a, at_b, run_a, run_b = lax.optimization_barrier(
+        (scalars, at_a, at_b, run_a, run_b)
+    )
+
+    hop_even, hop_odd = swaps(hop, 1)
     block, pair, two = shape(2 * w, w), shape(4 * w, w), shape(2, 2 * w, w)
-    up, down = pl.pallas_call(
+    z_even, z_odd, z_own = pl.pallas_call(
         first_kernel,
-        out_shape=(block, pair),
-        in_specs=[VMEM, pl.BlockSpec(memory_space=pl.ANY), SMEM],
-        out_specs=(VMEM,) * 2,
-        scratch_shapes=[pltpu.SemaphoreType.DMA] + work(rows, w),
+        out_shape=(block, block, two),
+        in_specs=[VMEM, SMEM, SMEM],
+        out_specs=(VMEM,) * 3,
+        scratch_shapes=work(rows, w),
         compiler_params=PARAMS,
         name="first",
-    )(onsite, pltpu.with_memory_space_constraint(hop, pltpu.HBM), scalars)
-    z_left = send(up, 1)
-    z_hop_right = send(down, -1)
-    whole = shape(rows, 2 * w, w)
+    )(onsite, scalars, at_a)
+    from_even, from_odd = swaps(z_even, 1, z_odd)
     kept = pl.BlockSpec(memory_space=pl.ANY)
-    gain = jax.ShapeDtypeStruct((4, w, 2 * w), BF)
-    d_a, d_b, u_a, l_b, g_a, g_b, k_a, d_out, u_out, l_out = pl.pallas_call(
+    gain = jax.ShapeDtypeStruct((2, 4, w, 2 * w), BF)
+    d_near, c_near, g_near, k_near, d_out, u_out, l_out = pl.pallas_call(
         near_kernel,
-        out_shape=(block,) * 4 + (gain, gain, block) + (whole,) * 3,
-        in_specs=[VMEM] * 5 + [SMEM],
-        out_specs=(VMEM,) * 7 + (kept,) * 3,
+        out_shape=(two, two, gain, two) + (two,) * 3,
+        in_specs=[VMEM] * 5 + [SMEM] * 2,
+        out_specs=(VMEM,) * 4 + (kept,) * 3,
         compiler_params=PARAMS,
         name="near",
-    )(onsite, hop, hop_left, up, down, scalars)
+    )(onsite, hop, hop_even, hop_odd, z_own, scalars, at_a)
+    whole = two
 
     second = pl.pallas_call(
         second_kernel,
@@ -380,17 +384,9 @@
         compiler_params=PARAMS,
         name="second",
     )
-    d_a, c_a, p_a = second(d_a, u_a, g_a, z_left, k_a, scalars, jnp.zeros((1,), jnp.int32))
+    d_b, c_b, p_a = second(d_near, c_near, g_near, from_even, k_near, scalars, run_a)
     even_a, odd_a = swaps(p_a, 1)
-    d_b, c_b, p_b = second(
-        d_b,
-        l_b,
-        g_b,
-        z_hop_right[: 2 * w],
-        z_hop_right[2 * w :],
-        scalars,
-        jnp.ones((1,), jnp.int32),
-    )
+    d_a, c_a, p_b = second(d_near, c_near, g_near, from_odd, k_near, scalars, run_b)
     even_b, odd_b = swaps(p_b, 1)
 
     third = pl.pallas_call(

time: 162 us -> 171 us (1.056)
  the two profiles are of different devices: /device:TPU:58 before, /device:TPU:60 now
where the time goes in v5:
time: 171 us; the launch traced here: 170 us
  starting transfers between devices  103 us (60%)
  Pallas kernels  51.8 us (30%)
  waiting for transfers between devices  10.6 us (6%)
  local copies, waits for them, and re-layouts  2.67 us (2%)
  between operations  2.36 us (1%)
    ppermute x8, starting transfers between devices, swaps(): from_even = lax.ppermute(x, 'slab', even)  66.2 us
    ppermute x8, starting transfers between devices, swaps(): from_odd = lax.ppermute(x if for_odd is None else for_odd, 'slab', odd)  36.3 us
    ppermute x8, waiting for transfers between devices, swaps(): from_odd = lax.ppermute(x if for_odd is None else for_odd, 'slab', odd)  10.6 us
    pallas_call x1, Pallas kernels, reduce_levels(): second(d_near, c_near, g_near, from_odd, k_near, scalars, run_b)  7.64 us
    pallas_call x1, Pallas kernels, reduce_levels(): d_a, c_a, p_a = third(d_a, c_a, even_a, odd_a, scalars, at_a)  7.46 us
    pallas_call x1, Pallas kernels, reduce_levels(): second(d_near, c_near, g_near, from_even, k_near, scalars, run_a)  7.33 us
    pallas_call x1, Pallas kernels, reduce_levels(): d_b, c_b, p_b = third(d_b, c_b, even_b, odd_b, scalars, at_a)  6.99 us
    pallas_call x1, Pallas kernels, reduce_levels(): pl.pallas_call(first_kernel, out_shape=(block, block, two), in_specs=[VME...  6.83 us
  transfers between devices with their start and end apart: 16, of which 2 were waited for; matrix products, arithmetic and copies ran while one was open for 0% of the time, Pallas kernels for 29%

profile of v5, /device:TPU:60, one launch (start us, length us, event | category | flops | bytes accessed | tf_op | source)
XLA Modules:
  0.0 170.2 jit_solution(16611570996674919397)
XLA Ops:
  0.6 1.9 %collective-permute-start.1 = (f32[2,512,256]{2,1,0:T(8,128)}, f32[2,512,256]{2,1,0:T(8,128)S(1)}, u32[]{:S(2)}, u32[]{:S(2)}) collective-permute-start(f32[2,512,256]{2,1,0:T(8,128)} %bitcast.11), channel_id=1, source_target_pairs={{4,8},{8,4},{12,16},{16,12},{20,24},{24,20},{28,32},{32,28},{36,40... | collective-permute-start | bytes 3145736 | tf_op jit(solution)/shard_map/ppermute | solution.py:332
  2.6 1.4 collective-permute-start
  5.5 1.2 copy-done
  6.7 6.8 %first.1 = (f32[512,256]{1,0:T(8,128)S(1)}, f32[512,256]{1,0:T(8,128)S(1)}, f32[2,512,256]{2,1,0:T(8,128)S(1)}) custom-call(f32[2,512,256]{2,1,0:T(8,128)S(1)} %bitcast.9, f32[3]{0:T(128)S(1)} %pad_maximum_fusion.scalars, s32[3]{0:T(128)S(1)} %get-tuple-element.43.ints.parity), custom_call_target="tpu_custom_call" | custom-call | tf_op jit(solution)/shard_map/first/pallas_call | solution.py:356
  13.5 0.1 collective-permute-start.2
  13.6 2.8 %collective-permute-start.3 = (f32[512,256]{1,0:T(8,128)S(1)}, f32[512,256]{1,0:T(8,128)S(1)}, u32[]{:S(2)}, u32[]{:S(2)}) collective-permute-start(f32[512,256]{1,0:T(8,128)S(1)} %get-tuple-element.53), channel_id=1, source_target_pairs={{4,8},{8,4},{12,16},{16,12},{20,24},{24,20},{28,32},{32,28},{36,40... | collective-permute-start | bytes 1572872 | tf_op jit(solution)/shard_map/ppermute | solution.py:332
  16.5 0.5 collective-permute-done.1.hop_odd
  17.0 1.2 copy-done.1
  18.2 3.5 %near.1 = (f32[2,512,256]{2,1,0:T(8,128)S(1)}, f32[2,512,256]{2,1,0:T(8,128)S(1)}, bf16[2,4,256,512]{3,2,1,0:T(8,128)(2,1)S(1)}, f32[2,512,256]{2,1,0:T(8,128)S(...) custom-call(f32[2,512,256]{2,1,0:T(8,128)S(1)} %bitcast.10, ...), custom_call_target="tpu_custom_call" | custom-call | tf_op jit(solution)/shard_map/near/pallas_call | solution.py:368
  21.7 7.3 %second.2 = (f32[512,256]{1,0:T(8,128)S(1)}, f32[2,512,256]{2,1,0:T(8,128)S(1)}, f32[1024,256]{1,0:T(8,128)S(1)}) custom-call(f32[2,512,256]{2,1,0:T(8,128)S(1)} %get-tuple-element.45.d_in, f32[2,512,256]{2,1,0:T(8,128)S(1)} %get-tuple-element.46.c_in, bf16[2,4,256,512]{3,2,1,0:T(8,128)(2,1)S(1)} %get-tuple-element.47.g, ...), custom_call_target="tpu_custom_call" | custom-call | tf_op jit(solution)/shard_map/second/pallas_call | solution.py:387
  29.0 2.7 %collective-permute-start.9 = (f32[1024,256]{1,0:T(8,128)S(1)}, f32[1024,256]{1,0:T(8,128)S(1)}, u32[]{:S(2)}, u32[]{:S(2)}) collective-permute-start(f32[1024,256]{1,0:T(8,128)S(1)} %get-tuple-element.62), channel_id=1, source_target_pairs={{4,8},{8,4},{12,16},{16,12},{20,24},{24,20},{28,32},{32,28},{36,40... | collective-permute-start | bytes 3145736 | tf_op jit(solution)/shard_map/ppermute | solution.py:332
  31.8 1.0 collective-permute-start.8
  32.8 7.6 %second.3 = (f32[512,256]{1,0:T(8,128)S(1)}, f32[2,512,256]{2,1,0:T(8,128)S(1)}, f32[1024,256]{1,0:T(8,128)S(1)}) custom-call(f32[2,512,256]{2,1,0:T(8,128)S(1)} %get-tuple-element.45.d_in, f32[2,512,256]{2,1,0:T(8,128)S(1)} %get-tuple-element.46.c_in, bf16[2,4,256,512]{3,2,1,0:T(8,128)(2,1)S(1)} %get-tuple-element.47.g, ...), custom_call_target="tpu_custom_call" | custom-call | tf_op jit(solution)/shard_map/second/pallas_call | solution.py:389
  40.5 21.2 %collective-permute-start.5 = (f32[1024,256]{1,0:T(8,128)S(1)}, f32[1024,256]{1,0:T(8,128)S(1)}, u32[]{:S(2)}, u32[]{:S(2)}) collective-permute-start(f32[1024,256]{1,0:T(8,128)S(1)} %get-tuple-element.55), channel_id=1, source_target_pairs={{4,8},{8,4},{12,16},{16,12},{20,24},{24,20},{28,32},{32,28},{36,40... | collective-permute-start | bytes 3145736 | tf_op jit(solution)/shard_map/ppermute | solution.py:332
  61.6 24.6 %collective-permute-start.4 = (f32[1024,256]{1,0:T(8,128)S(1)}, f32[1024,256]{1,0:T(8,128)S(1)}, u32[]{:S(2)}, u32[]{:S(2)}) collective-permute-start(f32[1024,256]{1,0:T(8,128)S(1)} %get-tuple-element.55), channel_id=1, source_target_pairs={{0,4},{4,0},{8,12},{12,8},{16,20},{20,16},{24,28},{28,24},{32,36},... | collective-permute-start | bytes 3145736 | tf_op jit(solution)/shard_map/ppermute | solution.py:333
  86.3 7.5 %third.3 = (f32[512,256]{1,0:T(8,128)S(1)}, f32[2,512,256]{2,1,0:T(8,128)S(1)}, f32[1024,256]{1,0:T(8,128)S(1)}) custom-call(f32[512,256]{1,0:T(8,128)S(1)} %get-tuple-element.60.d_in, f32[2,512,256]{2,1,0:T(8,128)S(1)} %get-tuple-element.61.c_in, f32[1024,256]{1,0:T(8,128)S(1)} %collective-permute-done.8.even, f32[1024,256]{1,0:T(8,128)S(1)} %collective-permute-done.9.odd, ...), custom_call_target="tpu_custom_call" | custom-call | tf_op jit(solution)/shard_map/third/pallas_call | solution.py:401
  93.7 1.9 %collective-permute-start.11 = (f32[1024,256]{1,0:T(8,128)S(1)}, f32[1024,256]{1,0:T(8,128)S(1)}, u32[]{:S(2)}, u32[]{:S(2)}) collective-permute-start(f32[1024,256]{1,0:T(8,128)S(1)} %get-tuple-element.65), channel_id=1, source_target_pairs={{8,16},{16,8},{12,20},{20,12},{24,32},{32,24},{28,36},{36,28},{40,... | collective-permute-start | bytes 3145736 | tf_op jit(solution)/shard_map/ppermute | solution.py:332
  95.7 21.0 %collective-permute-start.10 = (f32[1024,256]{1,0:T(8,128)S(1)}, f32[1024,256]{1,0:T(8,128)S(1)}, u32[]{:S(2)}, u32[]{:S(2)}) collective-permute-start(f32[1024,256]{1,0:T(8,128)S(1)} %get-tuple-element.65), channel_id=1, source_target_pairs={{0,8},{8,0},{4,12},{12,4},{16,24},{24,16},{20,28},{28,20},{32,40},... | collective-permute-start | bytes 3145736 | tf_op jit(solution)/shard_map/ppermute | solution.py:333
  116.7 7.0 %third.2 = (f32[512,256]{1,0:T(8,128)S(1)}, f32[2,512,256]{2,1,0:T(8,128)S(1)}, f32[1024,256]{1,0:T(8,128)S(1)}) custom-call(f32[512,256]{1,0:T(8,128)S(1)} %get-tuple-element.51.d_in, f32[2,512,256]{2,1,0:T(8,128)S(1)} %get-tuple-element.52.c_in, f32[1024,256]{1,0:T(8,128)S(1)} %collective-permute-done.4.even, f32[1024,256]{1,0:T(8,128)S(1)} %collective-permute-done.5.odd, ...), custom_call_target="tpu_custom_call" | custom-call | tf_op jit(solution)/shard_map/third/pallas_call | solution.py:403
  123.7 1.9 %collective-permute-start.7 = (f32[512,256]{1,0:T(8,128)S(1)}, f32[512,256]{1,0:T(8,128)S(1)}, u32[]{:S(2)}, u32[]{:S(2)}) collective-permute-start(f32[512,256]{1,0:T(8,128)S(1)} %slice.27), channel_id=1, source_target_pairs={{8,16},{16,8},{12,20},{20,12},{24,32},{32,24},{28,36},{36,28},{40,... | collective-permute-start | bytes 1572872 | tf_op jit(solution)/shard_map/ppermute | solution.py:332
  125.6 2.7 %collective-permute-start.6 = (f32[512,256]{1,0:T(8,128)S(1)}, f32[512,256]{1,0:T(8,128)S(1)}, u32[]{:S(2)}, u32[]{:S(2)}) collective-permute-start(f32[512,256]{1,0:T(8,128)S(1)} %slice.27), channel_id=1, source_target_pairs={{0,8},{8,0},{4,12},{12,4},{16,24},{24,16},{20,28},{28,20},{32,40},... | collective-permute-start | bytes 1572872 | tf_op jit(solution)/shard_map/ppermute | solution.py:333
  128.4 1.9 %collective-permute-start.15 = (f32[512,128]{1,0:T(8,128)S(1)}, f32[512,128]{1,0:T(8,128)S(1)}, u32[]{:S(2)}, u32[]{:S(2)}) collective-permute-start(f32[512,128]{1,0:T(8,128)S(1)} %get-tuple-element.85), channel_id=1, source_target_pairs={{8,16},{16,8},{12,20},{20,12},{24,32},{32,24},{28,36},{36,28},{40,... | collective-permute-start | bytes 786440 | tf_op jit(solution)/shard_map/ppermute | solution.py:332
  130.3 10.1 %collective-permute-done.7.odd = f32[512,256]{1,0:T(8,128)S(1)} collective-permute-done((f32[512,256]{1,0:T(8,128)S(1)}, f32[512,256]{1,0:T(8,128)S(1)}, u32[]{:S(2)}, u32[]{:S(2)}) %collective-permute-start.7) | collective-permute-done | bytes 524320 | tf_op jit(solution)/shard_map/ppermute | solution.py:332
  140.4 11.2 %collective-permute-start.14 = (f32[512,128]{1,0:T(8,128)S(1)}, f32[512,128]{1,0:T(8,128)S(1)}, u32[]{:S(2)}, u32[]{:S(2)}) collective-permute-start(f32[512,128]{1,0:T(8,128)S(1)} %get-tuple-element.85), channel_id=1, source_target_pairs={{0,8},{8,0},{4,12},{12,4},{16,24},{24,16},{20,28},{28,20},{32,40},... | collective-permute-start | bytes 786440 | tf_op jit(solution)/shard_map/ppermute | solution.py:333
  151.6 1.9 %collective-permute-start.13 = (f32[512,128]{1,0:T(8,128)S(1)}, f32[512,128]{1,0:T(8,128)S(1)}, u32[]{:S(2)}, u32[]{:S(2)}) collective-permute-start(f32[512,128]{1,0:T(8,128)S(1)} %get-tuple-element.86), channel_id=1, source_target_pairs={{8,16},{16,8},{12,20},{20,12},{24,32},{32,24},{28,36},{36,28},{40,... | collective-permute-start | bytes 786440 | tf_op jit(solution)/shard_map/ppermute | solution.py:332
  153.5 4.2 %collective-permute-start.12 = (f32[512,128]{1,0:T(8,128)S(1)}, f32[512,128]{1,0:T(8,128)S(1)}, u32[]{:S(2)}, u32[]{:S(2)}) collective-permute-start(f32[512,128]{1,0:T(8,128)S(1)} %get-tuple-element.86), channel_id=1, source_target_pairs={{0,8},{8,0},{4,12},{12,4},{16,24},{24,16},{20,28},{28,20},{32,40},... | collective-permute-start | bytes 786440 | tf_op jit(solution)/shard_map/ppermute | solution.py:333
  157.8 2.0 %take_upper.2 = (f32[512,256]{1,0:T(8,128)S(1)}, f32[2,512,256]{2,1,0:T(8,128)}) custom-call(f32[512,256]{1,0:T(8,128)S(1)} %get-tuple-element.63.d_in, f32[2,512,256]{2,1,0:T(8,128)S(1)} %get-tuple-element.64.c_in, f32[512,256]{1,0:T(8,128)S(1)} %slice.36.even, f32[512,256]{1,0:T(8,128)S(1)} %slice.37.odd, ...), custom_call_target="tpu_custom_call", output_to_operand_aliasing={{1}: (5, {})} | custom-call | tf_op jit(solution)/shard_map/take_upper/pallas_call | solution.py:433
  159.9 2.0 %shard_map.67 = (f32[2,512,256]{2,1,0:T(8,128)}, f32[2,512,256]{2,1,0:T(8,128)}) custom-call(f32[512,256]{1,0:T(8,128)S(1)} %get-tuple-element.69.d_in, f32[2,512,256]{2,1,0:T(8,128)S(1)} %get-tuple-element.64.c_in, f32[512,128]{1,0:T(8,128)S(1)} %get-tuple-element.83.even, ...), custom_call_target="tpu_custom_call", output_to_operand_aliasing={{1}: (5, {}), {0}: (6, {})} | custom-call | tf_op jit(solution)/shard_map/pallas_call | solution.py:436
  161.9 2.0 %shard_map.68 = (f32[2,512,256]{2,1,0:T(8,128)}, f32[2,512,256]{2,1,0:T(8,128)}) custom-call(f32[512,256]{1,0:T(8,128)S(1)} %get-tuple-element.69.d_in, f32[2,512,256]{2,1,0:T(8,128)S(1)} %get-tuple-element.64.c_in, f32[512,128]{1,0:T(8,128)S(1)} %get-tuple-element.84.even, ...), custom_call_target="tpu_custom_call", output_to_operand_aliasing={{1}: (5, {}), {0}: (6, {})} | custom-call | tf_op jit(solution)/shard_map/pallas_call | solution.py:436
  163.9 2.0 %take_upper.3 = (f32[512,256]{1,0:T(8,128)S(1)}, f32[2,512,256]{2,1,0:T(8,128)}) custom-call(f32[512,256]{1,0:T(8,128)S(1)} %get-tuple-element.56.d_in, f32[2,512,256]{2,1,0:T(8,128)S(1)} %get-tuple-element.57.c_in, f32[512,256]{1,0:T(8,128)S(1)} %collective-permute-done.6.even, ...), custom_call_target="tpu_custom_call", output_to_operand_aliasing={{1}: (5, {})} | custom-call | tf_op jit(solution)/shard_map/take_upper/pallas_call | solution.py:437
  166.0 2.0 %shard_map.69 = (f32[2,512,256]{2,1,0:T(8,128)}, f32[2,512,256]{2,1,0:T(8,128)}) custom-call(f32[512,256]{1,0:T(8,128)S(1)} %get-tuple-element.68.d_in, f32[2,512,256]{2,1,0:T(8,128)S(1)} %get-tuple-element.57.c_in, f32[512,128]{1,0:T(8,128)S(1)} %collective-permute-done.14.even, ...), custom_call_target="tpu_custom_call", output_to_operand_aliasing={{1}: (5, {}), {0}: (6, {})} | custom-call | tf_op jit(solution)/shard_map/pallas_call | solution.py:439
  168.0 2.0 %shard_map.70 = (f32[2,512,256]{2,1,0:T(8,128)}, f32[2,512,256]{2,1,0:T(8,128)}) custom-call(f32[512,256]{1,0:T(8,128)S(1)} %get-tuple-element.68.d_in, f32[2,512,256]{2,1,0:T(8,128)S(1)} %get-tuple-element.57.c_in, f32[512,128]{1,0:T(8,128)S(1)} %collective-permute-done.12.even, ...), custom_call_target="tpu_custom_call", output_to_operand_aliasing={{1}: (5, {}), {0}: (6, {})} | custom-call | tf_op jit(solution)/shard_map/pallas_call | solution.py:439
  (25 shorter events, 0.5 us)
Async XLA Ops:
  0.6 16.3 %collective-permute-start.1 = (f32[2,512,256]{2,1,0:T(8,128)}, f32[2,512,256]{2,1,0:T(8,128)S(1)}, u32[]{:S(2)}, u32[]{:S(2)}) collective-permute-start(f32[2,512,256]{2,1,0:T(8,128)} %bitcast.11), channel_id=1, source_target_pairs={{4,8},{8,4},{12,16},{16,12},{20,24},{24,20},{28,32},{32,28},{36,40... | collective-permute-start | bytes 3145736 | tf_op jit(solution)/shard_map/ppermute | solution.py:332
  2.6 14.4 %collective-permute-start = (f32[2,512,256]{2,1,0:T(8,128)}, f32[2,512,256]{2,1,0:T(8,128)S(1)}, u32[]{:S(2)}, u32[]{:S(2)}) collective-permute-start(f32[2,512,256]{2,1,0:T(8,128)} %bitcast.12), channel_id=1, source_target_pairs={{0,4},{4,0},{8,12},{12,8},{16,20},{20,16},{24,28},{28,24},{32,36},... | collective-permute-start | bytes 3145736 | tf_op jit(solution)/shard_map/ppermute | solution.py:333
  5.5 1.2 copy-start
  13.5 8.1 %collective-permute-start.2 = (f32[512,256]{1,0:T(8,128)S(1)}, f32[512,256]{1,0:T(8,128)S(1)}, u32[]{:S(2)}, u32[]{:S(2)}) collective-permute-start(f32[512,256]{1,0:T(8,128)S(1)} %get-tuple-element.48), channel_id=1, source_target_pairs={{0,4},{4,0},{8,12},{12,8},{16,20},{20,16},{24,28},{28,24},{32,36},... | collective-permute-start | bytes 1572872 | tf_op jit(solution)/shard_map/ppermute | solution.py:333
  13.6 19.2 %collective-permute-start.3 = (f32[512,256]{1,0:T(8,128)S(1)}, f32[512,256]{1,0:T(8,128)S(1)}, u32[]{:S(2)}, u32[]{:S(2)}) collective-permute-start(f32[512,256]{1,0:T(8,128)S(1)} %get-tuple-element.53), channel_id=1, source_target_pairs={{4,8},{8,4},{12,16},{16,12},{20,24},{24,20},{28,32},{32,28},{36,40... | collective-permute-start | bytes 1572872 | tf_op jit(solution)/shard_map/ppermute | solution.py:332
  17.0 1.2 copy-start.1
  29.0 57.3 %collective-permute-start.9 = (f32[1024,256]{1,0:T(8,128)S(1)}, f32[1024,256]{1,0:T(8,128)S(1)}, u32[]{:S(2)}, u32[]{:S(2)}) collective-permute-start(f32[1024,256]{1,0:T(8,128)S(1)} %get-tuple-element.62), channel_id=1, source_target_pairs={{4,8},{8,4},{12,16},{16,12},{20,24},{24,20},{28,32},{32,28},{36,40... | collective-permute-start | bytes 3145736 | tf_op jit(solution)/shard_map/ppermute | solution.py:332
  31.8 54.5 %collective-permute-start.8 = (f32[1024,256]{1,0:T(8,128)S(1)}, f32[1024,256]{1,0:T(8,128)S(1)}, u32[]{:S(2)}, u32[]{:S(2)}) collective-permute-start(f32[1024,256]{1,0:T(8,128)S(1)} %get-tuple-element.62), channel_id=1, source_target_pairs={{0,4},{4,0},{8,12},{12,8},{16,20},{20,16},{24,28},{28,24},{32,36},... | collective-permute-start | bytes 3145736 | tf_op jit(solution)/shard_map/ppermute | solution.py:333
  40.5 76.2 %collective-permute-start.5 = (f32[1024,256]{1,0:T(8,128)S(1)}, f32[1024,256]{1,0:T(8,128)S(1)}, u32[]{:S(2)}, u32[]{:S(2)}) collective-permute-start(f32[1024,256]{1,0:T(8,128)S(1)} %get-tuple-element.55), channel_id=1, source_target_pairs={{4,8},{8,4},{12,16},{16,12},{20,24},{24,20},{28,32},{32,28},{36,40... | collective-permute-start | bytes 3145736 | tf_op jit(solution)/shard_map/ppermute | solution.py:332
  61.6 55.0 %collective-permute-start.4 = (f32[1024,256]{1,0:T(8,128)S(1)}, f32[1024,256]{1,0:T(8,128)S(1)}, u32[]{:S(2)}, u32[]{:S(2)}) collective-permute-start(f32[1024,256]{1,0:T(8,128)S(1)} %get-tuple-element.55), channel_id=1, source_target_pairs={{0,4},{4,0},{8,12},{12,8},{16,20},{20,16},{24,28},{28,24},{32,36},... | collective-permute-start | bytes 3145736 | tf_op jit(solution)/shard_map/ppermute | solution.py:333
  93.7 57.8 %collective-permute-start.11 = (f32[1024,256]{1,0:T(8,128)S(1)}, f32[1024,256]{1,0:T(8,128)S(1)}, u32[]{:S(2)}, u32[]{:S(2)}) collective-permute-start(f32[1024,256]{1,0:T(8,128)S(1)} %get-tuple-element.65), channel_id=1, source_target_pairs={{8,16},{16,8},{12,20},{20,12},{24,32},{32,24},{28,36},{36,28},{40,... | collective-permute-start | bytes 3145736 | tf_op jit(solution)/shard_map/ppermute | solution.py:332
  95.7 57.8 %collective-permute-start.10 = (f32[1024,256]{1,0:T(8,128)S(1)}, f32[1024,256]{1,0:T(8,128)S(1)}, u32[]{:S(2)}, u32[]{:S(2)}) collective-permute-start(f32[1024,256]{1,0:T(8,128)S(1)} %get-tuple-element.65), channel_id=1, source_target_pairs={{0,8},{8,0},{4,12},{12,4},{16,24},{24,16},{20,28},{28,20},{32,40},... | collective-permute-start | bytes 3145736 | tf_op jit(solution)/shard_map/ppermute | solution.py:333
  123.7 16.7 %collective-permute-start.7 = (f32[512,256]{1,0:T(8,128)S(1)}, f32[512,256]{1,0:T(8,128)S(1)}, u32[]{:S(2)}, u32[]{:S(2)}) collective-permute-start(f32[512,256]{1,0:T(8,128)S(1)} %slice.27), channel_id=1, source_target_pairs={{8,16},{16,8},{12,20},{20,12},{24,32},{32,24},{28,36},{36,28},{40,... | collective-permute-start | bytes 1572872 | tf_op jit(solution)/shard_map/ppermute | solution.py:332
  125.6 38.3 %collective-permute-start.6 = (f32[512,256]{1,0:T(8,128)S(1)}, f32[512,256]{1,0:T(8,128)S(1)}, u32[]{:S(2)}, u32[]{:S(2)}) collective-permute-start(f32[512,256]{1,0:T(8,128)S(1)} %slice.27), channel_id=1, source_target_pairs={{0,8},{8,0},{4,12},{12,4},{16,24},{24,16},{20,28},{28,20},{32,40},... | collective-permute-start | bytes 1572872 | tf_op jit(solution)/shard_map/ppermute | solution.py:333
  128.4 37.6 %collective-permute-start.15 = (f32[512,128]{1,0:T(8,128)S(1)}, f32[512,128]{1,0:T(8,128)S(1)}, u32[]{:S(2)}, u32[]{:S(2)}) collective-permute-start(f32[512,128]{1,0:T(8,128)S(1)} %get-tuple-element.85), channel_id=1, source_target_pairs={{8,16},{16,8},{12,20},{20,12},{24,32},{32,24},{28,36},{36,28},{40,... | collective-permute-start | bytes 786440 | tf_op jit(solution)/shard_map/ppermute | solution.py:332
  140.4 25.6 %collective-permute-start.14 = (f32[512,128]{1,0:T(8,128)S(1)}, f32[512,128]{1,0:T(8,128)S(1)}, u32[]{:S(2)}, u32[]{:S(2)}) collective-permute-start(f32[512,128]{1,0:T(8,128)S(1)} %get-tuple-element.85), channel_id=1, source_target_pairs={{0,8},{8,0},{4,12},{12,4},{16,24},{24,16},{20,28},{28,20},{32,40},... | collective-permute-start | bytes 786440 | tf_op jit(solution)/shard_map/ppermute | solution.py:333
  151.6 16.4 %collective-permute-start.13 = (f32[512,128]{1,0:T(8,128)S(1)}, f32[512,128]{1,0:T(8,128)S(1)}, u32[]{:S(2)}, u32[]{:S(2)}) collective-permute-start(f32[512,128]{1,0:T(8,128)S(1)} %get-tuple-element.86), channel_id=1, source_target_pairs={{8,16},{16,8},{12,20},{20,12},{24,32},{32,24},{28,36},{36,28},{40,... | collective-permute-start | bytes 786440 | tf_op jit(solution)/shard_map/ppermute | solution.py:332
  153.5 14.5 %collective-permute-start.12 = (f32[512,128]{1,0:T(8,128)S(1)}, f32[512,128]{1,0:T(8,128)S(1)}, u32[]{:S(2)}, u32[]{:S(2)}) collective-permute-start(f32[512,128]{1,0:T(8,128)S(1)} %get-tuple-element.86), channel_id=1, source_target_pairs={{0,8},{8,0},{4,12},{12,4},{16,24},{24,16},{20,28},{28,20},{32,40},... | collective-permute-start | bytes 786440 | tf_op jit(solution)/shard_map/ppermute | solution.py:333

commit v6 on v5

--- a/solution.py
+++ b/solution.py
@@ -227,12 +227,15 @@
     return 1 - parity, parity
 
 
-def first_kernel(onsite, scalars, ints, z_even, z_odd, z_own, *work):
+def first_kernel(onsite, hop, scalars, ints, z_even, z_odd, z_own, hop_own, sem, *work):
+    beside = pltpu.make_async_copy(hop, hop_own, sem)
+    beside.start()
     invert([initial(row(onsite[i]), scalars) for i in range(2)], scalars[1], work)
     for i in range(2):
         put(z_own.at[i], work[0][i])
     put(z_even, work[0][1 - ints[0]])
     put(z_odd, work[0][ints[0]])
+    beside.wait()
 
 
 def near_kernel(
@@ -353,15 +356,15 @@
 
     hop_even, hop_odd = swaps(hop, 1)
     block, pair, two = shape(2 * w, w), shape(4 * w, w), shape(2, 2 * w, w)
-    z_even, z_odd, z_own = pl.pallas_call(
+    z_even, z_odd, z_own, hop_own = pl.pallas_call(
         first_kernel,
-        out_shape=(block, block, two),
-        in_specs=[VMEM, SMEM, SMEM],
-        out_specs=(VMEM,) * 3,
-        scratch_shapes=work(rows, w),
+        out_shape=(block, block, two, two),
+        in_specs=[VMEM, pl.BlockSpec(memory_space=pl.ANY), SMEM, SMEM],
+        out_specs=(VMEM,) * 4,
+        scratch_shapes=[pltpu.SemaphoreType.DMA] + work(rows, w),
         compiler_params=PARAMS,
         name="first",
-    )(onsite, scalars, at_a)
+    )(onsite, pltpu.with_memory_space_constraint(hop, pltpu.HBM), scalars, at_a)
     from_even, from_odd = swaps(z_even, 1, z_odd)
     kept = pl.BlockSpec(memory_space=pl.ANY)
     gain = jax.ShapeDtypeStruct((2, 4, w, 2 * w), BF)
@@ -372,7 +375,7 @@
         out_specs=(VMEM,) * 4 + (kept,) * 3,
         compiler_params=PARAMS,
         name="near",
-    )(onsite, hop, hop_even, hop_odd, z_own, scalars, at_a)
+    )(onsite, hop_own, hop_even, hop_odd, z_own, scalars, at_a)
     whole = two
 
     second = pl.pallas_call(

time: 171 us -> 169 us (0.988)
  no operation moved by 1% of the time
where the time goes in v6:
time: 169 us
  starting transfers between devices  103 us (61%)
  Pallas kernels  51.8 us (31%)
  waiting for transfers between devices  10.6 us (6%)
  between operations  2.36 us (1%)
    ppermute x8, starting transfers between devices, swaps(): from_even = lax.ppermute(x, 'slab', even)  66.2 us
    ppermute x8, starting transfers between devices, swaps(): from_odd = lax.ppermute(x if for_odd is None else for_odd, 'slab', odd)  36.3 us
    ppermute x8, waiting for transfers between devices, swaps(): from_odd = lax.ppermute(x if for_odd is None else for_odd, 'slab', odd)  10.6 us
    pallas_call x1, Pallas kernels, reduce_levels(): second(d_near, c_near, g_near, from_odd, k_near, scalars, run_b)  7.64 us
    pallas_call x1, Pallas kernels, reduce_levels(): d_a, c_a, p_a = third(d_a, c_a, even_a, odd_a, scalars, at_a)  7.46 us
    pallas_call x1, Pallas kernels, reduce_levels(): second(d_near, c_near, g_near, from_even, k_near, scalars, run_a)  7.33 us
    pallas_call x1, Pallas kernels, reduce_levels(): d_b, c_b, p_b = third(d_b, c_b, even_b, odd_b, scalars, at_a)  6.99 us
    pallas_call x1, Pallas kernels, reduce_levels(): pl.pallas_call(first_kernel, out_shape=(block, block, two, two), in_specs...  6.84 us
  transfers between devices with their start and end apart: 16, of which 2 were waited for; matrix products, arithmetic and copies ran while one was open for 0% of the time, Pallas kernels for 29%

profile of v6, /device:TPU:60, one launch (start us, length us, event | category | flops | bytes accessed | tf_op | source)
XLA Modules:
  0.0 169.0 jit_solution(9228002824559310924)
XLA Ops:
  0.6 1.9 %collective-permute-start.1 = (f32[2,512,256]{2,1,0:T(8,128)}, f32[2,512,256]{2,1,0:T(8,128)S(1)}, u32[]{:S(2)}, u32[]{:S(2)}) collective-permute-start(f32[2,512,256]{2,1,0:T(8,128)} %bitcast.14), channel_id=1, source_target_pairs={{4,8},{8,4},{12,16},{16,12},{20,24},{24,20},{28,32},{32,28},{36,40... | collective-permute-start | bytes 3145736 | tf_op jit(solution)/shard_map/ppermute | solution.py:335
  2.6 1.4 collective-permute-start
  5.2 0.1 pad_maximum_fusion.scalars
  5.5 1.2 copy-done
  6.7 6.8 %first.1 = (f32[512,256]{1,0:T(8,128)S(1)}, f32[512,256]{1,0:T(8,128)S(1)}, f32[2,512,256]{2,1,0:T(8,128)S(1)}, f32[2,512,256]{2,1,0:T(8,128)S(1)}) custom-call(f32[2,512,256]{2,1,0:T(8,128)S(1)} %bitcast.9, f32[2,512,256]{2,1,0:T(8,128)} %bitcast.16, f32[3]{0:T(128)S(1)} %pad_maximum_fusion.scalars, s32[3]{0:T(128)S(1)} %get-tuple-element.44.ints.parity), custom_call_target="tpu_custom_call" | custom-call | tf_op jit(solution)/shard_map/first/pallas_call | solution.py:359
  13.5 0.1 collective-permute-start.2
  13.6 2.8 %collective-permute-start.3 = (f32[512,256]{1,0:T(8,128)S(1)}, f32[512,256]{1,0:T(8,128)S(1)}, u32[]{:S(2)}, u32[]{:S(2)}) collective-permute-start(f32[512,256]{1,0:T(8,128)S(1)} %get-tuple-element.55), channel_id=1, source_target_pairs={{4,8},{8,4},{12,16},{16,12},{20,24},{24,20},{28,32},{32,28},{36,40... | collective-permute-start | bytes 1572872 | tf_op jit(solution)/shard_map/ppermute | solution.py:335
  16.5 0.5 collective-permute-done.1.hop_odd
  17.0 3.5 %near.1 = (f32[2,512,256]{2,1,0:T(8,128)S(1)}, f32[2,512,256]{2,1,0:T(8,128)S(1)}, bf16[2,4,256,512]{3,2,1,0:T(8,128)(2,1)S(1)}, f32[2,512,256]{2,1,0:T(8,128)S(...) custom-call(f32[2,512,256]{2,1,0:T(8,128)S(1)} %bitcast.10, ...), custom_call_target="tpu_custom_call" | custom-call | tf_op jit(solution)/shard_map/near/pallas_call | solution.py:371
  20.5 7.3 %second.2 = (f32[512,256]{1,0:T(8,128)S(1)}, f32[2,512,256]{2,1,0:T(8,128)S(1)}, f32[1024,256]{1,0:T(8,128)S(1)}) custom-call(f32[2,512,256]{2,1,0:T(8,128)S(1)} %get-tuple-element.47.d_in, f32[2,512,256]{2,1,0:T(8,128)S(1)} %get-tuple-element.48.c_in, bf16[2,4,256,512]{3,2,1,0:T(8,128)(2,1)S(1)} %get-tuple-element.49.g, ...), custom_call_target="tpu_custom_call" | custom-call | tf_op jit(solution)/shard_map/second/pallas_call | solution.py:390
  27.8 2.7 %collective-permute-start.9 = (f32[1024,256]{1,0:T(8,128)S(1)}, f32[1024,256]{1,0:T(8,128)S(1)}, u32[]{:S(2)}, u32[]{:S(2)}) collective-permute-start(f32[1024,256]{1,0:T(8,128)S(1)} %get-tuple-element.64), channel_id=1, source_target_pairs={{4,8},{8,4},{12,16},{16,12},{20,24},{24,20},{28,32},{32,28},{36,40... | collective-permute-start | bytes 3145736 | tf_op jit(solution)/shard_map/ppermute | solution.py:335
  30.5 1.0 collective-permute-start.8
  31.6 7.6 %second.3 = (f32[512,256]{1,0:T(8,128)S(1)}, f32[2,512,256]{2,1,0:T(8,128)S(1)}, f32[1024,256]{1,0:T(8,128)S(1)}) custom-call(f32[2,512,256]{2,1,0:T(8,128)S(1)} %get-tuple-element.47.d_in, f32[2,512,256]{2,1,0:T(8,128)S(1)} %get-tuple-element.48.c_in, bf16[2,4,256,512]{3,2,1,0:T(8,128)(2,1)S(1)} %get-tuple-element.49.g, ...), custom_call_target="tpu_custom_call" | custom-call | tf_op jit(solution)/shard_map/second/pallas_call | solution.py:392
  39.2 21.2 %collective-permute-start.5 = (f32[1024,256]{1,0:T(8,128)S(1)}, f32[1024,256]{1,0:T(8,128)S(1)}, u32[]{:S(2)}, u32[]{:S(2)}) collective-permute-start(f32[1024,256]{1,0:T(8,128)S(1)} %get-tuple-element.57), channel_id=1, source_target_pairs={{4,8},{8,4},{12,16},{16,12},{20,24},{24,20},{28,32},{32,28},{36,40... | collective-permute-start | bytes 3145736 | tf_op jit(solution)/shard_map/ppermute | solution.py:335
  60.4 24.6 %collective-permute-start.4 = (f32[1024,256]{1,0:T(8,128)S(1)}, f32[1024,256]{1,0:T(8,128)S(1)}, u32[]{:S(2)}, u32[]{:S(2)}) collective-permute-start(f32[1024,256]{1,0:T(8,128)S(1)} %get-tuple-element.57), channel_id=1, source_target_pairs={{0,4},{4,0},{8,12},{12,8},{16,20},{20,16},{24,28},{28,24},{32,36},... | collective-permute-start | bytes 3145736 | tf_op jit(solution)/shard_map/ppermute | solution.py:336
  85.0 7.5 %third.3 = (f32[512,256]{1,0:T(8,128)S(1)}, f32[2,512,256]{2,1,0:T(8,128)S(1)}, f32[1024,256]{1,0:T(8,128)S(1)}) custom-call(f32[512,256]{1,0:T(8,128)S(1)} %get-tuple-element.62.d_in, f32[2,512,256]{2,1,0:T(8,128)S(1)} %get-tuple-element.63.c_in, f32[1024,256]{1,0:T(8,128)S(1)} %collective-permute-done.8.even, f32[1024,256]{1,0:T(8,128)S(1)} %collective-permute-done.9.odd, ...), custom_call_target="tpu_custom_call" | custom-call | tf_op jit(solution)/shard_map/third/pallas_call | solution.py:404
  92.5 1.9 %collective-permute-start.11 = (f32[1024,256]{1,0:T(8,128)S(1)}, f32[1024,256]{1,0:T(8,128)S(1)}, u32[]{:S(2)}, u32[]{:S(2)}) collective-permute-start(f32[1024,256]{1,0:T(8,128)S(1)} %get-tuple-element.67), channel_id=1, source_target_pairs={{8,16},{16,8},{12,20},{20,12},{24,32},{32,24},{28,36},{36,28},{40,... | collective-permute-start | bytes 3145736 | tf_op jit(solution)/shard_map/ppermute | solution.py:335
  94.4 21.0 %collective-permute-start.10 = (f32[1024,256]{1,0:T(8,128)S(1)}, f32[1024,256]{1,0:T(8,128)S(1)}, u32[]{:S(2)}, u32[]{:S(2)}) collective-permute-start(f32[1024,256]{1,0:T(8,128)S(1)} %get-tuple-element.67), channel_id=1, source_target_pairs={{0,8},{8,0},{4,12},{12,4},{16,24},{24,16},{20,28},{28,20},{32,40},... | collective-permute-start | bytes 3145736 | tf_op jit(solution)/shard_map/ppermute | solution.py:336
  115.4 7.0 %third.2 = (f32[512,256]{1,0:T(8,128)S(1)}, f32[2,512,256]{2,1,0:T(8,128)S(1)}, f32[1024,256]{1,0:T(8,128)S(1)}) custom-call(f32[512,256]{1,0:T(8,128)S(1)} %get-tuple-element.53.d_in, f32[2,512,256]{2,1,0:T(8,128)S(1)} %get-tuple-element.54.c_in, f32[1024,256]{1,0:T(8,128)S(1)} %collective-permute-done.4.even, f32[1024,256]{1,0:T(8,128)S(1)} %collective-permute-done.5.odd, ...), custom_call_target="tpu_custom_call" | custom-call | tf_op jit(solution)/shard_map/third/pallas_call | solution.py:406
  122.5 1.9 %collective-permute-start.7 = (f32[512,256]{1,0:T(8,128)S(1)}, f32[512,256]{1,0:T(8,128)S(1)}, u32[]{:S(2)}, u32[]{:S(2)}) collective-permute-start(f32[512,256]{1,0:T(8,128)S(1)} %slice.27), channel_id=1, source_target_pairs={{8,16},{16,8},{12,20},{20,12},{24,32},{32,24},{28,36},{36,28},{40,... | collective-permute-start | bytes 1572872 | tf_op jit(solution)/shard_map/ppermute | solution.py:335
  124.4 2.7 %collective-permute-start.6 = (f32[512,256]{1,0:T(8,128)S(1)}, f32[512,256]{1,0:T(8,128)S(1)}, u32[]{:S(2)}, u32[]{:S(2)}) collective-permute-start(f32[512,256]{1,0:T(8,128)S(1)} %slice.27), channel_id=1, source_target_pairs={{0,8},{8,0},{4,12},{12,4},{16,24},{24,16},{20,28},{28,20},{32,40},... | collective-permute-start | bytes 1572872 | tf_op jit(solution)/shard_map/ppermute | solution.py:336
  127.1 1.9 %collective-permute-start.15 = (f32[512,128]{1,0:T(8,128)S(1)}, f32[512,128]{1,0:T(8,128)S(1)}, u32[]{:S(2)}, u32[]{:S(2)}) collective-permute-start(f32[512,128]{1,0:T(8,128)S(1)} %get-tuple-element.87), channel_id=1, source_target_pairs={{8,16},{16,8},{12,20},{20,12},{24,32},{32,24},{28,36},{36,28},{40,... | collective-permute-start | bytes 786440 | tf_op jit(solution)/shard_map/ppermute | solution.py:335
  129.1 10.1 %collective-permute-done.7.odd = f32[512,256]{1,0:T(8,128)S(1)} collective-permute-done((f32[512,256]{1,0:T(8,128)S(1)}, f32[512,256]{1,0:T(8,128)S(1)}, u32[]{:S(2)}, u32[]{:S(2)}) %collective-permute-start.7) | collective-permute-done | bytes 524320 | tf_op jit(solution)/shard_map/ppermute | solution.py:335
  139.2 11.2 %collective-permute-start.14 = (f32[512,128]{1,0:T(8,128)S(1)}, f32[512,128]{1,0:T(8,128)S(1)}, u32[]{:S(2)}, u32[]{:S(2)}) collective-permute-start(f32[512,128]{1,0:T(8,128)S(1)} %get-tuple-element.87), channel_id=1, source_target_pairs={{0,8},{8,0},{4,12},{12,4},{16,24},{24,16},{20,28},{28,20},{32,40},... | collective-permute-start | bytes 786440 | tf_op jit(solution)/shard_map/ppermute | solution.py:336
  150.4 1.9 %collective-permute-start.13 = (f32[512,128]{1,0:T(8,128)S(1)}, f32[512,128]{1,0:T(8,128)S(1)}, u32[]{:S(2)}, u32[]{:S(2)}) collective-permute-start(f32[512,128]{1,0:T(8,128)S(1)} %get-tuple-element.88), channel_id=1, source_target_pairs={{8,16},{16,8},{12,20},{20,12},{24,32},{32,24},{28,36},{36,28},{40,... | collective-permute-start | bytes 786440 | tf_op jit(solution)/shard_map/ppermute | solution.py:335
  152.3 4.2 %collective-permute-start.12 = (f32[512,128]{1,0:T(8,128)S(1)}, f32[512,128]{1,0:T(8,128)S(1)}, u32[]{:S(2)}, u32[]{:S(2)}) collective-permute-start(f32[512,128]{1,0:T(8,128)S(1)} %get-tuple-element.88), channel_id=1, source_target_pairs={{0,8},{8,0},{4,12},{12,4},{16,24},{24,16},{20,28},{28,20},{32,40},... | collective-permute-start | bytes 786440 | tf_op jit(solution)/shard_map/ppermute | solution.py:336
  156.6 2.0 %take_upper.2 = (f32[512,256]{1,0:T(8,128)S(1)}, f32[2,512,256]{2,1,0:T(8,128)}) custom-call(f32[512,256]{1,0:T(8,128)S(1)} %get-tuple-element.65.d_in, f32[2,512,256]{2,1,0:T(8,128)S(1)} %get-tuple-element.66.c_in, f32[512,256]{1,0:T(8,128)S(1)} %slice.36.even, f32[512,256]{1,0:T(8,128)S(1)} %slice.37.odd, ...), custom_call_target="tpu_custom_call", output_to_operand_aliasing={{1}: (5, {})} | custom-call | tf_op jit(solution)/shard_map/take_upper/pallas_call | solution.py:436
  158.7 2.0 %shard_map.67 = (f32[2,512,256]{2,1,0:T(8,128)}, f32[2,512,256]{2,1,0:T(8,128)}) custom-call(f32[512,256]{1,0:T(8,128)S(1)} %get-tuple-element.71.d_in, f32[2,512,256]{2,1,0:T(8,128)S(1)} %get-tuple-element.66.c_in, f32[512,128]{1,0:T(8,128)S(1)} %get-tuple-element.85.even, ...), custom_call_target="tpu_custom_call", output_to_operand_aliasing={{1}: (5, {}), {0}: (6, {})} | custom-call | tf_op jit(solution)/shard_map/pallas_call | solution.py:439
  160.7 2.0 %shard_map.68 = (f32[2,512,256]{2,1,0:T(8,128)}, f32[2,512,256]{2,1,0:T(8,128)}) custom-call(f32[512,256]{1,0:T(8,128)S(1)} %get-tuple-element.71.d_in, f32[2,512,256]{2,1,0:T(8,128)S(1)} %get-tuple-element.66.c_in, f32[512,128]{1,0:T(8,128)S(1)} %get-tuple-element.86.even, ...), custom_call_target="tpu_custom_call", output_to_operand_aliasing={{1}: (5, {}), {0}: (6, {})} | custom-call | tf_op jit(solution)/shard_map/pallas_call | solution.py:439
  162.7 2.0 %take_upper.3 = (f32[512,256]{1,0:T(8,128)S(1)}, f32[2,512,256]{2,1,0:T(8,128)}) custom-call(f32[512,256]{1,0:T(8,128)S(1)} %get-tuple-element.58.d_in, f32[2,512,256]{2,1,0:T(8,128)S(1)} %get-tuple-element.59.c_in, f32[512,256]{1,0:T(8,128)S(1)} %collective-permute-done.6.even, ...), custom_call_target="tpu_custom_call", output_to_operand_aliasing={{1}: (5, {})} | custom-call | tf_op jit(solution)/shard_map/take_upper/pallas_call | solution.py:440
  164.8 2.0 %shard_map.69 = (f32[2,512,256]{2,1,0:T(8,128)}, f32[2,512,256]{2,1,0:T(8,128)}) custom-call(f32[512,256]{1,0:T(8,128)S(1)} %get-tuple-element.70.d_in, f32[2,512,256]{2,1,0:T(8,128)S(1)} %get-tuple-element.59.c_in, f32[512,128]{1,0:T(8,128)S(1)} %collective-permute-done.14.even, ...), custom_call_target="tpu_custom_call", output_to_operand_aliasing={{1}: (5, {}), {0}: (6, {})} | custom-call | tf_op jit(solution)/shard_map/pallas_call | solution.py:442
  166.8 2.0 %shard_map.70 = (f32[2,512,256]{2,1,0:T(8,128)}, f32[2,512,256]{2,1,0:T(8,128)}) custom-call(f32[512,256]{1,0:T(8,128)S(1)} %get-tuple-element.70.d_in, f32[2,512,256]{2,1,0:T(8,128)S(1)} %get-tuple-element.59.c_in, f32[512,128]{1,0:T(8,128)S(1)} %collective-permute-done.12.even, ...), custom_call_target="tpu_custom_call", output_to_operand_aliasing={{1}: (5, {}), {0}: (6, {})} | custom-call | tf_op jit(solution)/shard_map/pallas_call | solution.py:442
  (23 shorter events, 0.4 us)
Async XLA Ops:
  0.6 16.3 %collective-permute-start.1 = (f32[2,512,256]{2,1,0:T(8,128)}, f32[2,512,256]{2,1,0:T(8,128)S(1)}, u32[]{:S(2)}, u32[]{:S(2)}) collective-permute-start(f32[2,512,256]{2,1,0:T(8,128)} %bitcast.14), channel_id=1, source_target_pairs={{4,8},{8,4},{12,16},{16,12},{20,24},{24,20},{28,32},{32,28},{36,40... | collective-permute-start | bytes 3145736 | tf_op jit(solution)/shard_map/ppermute | solution.py:335
  2.6 14.4 %collective-permute-start = (f32[2,512,256]{2,1,0:T(8,128)}, f32[2,512,256]{2,1,0:T(8,128)S(1)}, u32[]{:S(2)}, u32[]{:S(2)}) collective-permute-start(f32[2,512,256]{2,1,0:T(8,128)} %bitcast.15), channel_id=1, source_target_pairs={{0,4},{4,0},{8,12},{12,8},{16,20},{20,16},{24,28},{28,24},{32,36},... | collective-permute-start | bytes 3145736 | tf_op jit(solution)/shard_map/ppermute | solution.py:336
  5.5 1.2 copy-start
  13.5 6.9 %collective-permute-start.2 = (f32[512,256]{1,0:T(8,128)S(1)}, f32[512,256]{1,0:T(8,128)S(1)}, u32[]{:S(2)}, u32[]{:S(2)}) collective-permute-start(f32[512,256]{1,0:T(8,128)S(1)} %get-tuple-element.50), channel_id=1, source_target_pairs={{0,4},{4,0},{8,12},{12,8},{16,20},{20,16},{24,28},{28,24},{32,36},... | collective-permute-start | bytes 1572872 | tf_op jit(solution)/shard_map/ppermute | solution.py:336
  13.6 17.9 %collective-permute-start.3 = (f32[512,256]{1,0:T(8,128)S(1)}, f32[512,256]{1,0:T(8,128)S(1)}, u32[]{:S(2)}, u32[]{:S(2)}) collective-permute-start(f32[512,256]{1,0:T(8,128)S(1)} %get-tuple-element.55), channel_id=1, source_target_pairs={{4,8},{8,4},{12,16},{16,12},{20,24},{24,20},{28,32},{32,28},{36,40... | collective-permute-start | bytes 1572872 | tf_op jit(solution)/shard_map/ppermute | solution.py:335
  27.8 57.2 %collective-permute-start.9 = (f32[1024,256]{1,0:T(8,128)S(1)}, f32[1024,256]{1,0:T(8,128)S(1)}, u32[]{:S(2)}, u32[]{:S(2)}) collective-permute-start(f32[1024,256]{1,0:T(8,128)S(1)} %get-tuple-element.64), channel_id=1, source_target_pairs={{4,8},{8,4},{12,16},{16,12},{20,24},{24,20},{28,32},{32,28},{36,40... | collective-permute-start | bytes 3145736 | tf_op jit(solution)/shard_map/ppermute | solution.py:335
  30.5 54.5 %collective-permute-start.8 = (f32[1024,256]{1,0:T(8,128)S(1)}, f32[1024,256]{1,0:T(8,128)S(1)}, u32[]{:S(2)}, u32[]{:S(2)}) collective-permute-start(f32[1024,256]{1,0:T(8,128)S(1)} %get-tuple-element.64), channel_id=1, source_target_pairs={{0,4},{4,0},{8,12},{12,8},{16,20},{20,16},{24,28},{28,24},{32,36},... | collective-permute-start | bytes 3145736 | tf_op jit(solution)/shard_map/ppermute | solution.py:336
  39.2 76.2 %collective-permute-start.5 = (f32[1024,256]{1,0:T(8,128)S(1)}, f32[1024,256]{1,0:T(8,128)S(1)}, u32[]{:S(2)}, u32[]{:S(2)}) collective-permute-start(f32[1024,256]{1,0:T(8,128)S(1)} %get-tuple-element.57), channel_id=1, source_target_pairs={{4,8},{8,4},{12,16},{16,12},{20,24},{24,20},{28,32},{32,28},{36,40... | collective-permute-start | bytes 3145736 | tf_op jit(solution)/shard_map/ppermute | solution.py:335
  60.4 55.0 %collective-permute-start.4 = (f32[1024,256]{1,0:T(8,128)S(1)}, f32[1024,256]{1,0:T(8,128)S(1)}, u32[]{:S(2)}, u32[]{:S(2)}) collective-permute-start(f32[1024,256]{1,0:T(8,128)S(1)} %get-tuple-element.57), channel_id=1, source_target_pairs={{0,4},{4,0},{8,12},{12,8},{16,20},{20,16},{24,28},{28,24},{32,36},... | collective-permute-start | bytes 3145736 | tf_op jit(solution)/shard_map/ppermute | solution.py:336
  92.5 57.8 %collective-permute-start.11 = (f32[1024,256]{1,0:T(8,128)S(1)}, f32[1024,256]{1,0:T(8,128)S(1)}, u32[]{:S(2)}, u32[]{:S(2)}) collective-permute-start(f32[1024,256]{1,0:T(8,128)S(1)} %get-tuple-element.67), channel_id=1, source_target_pairs={{8,16},{16,8},{12,20},{20,12},{24,32},{32,24},{28,36},{36,28},{40,... | collective-permute-start | bytes 3145736 | tf_op jit(solution)/shard_map/ppermute | solution.py:335
  94.4 57.8 %collective-permute-start.10 = (f32[1024,256]{1,0:T(8,128)S(1)}, f32[1024,256]{1,0:T(8,128)S(1)}, u32[]{:S(2)}, u32[]{:S(2)}) collective-permute-start(f32[1024,256]{1,0:T(8,128)S(1)} %get-tuple-element.67), channel_id=1, source_target_pairs={{0,8},{8,0},{4,12},{12,4},{16,24},{24,16},{20,28},{28,20},{32,40},... | collective-permute-start | bytes 3145736 | tf_op jit(solution)/shard_map/ppermute | solution.py:336
  122.5 16.7 %collective-permute-start.7 = (f32[512,256]{1,0:T(8,128)S(1)}, f32[512,256]{1,0:T(8,128)S(1)}, u32[]{:S(2)}, u32[]{:S(2)}) collective-permute-start(f32[512,256]{1,0:T(8,128)S(1)} %slice.27), channel_id=1, source_target_pairs={{8,16},{16,8},{12,20},{20,12},{24,32},{32,24},{28,36},{36,28},{40,... | collective-permute-start | bytes 1572872 | tf_op jit(solution)/shard_map/ppermute | solution.py:335
  124.4 38.3 %collective-permute-start.6 = (f32[512,256]{1,0:T(8,128)S(1)}, f32[512,256]{1,0:T(8,128)S(1)}, u32[]{:S(2)}, u32[]{:S(2)}) collective-permute-start(f32[512,256]{1,0:T(8,128)S(1)} %slice.27), channel_id=1, source_target_pairs={{0,8},{8,0},{4,12},{12,4},{16,24},{24,16},{20,28},{28,20},{32,40},... | collective-permute-start | bytes 1572872 | tf_op jit(solution)/shard_map/ppermute | solution.py:336
  127.1 37.6 %collective-permute-start.15 = (f32[512,128]{1,0:T(8,128)S(1)}, f32[512,128]{1,0:T(8,128)S(1)}, u32[]{:S(2)}, u32[]{:S(2)}) collective-permute-start(f32[512,128]{1,0:T(8,128)S(1)} %get-tuple-element.87), channel_id=1, source_target_pairs={{8,16},{16,8},{12,20},{20,12},{24,32},{32,24},{28,36},{36,28},{40,... | collective-permute-start | bytes 786440 | tf_op jit(solution)/shard_map/ppermute | solution.py:335
  139.2 25.6 %collective-permute-start.14 = (f32[512,128]{1,0:T(8,128)S(1)}, f32[512,128]{1,0:T(8,128)S(1)}, u32[]{:S(2)}, u32[]{:S(2)}) collective-permute-start(f32[512,128]{1,0:T(8,128)S(1)} %get-tuple-element.87), channel_id=1, source_target_pairs={{0,8},{8,0},{4,12},{12,4},{16,24},{24,16},{20,28},{28,20},{32,40},... | collective-permute-start | bytes 786440 | tf_op jit(solution)/shard_map/ppermute | solution.py:336
  150.4 16.4 %collective-permute-start.13 = (f32[512,128]{1,0:T(8,128)S(1)}, f32[512,128]{1,0:T(8,128)S(1)}, u32[]{:S(2)}, u32[]{:S(2)}) collective-permute-start(f32[512,128]{1,0:T(8,128)S(1)} %get-tuple-element.88), channel_id=1, source_target_pairs={{8,16},{16,8},{12,20},{20,12},{24,32},{32,24},{28,36},{36,28},{40,... | collective-permute-start | bytes 786440 | tf_op jit(solution)/shard_map/ppermute | solution.py:335
  152.3 14.5 %collective-permute-start.12 = (f32[512,128]{1,0:T(8,128)S(1)}, f32[512,128]{1,0:T(8,128)S(1)}, u32[]{:S(2)}, u32[]{:S(2)}) collective-permute-start(f32[512,128]{1,0:T(8,128)S(1)} %get-tuple-element.88), channel_id=1, source_target_pairs={{0,8},{8,0},{4,12},{12,4},{16,24},{24,16},{20,28},{28,20},{32,40},... | collective-permute-start | bytes 786440 | tf_op jit(solution)/shard_map/ppermute | solution.py:336
